TPU v7x, 32 devices: a whole 2x2x4 slice. The times are simulated.
32 devices in a mesh: row: 4 (over x, core), col: 8 (over z, y).
Axes of the slice: x: 2, y: 2, z: 4, core: 2. Of those that a mesh axis runs over, the one named last changes fastest.
Arguments:
- object_slices: float32 [2, 2, 1024, 2048], P(None, None, 'row', 'col'), may hold values from -5 to 5
- probe: float32 [2, 128, 128], replicated, may hold values from -6 to 6
- amplitudes: float32 [4, 8, 16, 128, 128], P('row', 'col'), may hold values from 0.3 to 3
- scan_pos: int32 [2, 4, 8, 16], P(None, 'row', 'col'), may hold values from 0 to 2047, as said below
- scan_count: int32 [4, 8], P('row', 'col'), may hold values from 0 to 16, as said below
Outputs:
- object_new: float32 [2, 2, 1024, 2048], P(None, None, 'row', 'col')
Inputs may be any that keep to these rules, and one draw needn't show every extreme that they name: `scan_pos`: entry [0, i, j, k] is the pixel row and [1, i, j, k] the pixel column of the centre of slot k of tile (i, j); the centre lies within that tile's 256 x 256 pixels, also for slots that are not live. The live scans of a tile are its first scan_count slots; in every tile row the counts of its 8 tiles sum to exactly 64, and some tile of every row holds 16 scans.
All inputs are finite; a program needn't handle non-finite values.
Results may differ from a plain program's by a relative error of at most 0.00029.
Values sent between devices are 32-bit elements; how exact they have to be, the bound alone decides.
No kernel may reach another device: no remote copies, remote signals or barrier semaphores. Data moves between devices by JAX's collectives and lax.ppermute only.
A program may use at most 128 MiB of HBM per device.

v0:
```python
import math

import jax
import jax.numpy as jnp
from jax import lax
from jax.sharding import PartitionSpec as P

ITERS = 2


modulus_offset = 0.5
fresnel_scale = 0.9
highest = lax.Precision.HIGHEST


def with_halo(cells, sides, width):
    for axis, dim in sides:
        count = lax.axis_size(axis)
        ends = count - 1
        head = lax.slice_in_dim(cells, 0, width, axis=dim)
        tail = lax.slice_in_dim(cells, cells.shape[dim] - width, cells.shape[dim], axis=dim)
        cells = jnp.concatenate(
            [
                lax.ppermute(tail, axis, [(i, (i + 1) % count) for i in range(ends)]),
                cells,
                lax.ppermute(head, axis, [((i + 1) % count, i) for i in range(ends)]),
            ],
            axis=dim,
        )
    return cells


def dft_tables(frame_size):
    positions = jnp.arange(frame_size, dtype=jnp.int32)
    wrapped = positions[:, None] * positions[None, :] % frame_size
    angles = -2.0 * math.pi / frame_size * wrapped.astype(jnp.float32)
    scaling = 1.0 / math.sqrt(frame_size)
    return (jnp.cos(angles) * scaling, jnp.sin(angles) * scaling)


def propagator(frame_size):
    positions = jnp.arange(frame_size, dtype=jnp.int32)
    frequency = jnp.where(positions < frame_size // 2, positions, positions - frame_size).astype(
        jnp.float32
    )
    phase = (
        math.pi * fresnel_scale * (frequency[:, None] ** 2 + frequency[None, :] ** 2) / frame_size
    )
    return (jnp.cos(phase), jnp.sin(phase))


def apply_left(matrix, values):
    return jnp.einsum("jk,bkl->bjl", matrix, values, precision=highest)


def apply_right(values, matrix):
    return jnp.einsum("bjk,kl->bjl", values, matrix, precision=highest)


def transform(real_part, imag_part, table_re, table_im):
    mid_re = apply_left(table_re, real_part) - apply_left(table_im, imag_part)
    mid_im = apply_left(table_re, imag_part) + apply_left(table_im, real_part)
    out_re = apply_right(mid_re, table_re) - apply_right(mid_im, table_im)
    out_im = apply_right(mid_re, table_im) + apply_right(mid_im, table_re)
    return (out_re, out_im)


def slot_gradients(patches, local_amps, weights, probe, tables):
    table_re, table_im, inverse_im, prop_re, prop_im = tables
    layers = patches.shape[1]
    obj_re = [patches[:, layer_id, 0] for layer_id in range(layers)]
    obj_im = [patches[:, layer_id, 1] for layer_id in range(layers)]
    inc_re = [jnp.broadcast_to(probe[0], local_amps.shape)]
    inc_im = [jnp.broadcast_to(probe[1], local_amps.shape)]
    layer_id = 0
    exit_re = inc_re[layer_id] * obj_re[layer_id] - inc_im[layer_id] * obj_im[layer_id]
    exit_im = inc_re[layer_id] * obj_im[layer_id] + inc_im[layer_id] * obj_re[layer_id]
    spec_re, spec_im = transform(exit_re, exit_im, table_re, table_im)
    spec_re, spec_im = (
        spec_re * prop_re - spec_im * prop_im,
        spec_re * prop_im + spec_im * prop_re,
    )
    next_re, next_im = transform(spec_re, spec_im, table_re, inverse_im)
    inc_re.append(next_re)
    inc_im.append(next_im)
    exit_re = inc_re[-1] * obj_re[-1] - inc_im[-1] * obj_im[-1]
    exit_im = inc_re[-1] * obj_im[-1] + inc_im[-1] * obj_re[-1]
    psi_re, psi_im = transform(exit_re, exit_im, table_re, table_im)
    modulus = jnp.sqrt(psi_re * psi_re + psi_im * psi_im + modulus_offset)
    factor = 1.0 - local_amps / modulus
    back_re, back_im = transform(psi_re * factor, psi_im * factor, table_re, inverse_im)
    gradients = [None] * layers
    for layer_id in reversed(range(layers)):
        grad_re = inc_re[layer_id] * back_re + inc_im[layer_id] * back_im
        grad_im = inc_re[layer_id] * back_im - inc_im[layer_id] * back_re
        gradients[layer_id] = jnp.stack([grad_re, grad_im], axis=1)
        if layer_id > 0:
            adj_re = obj_re[layer_id] * back_re + obj_im[layer_id] * back_im
            adj_im = obj_re[layer_id] * back_im - obj_im[layer_id] * back_re
            spec_re, spec_im = transform(adj_re, adj_im, table_re, table_im)
            spec_re, spec_im = (
                spec_re * prop_re + spec_im * prop_im,
                spec_im * prop_re - spec_re * prop_im,
            )
            back_re, back_im = transform(spec_re, spec_im, table_re, inverse_im)
    return jnp.stack(gradients, axis=1) * weights[:, None, None, None, None]


def cut_patches(extended, patch_row, patch_col, frame_size):
    layers = extended.shape[0]
    zero_index = jnp.zeros((), jnp.int32)
    return jax.vmap(
        lambda row_at, col_at: lax.dynamic_slice(
            extended, (zero_index, zero_index, row_at, col_at), (layers, 2, frame_size, frame_size)
        )
    )(patch_row, patch_col)


def place_patches(ext_shape, gradients, patch_row, patch_col):
    zero_index = jnp.zeros((), jnp.int32)

    def add_one(item, accumulator):
        corner = (zero_index, zero_index, patch_row[item], patch_col[item])
        current_block = lax.dynamic_slice(accumulator, corner, gradients.shape[1:])
        return lax.dynamic_update_slice(accumulator, current_block + gradients[item], corner)

    return lax.fori_loop(0, gradients.shape[0], add_one, jnp.zeros(ext_shape, jnp.float32))


def fold_axis(widened, rim_width, frame_size, along_axis):
    total_len = widened.shape[along_axis] - 2 * rim_width
    inner_len = total_len - frame_size
    middle = lax.slice_in_dim(widened, rim_width, rim_width + total_len, axis=along_axis)
    lower_rim = lax.slice_in_dim(widened, 0, rim_width, axis=along_axis)
    upper_rim = lax.slice_in_dim(
        widened, rim_width + total_len, total_len + 2 * rim_width, axis=along_axis
    )
    lower_place = [slice(None)] * widened.ndim
    lower_place[along_axis] = slice(frame_size - rim_width, frame_size)
    upper_place = [slice(None)] * widened.ndim
    upper_place[along_axis] = slice(inner_len, inner_len + rim_width)
    return middle.at[tuple(lower_place)].add(lower_rim).at[tuple(upper_place)].add(upper_rim)


def fold_rims(widened, rim_width, frame_size):
    return fold_axis(fold_axis(widened, rim_width, frame_size, 2), rim_width, frame_size, 3)


def body(object_slices, probe, amplitudes, scan_pos, scan_count):
    layers, _, tile_r, tile_c = object_slices.shape
    frame_size = probe.shape[-1]
    half_frame = frame_size // 2
    own_slots = amplitudes.shape[2]
    row_start = lax.axis_index("row") * tile_r
    col_start = lax.axis_index("col") * tile_c
    patch_row = scan_pos[0, 0, 0] - row_start
    patch_col = scan_pos[1, 0, 0] - col_start
    local_amps = amplitudes[0, 0]
    tile_count = scan_count[0, 0]
    slot_ids = jnp.arange(own_slots, dtype=jnp.int32)
    live_mask = (slot_ids < tile_count).astype(jnp.float32)
    table_re, table_im = dft_tables(frame_size)
    prop_re, prop_im = propagator(frame_size)
    tables = (table_re, table_im, -table_im, prop_re, prop_im)
    ext_shape = (layers, 2, tile_r + frame_size, tile_c + frame_size)
    worker_state = None
    current = object_slices
    for iteration in range(ITERS):
        extended = with_halo(current, (("row", 2), ("col", 3)), half_frame)
        patches = cut_patches(extended, patch_row, patch_col, frame_size)
        gradients = slot_gradients(patches, local_amps, live_mask, probe, tables)
        grad_ext, worker_state = (
            place_patches(ext_shape, gradients, patch_row, patch_col),
            worker_state,
        )
        widened = with_halo(grad_ext, (("row", 2), ("col", 3)), half_frame)
        summed = fold_rims(widened, half_frame, frame_size)
        current = (
            current
            - summed[:, :, half_frame : half_frame + tile_r, half_frame : half_frame + tile_c]
        )
    return current


def solution(mesh):
    in_specs = (
        P(None, None, "row", "col"),
        P(),
        P("row", "col", None, None, None),
        P(None, "row", "col", None),
        P("row", "col"),
    )
    out_specs = P(None, None, "row", "col")
    return jax.shard_map(body, mesh=mesh, in_specs=in_specs, out_specs=out_specs, check_vma=False)
```

profile of v0, /device:TPU:1, one launch (start us, length us, event | category | flops | bytes accessed | tf_op | source)
XLA Modules:
  0.0 881.7 jit_solution(12787600794342778734)
XLA Ops:
  1.8 4.5 collective-permute-start
  12.4 4.4 collective-permute-done.1
  23.5 9.2 %collective-permute-done.2 = f32[2,2,384,64]{2,3,1,0:T(8,128)S(1)} collective-permute-done((f32[2,2,384,64]{2,3,1,0:T(8,128)}, f32[2,2,384,64]{2,3,1,0:T(8,128)S(1)}, u32[]{:S(2)}, u32[]{:S(2)}) %collective-permute-start.2) | collective-permute-done | bytes 393248 | tf_op jit(solution)/shard_map/ppermute | solution.py:24
  37.2 64.6 %while.38 = (s32[]{:T(128)}, f32[2,2,384,384]{2,3,1,0:T(8,128)}, s32[16,4]{0,1:T(4,128)S(1)}, f32[16,2,2,128,128]{4,3,0,2,1:T(8,128)}, s32[]{:T(128)}) while((s32[]{:T(128)}, f32[2,2,384,384]{2,3,1,0:T(8,128)}, s32[16,4]{0,1:T(4,128)S(1)}, f32[16,2,2,128,128]{4,3,0,2,1:T(8,128)}, s32[]{:T(128)}) %tuple.148), condition=%wide.while_cond.8, body=%wide.while_body.8.sunk | while | flops 2 | bytes 1573497 | solution.py:113
  207.8 170.7 %while.36 = (s32[]{:T(128)}, f32[2,2,384,384]{3,2,1,0:T(8,128)}, s32[16]{0:T(128)S(1)}, s32[16]{0:T(128)S(1)}, f32[16,2,2,128,128]{4,3,0,2,1:T(8,128)}, /*index=5*/s32[]{:T(128)}, s32[]{:T(128)}, s32[]{:T(128)}) while((s32[]{:T(128)}, f32[2,2,384,384]{3,2,1,0:T(8,128)}, s32[16]{0:T(128)S(1)}, s32[16]{0:T(128)S(1)}, ...), condition=%wide.region_1.2_spmd, body=%wide.region_0.1_spmd.sunk | while | flops 65544 | bytes 1310913 | solution.py:127
  214.1 4.4 dynamic_update_slice.16
  224.9 4.4 dynamic_update_slice.16
  331.6 4.4 dynamic_update_slice.16
  342.3 4.4 dynamic_update_slice.16
  400.4 19.5 %collective-permute-done.6 = f32[2,2,512,64]{2,3,1,0:T(8,128)S(1)} collective-permute-done((f32[2,2,512,64]{2,3,1,0:T(8,128)S(1)}, f32[2,2,512,64]{2,3,1,0:T(8,128)S(1)}, u32[]{:S(2)}, u32[]{:S(2)}) %collective-permute-start.6) | collective-permute-done | bytes 524320 | tf_op jit(solution)/shard_map/ppermute | solution.py:24
  424.2 6.5 scatter-add.26
  432.5 5.0 scatter-add.29
  450.3 4.4 collective-permute-done.9
  455.9 5.3 collective-permute-start.10
  462.4 10.4 %collective-permute-done.10 = f32[2,2,384,64]{2,3,1,0:T(8,128)} collective-permute-done((f32[2,2,384,64]{2,3,1,0:T(8,128)}, f32[2,2,384,64]{2,3,1,0:T(8,128)}, u32[]{:S(2)}, u32[]{:S(2)}) %collective-permute-start.10) | collective-permute-done | bytes 393248 | tf_op jit(solution)/shard_map/ppermute | solution.py:24
  478.5 64.5 %while.39 = (s32[]{:T(128)}, f32[2,2,384,384]{2,3,1,0:T(8,128)}, s32[16,4]{0,1:T(4,128)S(1)}, f32[16,2,2,128,128]{4,3,0,2,1:T(8,128)}, s32[]{:T(128)}) while((s32[]{:T(128)}, f32[2,2,384,384]{2,3,1,0:T(8,128)}, s32[16,4]{0,1:T(4,128)S(1)}, f32[16,2,2,128,128]{4,3,0,2,1:T(8,128)}, s32[]{:T(128)}) %tuple.160), condition=%wide.while_cond.9, body=%wide.while_body.9.sunk | while | flops 2 | bytes 1573497 | solution.py:113
  648.8 170.7 %while.37 = (s32[]{:T(128)}, f32[2,2,384,384]{3,2,1,0:T(8,128)}, s32[16]{0:T(128)S(1)}, s32[16]{0:T(128)S(1)}, f32[16,2,2,128,128]{4,3,0,2,1:T(8,128)}, /*index=5*/s32[]{:T(128)}, s32[]{:T(128)}, s32[]{:T(128)}) while((s32[]{:T(128)}, f32[2,2,384,384]{3,2,1,0:T(8,128)}, s32[16]{0:T(128)S(1)}, s32[16]{0:T(128)S(1)}, ...), condition=%wide.region_3.4_spmd, body=%wide.region_2.3_spmd.sunk | while | flops 65544 | bytes 1310913 | solution.py:127
  655.1 4.4 dynamic_update_slice.17
  665.9 4.4 dynamic_update_slice.17
  772.6 4.4 dynamic_update_slice.17
  783.4 4.4 dynamic_update_slice.17
  838.4 18.2 %collective-permute-done.14 = f32[2,2,512,64]{2,3,1,0:T(8,128)S(1)} collective-permute-done((f32[2,2,512,64]{2,3,1,0:T(8,128)S(1)}, f32[2,2,512,64]{2,3,1,0:T(8,128)S(1)}, u32[]{:S(2)}, u32[]{:S(2)}) %collective-permute-start.14) | collective-permute-done | bytes 524320 | tf_op jit(solution)/shard_map/ppermute | solution.py:24
  862.4 6.5 scatter-add.34
  870.8 5.0 scatter-add.35
  (470 shorter events, 620.2 us)
Async XLA Ops:
  0.0 8.3 copy-start.8
  0.0 23.4 %copy-start.7 = (f32[2,128,128]{2,1,0:T(8,128)S(1)}, f32[2,128,128]{2,1,0:T(8,128)}, u32[]{:S(2)}) copy-start(f32[2,128,128]{2,1,0:T(8,128)} %param.26) | copy-start | bytes 393220
  1.8 10.6 %collective-permute-start = (f32[2,2,64,256]{2,3,1,0:T(8,128)S(1)}, f32[2,2,64,256]{2,3,1,0:T(8,128)S(1)}, u32[]{:S(2)}, u32[]{:S(2)}) collective-permute-start(f32[2,2,64,256]{2,3,1,0:T(8,128)S(1)} %get-tuple-element.427), channel_id=1, source_target_pairs={{0,8},{8,16},{16,24},{1,9},{9,17},{17,25},{2,10},{10,18},{18,26},{... | collective-permute-start | bytes 786440 | tf_op jit(solution)/shard_map/ppermute | solution.py:24
  6.3 10.5 %collective-permute-start.1 = (f32[2,2,64,256]{2,3,1,0:T(8,128)S(1)}, f32[2,2,64,256]{2,3,1,0:T(8,128)S(1)}, u32[]{:S(2)}, u32[]{:S(2)}) collective-permute-start(f32[2,2,64,256]{2,3,1,0:T(8,128)S(1)} %get-tuple-element.428), channel_id=1, source_target_pairs={{8,0},{16,8},{24,16},{9,1},{17,9},{25,17},{10,2},{18,10},{26,18},{... | collective-permute-start | bytes 786440 | tf_op jit(solution)/shard_map/ppermute | solution.py:26
  18.0 14.7 %collective-permute-start.2 = (f32[2,2,384,64]{2,3,1,0:T(8,128)}, f32[2,2,384,64]{2,3,1,0:T(8,128)S(1)}, u32[]{:S(2)}, u32[]{:S(2)}) collective-permute-start(f32[2,2,384,64]{2,3,1,0:T(8,128)} %get-tuple-element.423), channel_id=1, source_target_pairs={{0,1},{1,2},{2,3},{3,4},{4,5},{5,6},{6,7},{8,9},{9,10},{10,11},{11... | collective-permute-start | bytes 1179656 | tf_op jit(solution)/shard_map/ppermute | solution.py:24
  21.5 11.2 %collective-permute-start.3 = (f32[2,2,384,64]{2,3,1,0:T(8,128)}, f32[2,2,384,64]{2,3,1,0:T(8,128)S(1)}, u32[]{:S(2)}, u32[]{:S(2)}) collective-permute-start(f32[2,2,384,64]{2,3,1,0:T(8,128)} %get-tuple-element.424), channel_id=1, source_target_pairs={{1,0},{2,1},{3,2},{4,3},{5,4},{6,5},{7,6},{9,8},{10,9},{11,10},{12... | collective-permute-start | bytes 1179656 | tf_op jit(solution)/shard_map/ppermute | solution.py:26
  101.8 7.3 copy-start.1
  149.6 3.9 copy-start
  380.4 8.1 collective-permute-start.4
  382.5 9.4 %collective-permute-start.5 = (f32[2,2,64,384]{3,2,1,0:T(8,128)}, f32[2,2,64,384]{3,2,1,0:T(8,128)}, u32[]{:S(2)}, u32[]{:S(2)}) collective-permute-start(f32[2,2,64,384]{3,2,1,0:T(8,128)} %get-tuple-element.412), channel_id=1, source_target_pairs={{8,0},{16,8},{24,16},{9,1},{17,9},{25,17},{10,2},{18,10},{26,18},{... | collective-permute-start | bytes 1179656 | tf_op jit(solution)/shard_map/ppermute | solution.py:26
  394.1 25.9 %copy-start.5 = (f32[2,2,384,384]{2,3,1,0:T(8,128)S(1)}, f32[2,2,384,384]{2,3,1,0:T(8,128)}, u32[]{:S(2)}) copy-start(f32[2,2,384,384]{2,3,1,0:T(8,128)} %copy.289) | copy-start | bytes 7077892
  394.1 25.9 %copy-start.6 = (f32[2,2,64,384]{2,3,1,0:T(8,128)S(1)}, f32[2,2,64,384]{2,3,1,0:T(8,128)}, u32[]{:S(2)}) copy-start(f32[2,2,64,384]{2,3,1,0:T(8,128)} %copy.290) | copy-start | bytes 1179652
  395.9 24.1 %collective-permute-start.6 = (f32[2,2,512,64]{2,3,1,0:T(8,128)S(1)}, f32[2,2,512,64]{2,3,1,0:T(8,128)S(1)}, u32[]{:S(2)}, u32[]{:S(2)}) collective-permute-start(f32[2,2,512,64]{2,3,1,0:T(8,128)S(1)} %get-tuple-element.407), channel_id=1, source_target_pairs={{0,1},{1,2},{2,3},{3,4},{4,5},{5,6},{6,7},{8,9},{9,10},{10,11},{11... | collective-permute-start | bytes 1572872 | tf_op jit(solution)/shard_map/ppermute | solution.py:24
  399.1 20.8 %collective-permute-start.7 = (f32[2,2,512,64]{2,3,1,0:T(8,128)S(1)}, f32[2,2,512,64]{2,3,1,0:T(8,128)S(1)}, u32[]{:S(2)}, u32[]{:S(2)}) collective-permute-start(f32[2,2,512,64]{2,3,1,0:T(8,128)S(1)} %get-tuple-element.408), channel_id=1, source_target_pairs={{1,0},{2,1},{3,2},{4,3},{5,4},{6,5},{7,6},{9,8},{10,9},{11,10},{12... | collective-permute-start | bytes 1572872 | tf_op jit(solution)/shard_map/ppermute | solution.py:26
  442.2 8.1 collective-permute-start.8
  444.2 10.5 %collective-permute-start.9 = (f32[2,2,64,256]{2,3,1,0:T(8,128)S(1)}, f32[2,2,64,256]{2,3,1,0:T(8,128)S(1)}, u32[]{:S(2)}, u32[]{:S(2)}) collective-permute-start(f32[2,2,64,256]{2,3,1,0:T(8,128)S(1)} %get-tuple-element.426), channel_id=1, source_target_pairs={{8,0},{16,8},{24,16},{9,1},{17,9},{25,17},{10,2},{18,10},{26,18},{... | collective-permute-start | bytes 786440 | tf_op jit(solution)/shard_map/ppermute | solution.py:26
  455.9 16.9 %collective-permute-start.10 = (f32[2,2,384,64]{2,3,1,0:T(8,128)}, f32[2,2,384,64]{2,3,1,0:T(8,128)}, u32[]{:S(2)}, u32[]{:S(2)}) collective-permute-start(f32[2,2,384,64]{2,3,1,0:T(8,128)} %get-tuple-element.419), channel_id=1, source_target_pairs={{0,1},{1,2},{2,3},{3,4},{4,5},{5,6},{6,7},{8,9},{9,10},{10,11},{11... | collective-permute-start | bytes 1179656 | tf_op jit(solution)/shard_map/ppermute | solution.py:24
  461.2 11.7 %collective-permute-start.11 = (f32[2,2,384,64]{2,3,1,0:T(8,128)}, f32[2,2,384,64]{2,3,1,0:T(8,128)}, u32[]{:S(2)}, u32[]{:S(2)}) collective-permute-start(f32[2,2,384,64]{2,3,1,0:T(8,128)} %get-tuple-element.420), channel_id=1, source_target_pairs={{1,0},{2,1},{3,2},{4,3},{5,4},{6,5},{7,6},{9,8},{10,9},{11,10},{12... | collective-permute-start | bytes 1179656 | tf_op jit(solution)/shard_map/ppermute | solution.py:26
  543.0 7.3 copy-start.2
  820.7 7.4 collective-permute-start.12
  822.7 9.1 %collective-permute-start.13 = (f32[2,2,64,384]{3,2,1,0:T(8,128)S(1)}, f32[2,2,64,384]{3,2,1,0:T(8,128)S(1)}, u32[]{:S(2)}, u32[]{:S(2)}) collective-permute-start(f32[2,2,64,384]{3,2,1,0:T(8,128)S(1)} %get-tuple-element.410), channel_id=1, source_target_pairs={{8,0},{16,8},{24,16},{9,1},{17,9},{25,17},{10,2},{18,10},{26,18},{... | collective-permute-start | bytes 1179656 | tf_op jit(solution)/shard_map/ppermute | solution.py:26
  833.6 23.0 %collective-permute-start.14 = (f32[2,2,512,64]{2,3,1,0:T(8,128)S(1)}, f32[2,2,512,64]{2,3,1,0:T(8,128)S(1)}, u32[]{:S(2)}, u32[]{:S(2)}) collective-permute-start(f32[2,2,512,64]{2,3,1,0:T(8,128)S(1)} %get-tuple-element.405), channel_id=1, source_target_pairs={{0,1},{1,2},{2,3},{3,4},{4,5},{5,6},{6,7},{8,9},{9,10},{10,11},{11... | collective-permute-start | bytes 1572872 | tf_op jit(solution)/shard_map/ppermute | solution.py:24
  837.1 19.5 %collective-permute-start.15 = (f32[2,2,512,64]{2,3,1,0:T(8,128)S(1)}, f32[2,2,512,64]{2,3,1,0:T(8,128)S(1)}, u32[]{:S(2)}, u32[]{:S(2)}) collective-permute-start(f32[2,2,512,64]{2,3,1,0:T(8,128)S(1)} %get-tuple-element.406), channel_id=1, source_target_pairs={{1,0},{2,1},{3,2},{4,3},{5,4},{6,5},{7,6},{9,8},{10,9},{11,10},{12... | collective-permute-start | bytes 1572872 | tf_op jit(solution)/shard_map/ppermute | solution.py:26
  859.3 2.9 copy-start.3
  (1 other events, 2.9 us)
where the time goes:
time: 898 us; the launch traced here: 882 us
  local copies, waits for them, and re-layouts  360 us (40%)
  matrix products  202 us (22%)
  loops' own time  126 us (14%)
  waiting for transfers between devices  79.2 us (9%)
  other arithmetic  71.5 us (8%)
  starting transfers between devices  40.7 us (5%)
    dynamic_update_slice x32, local copies, waits for them, and re-layouts, add_one(): lax.dynamic_update_slice(accumulator, current_block + gradients[item], co...  138 us
    gather x160, local copies, waits for them, and re-layouts  128 us
    another operation x2, loops' own time, place_patches(): lax.fori_loop(0, gradients.shape[0], add_one, jnp.zeros(ext_shape, jnp.fl...  125 us
    dot_general x48, matrix products, apply_left(): return jnp.einsum('jk,bkl->bjl', matrix, values, precision=highest)  106 us
    dot_general x48, matrix products, apply_right(): return jnp.einsum('bjk,kl->bjl', values, matrix, precision=highest)  96.4 us
    ppermute x8, waiting for transfers between devices, with_halo(): lax.ppermute(tail, axis, [(i, (i + 1) % count) for i in range(ends)])  64.8 us
    add x32, other arithmetic, add_one(): current_block + gradients[item]  41.4 us
    dynamic_slice x64, local copies, waits for them, and re-layouts, add_one(): corner = (zero_index, zero_index, patch_row[item], patch_col[item])  37.5 us
  transfers between devices with their start and end apart: 16, of which 10 were waited for; matrix products, arithmetic and copies ran while one was open for 1% of the time, Pallas kernels for 0%

commit v1 on v0

v1 whole, which is shorter than its diff:
```python
import functools
import math

import jax
import jax.numpy as jnp
import ml_dtypes
import numpy as np
from jax import lax
from jax.experimental import pallas as pl
from jax.experimental.pallas import tpu as pltpu
from jax.sharding import PartitionSpec as P

ITERS = 2
LANES = 128
GROUP = 4

modulus_offset = 0.5
fresnel_scale = 0.9


def split_table(table):
    high = table.astype(np.float32).astype(ml_dtypes.bfloat16)
    low = (table - high.astype(np.float64)).astype(np.float32).astype(ml_dtypes.bfloat16)
    return high, low


def transform_tables(frame_size):
    positions = np.arange(frame_size)
    dft = np.exp(-2j * math.pi * (positions[:, None] * positions[None, :] % frame_size) / frame_size)
    dft = dft / math.sqrt(frame_size)
    frequency = np.where(positions < frame_size // 2, positions, positions - frame_size)
    phase = np.exp(1j * math.pi * fresnel_scale * frequency.astype(np.float64) ** 2 / frame_size)
    hop = (np.conj(dft) * phase[None, :]) @ dft
    tables = []
    for matrix in (dft, hop):
        re, im = matrix.real, matrix.imag
        right = np.block([[re, im], [-im, re]])
        left = np.block([[re, -im], [im, re]])
        for table in (right, left):
            tables.extend(split_table(table))
    return np.stack(tables)


DFT_RIGHT, DFT_LEFT, HOP_RIGHT, HOP_LEFT = 0, 2, 4, 6


def neighbour(values, axis, step):
    count = lax.axis_size(axis)
    pairs = [(i, i + step) for i in range(count) if 0 <= i + step < count]
    return lax.ppermute(values, axis, pairs)


def lane_ids(shape):
    return lax.broadcasted_iota(jnp.int32, shape, len(shape) - 1)


def swap_halves(values):
    return pltpu.roll(values, LANES // 2, values.ndim - 1)


def vmem():
    return pl.BlockSpec(memory_space=pltpu.VMEM)


def smem():
    return pl.BlockSpec(memory_space=pltpu.SMEM)


def split(values):
    high = values.astype(jnp.bfloat16)
    return high, (values - high.astype(jnp.float32)).astype(jnp.bfloat16)


def dot(a, b):
    return jnp.dot(a, b, preferred_element_type=jnp.float32)


def pack_kernel(object_ref, left_ref, right_ref, up_ref, down_ref):
    planes, rows, cols = object_ref.shape
    half = rows // 2
    low = lane_ids((half, LANES)) < LANES // 2
    for plane in range(planes):
        first = object_ref[plane, :, 0:LANES]
        last = object_ref[plane, :, cols - LANES : cols]
        left_ref[plane] = jnp.where(low, first[half:], swap_halves(first[:half]))
        right_ref[plane] = jnp.where(low, swap_halves(last[:half]), last[half:])
        up_ref[plane] = object_ref[plane, 0:64, :]
        down_ref[plane] = object_ref[plane, rows - 64 : rows, :]


def gradients(pos_ref, amps_ref, probe_ref, tables_ref, field_ref, grad_ref, work):
    frame = probe_ref.shape[-1]
    o0, o1, inc, wave = work
    count = pos_ref[2, 0]
    lanes = lane_ids((frame, LANES))

    grad_ref[...] = jnp.zeros_like(grad_ref)

    def right(source, index):
        table_high, table_low = tables_ref[index], tables_ref[index + 1]
        high, low = split(source)
        return dot(high, table_high) + (dot(low, table_high) + dot(high, table_low))

    def left(source, index):
        table_high, table_low = tables_ref[index], tables_ref[index + 1]
        high, low = split(source)
        return dot(table_high, high) + (dot(table_high, low) + dot(table_low, high))

    def two_sided(zs, right_index, left_index):
        rows = jnp.concatenate([jnp.concatenate(z, axis=1) for z in zs], axis=0)
        out = right(rows, right_index)
        result = []
        for pair in range(0, len(zs), 2):
            re = jnp.concatenate(
                [out[(pair + k) * frame : (pair + k + 1) * frame, :frame] for k in range(2)], axis=1
            )
            im = jnp.concatenate(
                [out[(pair + k) * frame : (pair + k + 1) * frame, frame:] for k in range(2)], axis=1
            )
            mixed = left(jnp.concatenate([re, im], axis=0), left_index)
            for k in range(2):
                cols = slice(k * frame, (k + 1) * frame)
                result.append((mixed[:frame, cols], mixed[frame:, cols]))
        return result

    def group_step(group, carry):
        base = group * GROUP
        where = []
        for k in range(GROUP):
            row_at, col_at = pos_ref[0, base + k], pos_ref[1, base + k]
            block = lax.shift_right_logical(col_at, 7)
            shift = jnp.bitwise_and(col_at, LANES - 1)
            where.append((pl.ds(row_at, frame), block, shift))
            for plane in range(4):
                near = field_ref[plane, block, pl.ds(row_at, frame), :]
                far = field_ref[plane, block + 1, pl.ds(row_at, frame), :]
                joined = jnp.where(lanes >= shift, near, far)
                target = o0 if plane < 2 else o1
                target[k, plane % 2] = pltpu.roll(
                    joined, jnp.bitwise_and(LANES - shift, LANES - 1), 1
                )
        probe_re, probe_im = probe_ref[0], probe_ref[1]
        zs = []
        for k in range(GROUP):
            a, b = o0[k, 0], o0[k, 1]
            zs.append((probe_re * a - probe_im * b, probe_re * b + probe_im * a))
        for k, (re, im) in enumerate(two_sided(zs, HOP_RIGHT, HOP_LEFT)):
            inc[k, 0] = re
            inc[k, 1] = im
        zs = []
        for k in range(GROUP):
            a, b, c, d = inc[k, 0], inc[k, 1], o1[k, 0], o1[k, 1]
            zs.append((a * c - b * d, a * d + b * c))
        for k, (re, im) in enumerate(two_sided(zs, DFT_RIGHT, DFT_LEFT)):
            live = jnp.where(base + k < count, 1.0, 0.0)
            factor = (1.0 - amps_ref[base + k] * lax.rsqrt(re * re + im * im + modulus_offset)) * live
            wave[k, 0] = re * factor
            wave[k, 1] = im * factor
        zs = [(wave[k, 0], wave[k, 1]) for k in range(GROUP)]

        def place(k, first_plane, values):
            rows, block, shift = where[k]
            for part in range(2):
                moved = pltpu.roll(values[part], shift, 1)
                near = jnp.where(lanes >= shift, moved, 0.0)
                far = jnp.where(lanes >= shift, 0.0, moved)
                grad_ref[first_plane + part, block, rows, :] += near
                grad_ref[first_plane + part, block + 1, rows, :] += far

        for k, (re, im) in enumerate(two_sided(zs, DFT_LEFT, DFT_RIGHT)):
            wave[k, 0] = re
            wave[k, 1] = im
        zs = []
        for k in range(GROUP):
            re, im = wave[k, 0], wave[k, 1]
            a, b, c, d = inc[k, 0], inc[k, 1], o1[k, 0], o1[k, 1]
            place(k, 2, (a * re + b * im, a * im - b * re))
            zs.append((c * re + d * im, c * im - d * re))
        for k, (re, im) in enumerate(two_sided(zs, HOP_LEFT, HOP_RIGHT)):
            place(k, 0, (probe_re * re + probe_im * im, probe_re * im - probe_im * re))
        return carry

    lax.fori_loop(0, (count + GROUP - 1) // GROUP, group_step, 0)


def write_grad(grad_ref, top_ref, own_ref, bottom_ref):
    rim = top_ref.shape[2]
    rows = own_ref.shape[2]
    top_ref[...] = grad_ref[:, :, 0:rim, :]
    own_ref[...] = grad_ref[:, :, rim : rim + rows, :]
    bottom_ref[...] = grad_ref[:, :, rim + rows : rim + rows + rim, :]


def first_kernel(
    pos_ref, object_ref, from_left, from_right, from_up, from_down, corner_up, corner_down,
    amps_ref, probe_ref, tables_ref,
    field_ref, top_ref, own_ref, bottom_ref,
    grad_ref, *work,
):
    planes, rows, cols = object_ref.shape
    rim = from_up.shape[1]
    half = rows // 2
    blocks = cols // LANES

    def lay(plane, row_at, tiles, left, right):
        low = lane_ids(tiles[0].shape) < LANES // 2
        turned = [left] + [swap_halves(tile) for tile in tiles] + [right]
        for block in range(blocks + 1):
            field_ref[plane, block, row_at : row_at + tiles[0].shape[0], :] = jnp.where(
                low, turned[block], turned[block + 1]
            )

    def tiles_of(ref, plane, lo, hi):
        return [ref[plane, lo:hi, b * LANES : (b + 1) * LANES] for b in range(blocks)]

    for plane in range(planes):
        corner = corner_up[plane]
        turned = swap_halves(corner)
        lay(plane, 0, tiles_of(from_up, plane, 0, rim), turned, turned)
        lay(plane, rim, tiles_of(object_ref, plane, 0, half), from_left[plane], from_right[plane])
        lay(
            plane, rim + half, tiles_of(object_ref, plane, half, rows),
            swap_halves(from_left[plane]), swap_halves(from_right[plane]),
        )
        corner = corner_down[plane]
        lay(plane, rim + rows, tiles_of(from_down, plane, 0, rim), corner, corner)
    gradients(pos_ref, amps_ref, probe_ref, tables_ref, field_ref, grad_ref, work)
    write_grad(grad_ref, top_ref, own_ref, bottom_ref)


def fold_rows(own_ref, from_up, from_down, block, plane):
    rim = from_up.shape[2]
    rows = own_ref.shape[2]
    return [
        (0, rim, own_ref[plane, block, 0:rim, :] + from_up[plane, block]),
        (rim, rows - rim, own_ref[plane, block, rim : rows - rim, :]),
        (rows - rim, rows, own_ref[plane, block, rows - rim : rows, :] + from_down[plane, block]),
    ]


def fold_kernel(own_ref, from_up, from_down, left_ref, mid_ref, right_ref):
    planes, blocks = own_ref.shape[:2]
    for plane in range(planes):
        for block in range(blocks):
            for lo, hi, values in fold_rows(own_ref, from_up, from_down, block, plane):
                if block == 0:
                    left_ref[plane, lo:hi, :] = values
                elif block == blocks - 1:
                    right_ref[plane, lo:hi, :] = values
                else:
                    mid_ref[plane, block - 1, lo:hi, :] = values


def total_kernel(left_ref, mid_ref, right_ref, from_left, from_right, own_ref, up_ref, down_ref):
    planes, blocks, rows, _ = own_ref.shape
    rim = up_ref.shape[2]
    for plane in range(planes):
        for block in range(blocks):
            if block == 0:
                values = left_ref[plane] + from_left[plane]
            elif block == blocks - 1:
                values = right_ref[plane] + from_right[plane]
            else:
                values = mid_ref[plane, block - 1]
            own_ref[plane, block] = values
            up_ref[plane, block] = values[0:rim]
            down_ref[plane, block] = values[rows - rim : rows]


def next_kernel(
    pos_ref, old_ref, total_ref, from_up, from_down, amps_ref, probe_ref, tables_ref,
    field_ref, top_ref, own_ref, bottom_ref,
    grad_ref, *work,
):
    planes, blocks, rows, _ = total_ref.shape
    rim = from_up.shape[2]
    for block in range(blocks):
        lane = lane_ids((1, 1, LANES))
        inside = lane >= 0
        if block == 0:
            inside = lane >= pos_ref[2, 1] * (LANES // 2)
        if block == blocks - 1:
            inside = lane < LANES - pos_ref[2, 2] * (LANES // 2)
        for lo, hi, values in (
            (0, rim, from_up[:, block]),
            (rim, rim + rows, total_ref[:, block]),
            (rim + rows, rows + 2 * rim, from_down[:, block]),
        ):
            updated = old_ref[:, block, lo:hi, :] - values
            field_ref[:, block, lo:hi, :] = jnp.where(inside, updated, 0.0)
    gradients(pos_ref, amps_ref, probe_ref, tables_ref, field_ref, grad_ref, work)
    write_grad(grad_ref, top_ref, own_ref, bottom_ref)


def last_fold_kernel(own_ref, from_up, from_down, folded_ref, left_ref, right_ref):
    planes, blocks, rows, _ = own_ref.shape
    half = rows // 2
    low = lane_ids((half, LANES)) < LANES // 2
    for plane in range(planes):
        for block in range(blocks):
            for lo, hi, values in fold_rows(own_ref, from_up, from_down, block, plane):
                folded_ref[plane, block, lo:hi, :] = values
        first = folded_ref[plane, 0]
        left_ref[plane] = jnp.where(low, first[:half], swap_halves(first[half:]))
        last = folded_ref[plane, blocks - 1]
        right_ref[plane] = jnp.where(low, swap_halves(last[half:]), last[:half])


def finish_kernel(field_ref, folded_ref, from_left, from_right, out_ref):
    planes, blocks, rows, _ = folded_ref.shape
    rim = (field_ref.shape[2] - rows) // 2
    half = rows // 2
    low = lane_ids((half, LANES)) < LANES // 2
    for plane in range(planes):
        for part in range(2):
            turned = []
            for block in range(blocks):
                values = folded_ref[plane, block, part * half : (part + 1) * half, :]
                if block == 0:
                    extra = from_left[plane]
                    values += extra if part == 0 else swap_halves(extra)
                if block == blocks - 1:
                    extra = from_right[plane]
                    values += extra if part == 0 else swap_halves(extra)
                old = field_ref[plane, block, rim + part * half : rim + (part + 1) * half, :]
                turned.append(swap_halves(old - values))
            for block in range(blocks - 1):
                out_ref[
                    plane, part * half : (part + 1) * half, block * LANES : (block + 1) * LANES
                ] = jnp.where(low, turned[block], turned[block + 1])


def f32(*shape):
    return jax.ShapeDtypeStruct(shape, jnp.float32)


def body(object_slices, probe, amplitudes, scan_pos, scan_count):
    layers, _, tile_r, tile_c = object_slices.shape
    planes = layers * 2
    frame = probe.shape[-1]
    rim = frame // 2
    blocks = tile_c // LANES + 1
    slots = amplitudes.shape[2]
    row_id, col_id = lax.axis_index("row"), lax.axis_index("col")
    amps = amplitudes[0, 0]
    flags = jnp.stack(
        [
            scan_count[0, 0],
            (col_id == 0).astype(jnp.int32),
            (col_id == lax.axis_size("col") - 1).astype(jnp.int32),
        ]
    )
    pos = jnp.stack(
        [
            scan_pos[0, 0, 0] - row_id * tile_r,
            scan_pos[1, 0, 0] - col_id * tile_c,
            jnp.pad(flags, (0, slots - 3)),
        ]
    )
    tables = jnp.asarray(transform_tables(frame))
    tile = object_slices.reshape(planes, tile_r, tile_c)

    left, right, up, down = pl.pallas_call(
        pack_kernel,
        out_shape=[f32(planes, tile_r // 2, LANES)] * 2 + [f32(planes, rim, tile_c)] * 2,
        in_specs=[vmem()],
        out_specs=[vmem()] * 4,
    )(tile)
    from_left = neighbour(right, "col", 1)
    from_right = neighbour(left, "col", -1)
    from_up = neighbour(down, "row", 1)
    from_down = neighbour(up, "row", -1)
    low = lane_ids((1, 1, LANES)) < LANES // 2
    lower, upper = slice(0, rim), slice(tile_r // 2 - rim, tile_r // 2)
    corner_down = neighbour(jnp.where(low, from_left[:, lower], from_right[:, lower]), "row", -1)
    corner_up = neighbour(jnp.where(low, from_right[:, upper], from_left[:, upper]), "row", 1)

    work = [pltpu.VMEM((planes, blocks, tile_r + frame, LANES), jnp.float32)] + [
        pltpu.VMEM((GROUP, 2, frame, frame), jnp.float32)
    ] * 4
    outs = [
        f32(planes, blocks, tile_r + frame, LANES),
        f32(planes, blocks, rim, LANES),
        f32(planes, blocks, tile_r, LANES),
        f32(planes, blocks, rim, LANES),
    ]
    field, top, own, bottom = pl.pallas_call(
        first_kernel,
        out_shape=outs,
        in_specs=[smem()] + [vmem()] * 10,
        out_specs=[vmem()] * 4,
        scratch_shapes=work,
    )(pos, tile, from_left, from_right, from_up, from_down, corner_up, corner_down, amps, probe, tables)

    for iteration in range(1, ITERS):
        from_up = neighbour(bottom, "row", 1)
        from_down = neighbour(top, "row", -1)
        left, mid, right = pl.pallas_call(
            fold_kernel,
            out_shape=[
                f32(planes, tile_r, LANES),
                f32(planes, blocks - 2, tile_r, LANES),
                f32(planes, tile_r, LANES),
            ],
            in_specs=[vmem()] * 3,
            out_specs=[vmem()] * 3,
        )(own, from_up, from_down)
        from_left = neighbour(right, "col", 1)
        from_right = neighbour(left, "col", -1)
        total, up, down = pl.pallas_call(
            total_kernel,
            out_shape=[
                f32(planes, blocks, tile_r, LANES),
                f32(planes, blocks, rim, LANES),
                f32(planes, blocks, rim, LANES),
            ],
            in_specs=[vmem()] * 5,
            out_specs=[vmem()] * 3,
        )(left, mid, right, from_left, from_right)
        from_up = neighbour(down, "row", 1)
        from_down = neighbour(up, "row", -1)
        field, top, own, bottom = pl.pallas_call(
            next_kernel,
            out_shape=outs,
            in_specs=[smem()] + [vmem()] * 7,
            out_specs=[vmem()] * 4,
            scratch_shapes=work,
        )(pos, field, total, from_up, from_down, amps, probe, tables)

    from_up = neighbour(bottom, "row", 1)
    from_down = neighbour(top, "row", -1)
    folded, left, right = pl.pallas_call(
        last_fold_kernel,
        out_shape=[
            f32(planes, blocks, tile_r, LANES),
            f32(planes, tile_r // 2, LANES),
            f32(planes, tile_r // 2, LANES),
        ],
        in_specs=[vmem()] * 3,
        out_specs=[vmem()] * 3,
    )(own, from_up, from_down)
    from_left = neighbour(right, "col", 1)
    from_right = neighbour(left, "col", -1)
    out = pl.pallas_call(
        finish_kernel,
        out_shape=f32(planes, tile_r, tile_c),
        in_specs=[vmem()] * 4,
        out_specs=vmem(),
    )(field, folded, from_left, from_right)
    return out.reshape(object_slices.shape)


def solution(mesh):
    in_specs = (
        P(None, None, "row", "col"),
        P(),
        P("row", "col", None, None, None),
        P(None, "row", "col", None),
        P("row", "col"),
    )
    out_specs = P(None, None, "row", "col")
    return jax.shard_map(body, mesh=mesh, in_specs=in_specs, out_specs=out_specs, check_vma=False)
```

time: 898 us -> 158 us (0.18); the launches traced: 882 us -> 157 us
  local copies, waits for them, and re-layouts: 360 us -> 4.53 us
  matrix products: 202 us -> 0 us
  loops' own time: 126 us -> 0 us
  other arithmetic: 71.5 us -> 1.39 us
  Pallas kernels: 0 us -> 50.5 us
  waiting for transfers between devices: 79.2 us -> 48 us
  starting transfers between devices: 40.7 us -> 51.6 us
    dot_general x96 -> x0, matrix products: 202 us -> none  [the longest x48 106 us: apply_left(): return jnp.einsum('jk,bkl->bjl', matrix, values, precision=highest)]
    dynamic_update_slice x32 -> x0, local copies, waits for them, and re-layouts: 138 us -> none  [add_one(): lax.dynamic_update_slice(accumulator, current_block + gradients[item], co...]
    gather x160 -> x0, local copies, waits for them, and re-layouts: 128 us -> none
    another operation x4 -> x0, loops' own time: 126 us -> none  [the longest x2 125 us: place_patches(): lax.fori_loop(0, gradients.shape[0], add_one, jnp.zeros(ext_shape, jnp.fl...]
    pallas_call x0 -> x7, Pallas kernels: none -> 50.5 us  [the longest x1 17.7 us: body(): pl.pallas_call(next_kernel, out_shape=outs, in_specs=[smem()] + [vmem()]...]
    add x36 -> x0, other arithmetic: 45.5 us -> none  [the longest x32 41.4 us: add_one(): current_block + gradients[item]]
    dynamic_slice x64 -> x0, local copies, waits for them, and re-layouts: 37.5 us -> none  [add_one(): corner = (zero_index, zero_index, patch_row[item], patch_col[item])]
    ppermute x16, waiting for transfers between devices: 79.2 us -> 48 us  [neighbour(): return lax.ppermute(values, axis, pairs)]
  transfers between devices with their start and end apart: 16 -> 16, of which waited for: 10 -> 12; matrix products, arithmetic and copies ran while one was open for 1% -> 1% of each run, Pallas kernels for 0% -> 0%
where the time goes in v1:
time: 158 us; the launch traced here: 157 us
  starting transfers between devices  51.6 us (33%)
  Pallas kernels  50.5 us (32%)
  waiting for transfers between devices  48 us (30%)
  local copies, waits for them, and re-layouts  4.53 us (3%)
    ppermute x16, starting transfers between devices, neighbour(): return lax.ppermute(values, axis, pairs)  51.6 us
    ppermute x16, waiting for transfers between devices, neighbour(): return lax.ppermute(values, axis, pairs)  48 us
    pallas_call x1, Pallas kernels, body(): pl.pallas_call(next_kernel, out_shape=outs, in_specs=[smem()] + [vmem()]...  17.7 us
    pallas_call x1, Pallas kernels, body(): pl.pallas_call(first_kernel, out_shape=outs, in_specs=[smem()] + [vmem()]...  17.3 us
    unnamed x32, local copies, waits for them, and re-layouts  4.53 us
    pallas_call x1, Pallas kernels, body(): pl.pallas_call(finish_kernel, out_shape=f32(planes, tile_r, tile_c), in_s...  4.14 us
    pallas_call x1, Pallas kernels, body(): pl.pallas_call(total_kernel, out_shape=[f32(planes, blocks, tile_r, LANES...  3.19 us
  transfers between devices with their start and end apart: 16, of which 12 were waited for; matrix products, arithmetic and copies ran while one was open for 1% of the time, Pallas kernels for 0%

profile of v1, /device:TPU:1, one launch (start us, length us, event | category | flops | bytes accessed | tf_op | source)
XLA Modules:
  0.0 156.9 jit_solution(7645766062949451784)
XLA Ops:
  2.3 4.0 %collective-permute-start = (f32[4,128,128]{2,1,0:T(8,128)}, f32[4,128,128]{2,1,0:T(8,128)S(1)}, u32[]{:S(2)}, u32[]{:S(2)}) collective-permute-start(f32[4,128,128]{2,1,0:T(8,128)} %get-tuple-element.26), channel_id=1, source_target_pairs={{0,1},{1,2},{2,3},{3,4},{4,5},{5,6},{6,7},{8,9},{9,10},{10,11},{11... | collective-permute-start | bytes 786440 | tf_op jit(solution)/shard_map/ppermute | solution.py:50
  7.6 4.0 %collective-permute-start.2 = (f32[4,64,256]{2,1,0:T(8,128)}, f32[4,64,256]{2,1,0:T(8,128)S(1)}, u32[]{:S(2)}, u32[]{:S(2)}) collective-permute-start(f32[4,64,256]{2,1,0:T(8,128)} %get-tuple-element.28), channel_id=1, source_target_pairs={{0,8},{8,16},{16,24},{1,9},{9,17},{17,25},{2,10},{10,18},{18,26},{... | collective-permute-start | bytes 786440 | tf_op jit(solution)/shard_map/ppermute | solution.py:50
  15.4 5.3 %collective-permute-start.5 = (f32[4,64,128]{2,1,0:T(8,128)S(1)}, f32[4,64,128]{2,1,0:T(8,128)S(1)}, u32[]{:S(2)}, u32[]{:S(2)}) collective-permute-start(f32[4,64,128]{2,1,0:T(8,128)S(1)} %get-tuple-element.47), channel_id=1, source_target_pairs={{8,0},{16,8},{24,16},{9,1},{17,9},{25,17},{10,2},{18,10},{26,18},{... | collective-permute-start | bytes 393224 | tf_op jit(solution)/shard_map/ppermute | solution.py:50
  20.7 3.0 %collective-permute-start.4 = (f32[4,64,128]{2,1,0:T(8,128)S(1)}, f32[4,64,128]{2,1,0:T(8,128)S(1)}, u32[]{:S(2)}, u32[]{:S(2)}) collective-permute-start(f32[4,64,128]{2,1,0:T(8,128)S(1)} %get-tuple-element.48), channel_id=1, source_target_pairs={{0,8},{8,16},{16,24},{1,9},{9,17},{17,25},{2,10},{10,18},{18,26},{... | collective-permute-start | bytes 393224 | tf_op jit(solution)/shard_map/ppermute | solution.py:50
  26.3 17.3 %shard_map.65 = (f32[4,3,384,128]{3,2,1,0:T(8,128)}, f32[4,3,64,128]{3,2,1,0:T(8,128)}, f32[4,3,256,128]{3,2,1,0:T(8,128)}, f32[4,3,64,128]{3,2,1,0:T(8,128)}) custom-call(s32[3,16]{1,0:T(4,128)} %pad_add_fusion.pos_ref, f32[4,256,256]{2,1,0:T(8,128)} %bitcast.16, f32[4,128,128]{2,1,0:T(8,128)} %copy-done, f32[4,128,128]{2,1,0:T(8,128)} %copy-done.1, ...), custom_call_target="tpu_custom_call" | custom-call | tf_op jit(solution)/shard_map/pallas_call | solution.py:387
  45.5 2.4 %collective-permute-start.7 = (f32[4,3,64,128]{3,2,1,0:T(8,128)}, f32[4,3,64,128]{3,2,1,0:T(8,128)S(1)}, u32[]{:S(2)}, u32[]{:S(2)}) collective-permute-start(f32[4,3,64,128]{3,2,1,0:T(8,128)} %get-tuple-element.33), channel_id=1, source_target_pairs={{8,0},{16,8},{24,16},{9,1},{17,9},{25,17},{10,2},{18,10},{26,18},{... | collective-permute-start | bytes 1179656 | tf_op jit(solution)/shard_map/ppermute | solution.py:50
  47.9 2.6 %collective-permute-done.6.from_up = f32[4,3,64,128]{3,2,1,0:T(8,128)S(1)} collective-permute-done((f32[4,3,64,128]{3,2,1,0:T(8,128)}, f32[4,3,64,128]{3,2,1,0:T(8,128)S(1)}, u32[]{:S(2)}, u32[]{:S(2)}) %collective-permute-start.6) | collective-permute-done | bytes 393248 | tf_op jit(solution)/shard_map/ppermute | solution.py:50
  50.5 4.3 %collective-permute-done.7.from_down = f32[4,3,64,128]{3,2,1,0:T(8,128)S(1)} collective-permute-done((f32[4,3,64,128]{3,2,1,0:T(8,128)}, f32[4,3,64,128]{3,2,1,0:T(8,128)S(1)}, u32[]{:S(2)}, u32[]{:S(2)}) %collective-permute-start.7) | collective-permute-done | bytes 393248 | tf_op jit(solution)/shard_map/ppermute | solution.py:50
  55.6 2.8 %shard_map.66 = (f32[4,256,128]{2,1,0:T(8,128)}, f32[4,1,256,128]{3,2,1,0:T(8,128)}, f32[4,256,128]{2,1,0:T(8,128)}) custom-call(f32[4,3,256,128]{3,2,1,0:T(8,128)} %get-tuple-element.31.own_ref, f32[4,3,64,128]{3,2,1,0:T(8,128)} %copy-done.6, f32[4,3,64,128]{3,2,1,0:T(8,128)} %copy-done.8), custom_call_target="tpu_custom_call" | custom-call | tf_op jit(solution)/shard_map/pallas_call | solution.py:398
  59.6 8.7 %collective-permute-start.8 = (f32[4,256,128]{2,1,0:T(8,128)}, f32[4,256,128]{2,1,0:T(8,128)S(1)}, u32[]{:S(2)}, u32[]{:S(2)}) collective-permute-start(f32[4,256,128]{2,1,0:T(8,128)} %get-tuple-element.36.right_ref), channel_id=1, source_target_pairs={{0,1},{1,2},{2,3},{3,4},{4,5},{5,6},{6,7},{8,9},{9,10},{10,11},{11... | collective-permute-start | bytes 1572872 | tf_op jit(solution)/shard_map/ppermute | solution.py:50
  68.3 5.6 %collective-permute-done.9.from_right = f32[4,256,128]{2,1,0:T(8,128)S(1)} collective-permute-done((f32[4,256,128]{2,1,0:T(8,128)}, f32[4,256,128]{2,1,0:T(8,128)S(1)}, u32[]{:S(2)}, u32[]{:S(2)}) %collective-permute-start.9) | collective-permute-done | bytes 524320 | tf_op jit(solution)/shard_map/ppermute | solution.py:50
  74.0 12.1 %collective-permute-done.8.from_left = f32[4,256,128]{2,1,0:T(8,128)S(1)} collective-permute-done((f32[4,256,128]{2,1,0:T(8,128)}, f32[4,256,128]{2,1,0:T(8,128)S(1)}, u32[]{:S(2)}, u32[]{:S(2)}) %collective-permute-start.8) | collective-permute-done | bytes 524320 | tf_op jit(solution)/shard_map/ppermute | solution.py:50
  86.8 3.2 %shard_map.67 = (f32[4,3,256,128]{3,2,1,0:T(8,128)}, f32[4,3,64,128]{3,2,1,0:T(8,128)}, f32[4,3,64,128]{3,2,1,0:T(8,128)}) custom-call(f32[4,256,128]{2,1,0:T(8,128)} %get-tuple-element.34.left_ref, f32[4,1,256,128]{3,2,1,0:T(8,128)} %get-tuple-element.35.mid_ref, f32[4,256,128]{2,1,0:T(8,128)} %get-tuple-element.36.right_ref, f32[4,256,128]{2,1,0:T(8,128)} %copy-done.3, ...), custom_call_target="tpu_custom_call" | custom-call | tf_op jit(solution)/shard_map/pallas_call | solution.py:410
  91.9 2.4 %collective-permute-start.11 = (f32[4,3,64,128]{3,2,1,0:T(8,128)}, f32[4,3,64,128]{3,2,1,0:T(8,128)S(1)}, u32[]{:S(2)}, u32[]{:S(2)}) collective-permute-start(f32[4,3,64,128]{3,2,1,0:T(8,128)} %get-tuple-element.39), channel_id=1, source_target_pairs={{8,0},{16,8},{24,16},{9,1},{17,9},{25,17},{10,2},{18,10},{26,18},{... | collective-permute-start | bytes 1179656 | tf_op jit(solution)/shard_map/ppermute | solution.py:50
  94.4 2.6 %collective-permute-done.10.from_up = f32[4,3,64,128]{3,2,1,0:T(8,128)S(1)} collective-permute-done((f32[4,3,64,128]{3,2,1,0:T(8,128)}, f32[4,3,64,128]{3,2,1,0:T(8,128)S(1)}, u32[]{:S(2)}, u32[]{:S(2)}) %collective-permute-start.10) | collective-permute-done | bytes 393248 | tf_op jit(solution)/shard_map/ppermute | solution.py:50
  97.0 4.3 %collective-permute-done.11.from_down = f32[4,3,64,128]{3,2,1,0:T(8,128)S(1)} collective-permute-done((f32[4,3,64,128]{3,2,1,0:T(8,128)}, f32[4,3,64,128]{3,2,1,0:T(8,128)S(1)}, u32[]{:S(2)}, u32[]{:S(2)}) %collective-permute-start.11) | collective-permute-done | bytes 393248 | tf_op jit(solution)/shard_map/ppermute | solution.py:50
  102.0 17.7 %shard_map.68 = (f32[4,3,384,128]{3,2,1,0:T(8,128)}, f32[4,3,64,128]{3,2,1,0:T(8,128)}, f32[4,3,256,128]{3,2,1,0:T(8,128)}, f32[4,3,64,128]{3,2,1,0:T(8,128)}) custom-call(s32[3,16]{1,0:T(4,128)} %pad_add_fusion.pos_ref, f32[4,3,384,128]{3,2,1,0:T(8,128)} %get-tuple-element.30.old_ref, f32[4,3,256,128]{3,2,1,0:T(8,128)} %get-tuple-element.37.total_ref, ...), custom_call_target="tpu_custom_call" | custom-call | tf_op jit(solution)/shard_map/pallas_call | solution.py:422
  121.6 2.4 %collective-permute-start.13 = (f32[4,3,64,128]{3,2,1,0:T(8,128)}, f32[4,3,64,128]{3,2,1,0:T(8,128)S(1)}, u32[]{:S(2)}, u32[]{:S(2)}) collective-permute-start(f32[4,3,64,128]{3,2,1,0:T(8,128)} %get-tuple-element.43), channel_id=1, source_target_pairs={{8,0},{16,8},{24,16},{9,1},{17,9},{25,17},{10,2},{18,10},{26,18},{... | collective-permute-start | bytes 1179656 | tf_op jit(solution)/shard_map/ppermute | solution.py:50
  124.1 2.6 %collective-permute-done.12.from_up = f32[4,3,64,128]{3,2,1,0:T(8,128)S(1)} collective-permute-done((f32[4,3,64,128]{3,2,1,0:T(8,128)}, f32[4,3,64,128]{3,2,1,0:T(8,128)S(1)}, u32[]{:S(2)}, u32[]{:S(2)}) %collective-permute-start.12) | collective-permute-done | bytes 393248 | tf_op jit(solution)/shard_map/ppermute | solution.py:50
  126.7 4.3 %collective-permute-done.13.from_down = f32[4,3,64,128]{3,2,1,0:T(8,128)S(1)} collective-permute-done((f32[4,3,64,128]{3,2,1,0:T(8,128)}, f32[4,3,64,128]{3,2,1,0:T(8,128)S(1)}, u32[]{:S(2)}, u32[]{:S(2)}) %collective-permute-start.13) | collective-permute-done | bytes 393248 | tf_op jit(solution)/shard_map/ppermute | solution.py:50
  131.7 3.1 %shard_map.69 = (f32[4,3,256,128]{3,2,1,0:T(8,128)}, f32[4,128,128]{2,1,0:T(8,128)}, f32[4,128,128]{2,1,0:T(8,128)}) custom-call(f32[4,3,256,128]{3,2,1,0:T(8,128)} %get-tuple-element.41.own_ref, f32[4,3,64,128]{3,2,1,0:T(8,128)} %copy-done.7, f32[4,3,64,128]{3,2,1,0:T(8,128)} %copy-done.9), custom_call_target="tpu_custom_call" | custom-call | tf_op jit(solution)/shard_map/pallas_call | solution.py:432
  134.8 7.9 %collective-permute-start.14 = (f32[4,128,128]{2,1,0:T(8,128)}, f32[4,128,128]{2,1,0:T(8,128)S(1)}, u32[]{:S(2)}, u32[]{:S(2)}) collective-permute-start(f32[4,128,128]{2,1,0:T(8,128)} %get-tuple-element.45), channel_id=1, source_target_pairs={{0,1},{1,2},{2,3},{3,4},{4,5},{5,6},{6,7},{8,9},{9,10},{10,11},{11... | collective-permute-start | bytes 786440 | tf_op jit(solution)/shard_map/ppermute | solution.py:50
  144.0 7.9 %collective-permute-done.14.from_left = f32[4,128,128]{2,1,0:T(8,128)S(1)} collective-permute-done((f32[4,128,128]{2,1,0:T(8,128)}, f32[4,128,128]{2,1,0:T(8,128)S(1)}, u32[]{:S(2)}, u32[]{:S(2)}) %collective-permute-start.14) | collective-permute-done | bytes 262176 | tf_op jit(solution)/shard_map/ppermute | solution.py:50
  152.7 4.1 %shard_map.70 = f32[4,256,256]{2,1,0:T(8,128)} custom-call(f32[4,3,384,128]{3,2,1,0:T(8,128)} %get-tuple-element.40.field_ref, f32[4,3,256,128]{3,2,1,0:T(8,128)} %get-tuple-element.44.folded_ref, f32[4,128,128]{2,1,0:T(8,128)} %copy-done.12, f32[4,128,128]{2,1,0:T(8,128)} %copy-done.13), custom_call_target="tpu_custom_call" | custom-call | tf_op jit(solution)/shard_map/pallas_call | solution.py:444
  (53 shorter events, 21.5 us)
Async XLA Ops:
  2.3 12.6 %collective-permute-start = (f32[4,128,128]{2,1,0:T(8,128)}, f32[4,128,128]{2,1,0:T(8,128)S(1)}, u32[]{:S(2)}, u32[]{:S(2)}) collective-permute-start(f32[4,128,128]{2,1,0:T(8,128)} %get-tuple-element.26), channel_id=1, source_target_pairs={{0,1},{1,2},{2,3},{3,4},{4,5},{5,6},{6,7},{8,9},{9,10},{10,11},{11... | collective-permute-start | bytes 786440 | tf_op jit(solution)/shard_map/ppermute | solution.py:50
  6.3 9.0 %collective-permute-start.1 = (f32[4,128,128]{2,1,0:T(8,128)}, f32[4,128,128]{2,1,0:T(8,128)S(1)}, u32[]{:S(2)}, u32[]{:S(2)}) collective-permute-start(f32[4,128,128]{2,1,0:T(8,128)} %get-tuple-element.27), channel_id=1, source_target_pairs={{1,0},{2,1},{3,2},{4,3},{5,4},{6,5},{7,6},{9,8},{10,9},{11,10},{12... | collective-permute-start | bytes 786440 | tf_op jit(solution)/shard_map/ppermute | solution.py:50
  7.6 16.7 %collective-permute-start.2 = (f32[4,64,256]{2,1,0:T(8,128)}, f32[4,64,256]{2,1,0:T(8,128)S(1)}, u32[]{:S(2)}, u32[]{:S(2)}) collective-permute-start(f32[4,64,256]{2,1,0:T(8,128)} %get-tuple-element.28), channel_id=1, source_target_pairs={{0,8},{8,16},{16,24},{1,9},{9,17},{17,25},{2,10},{10,18},{18,26},{... | collective-permute-start | bytes 786440 | tf_op jit(solution)/shard_map/ppermute | solution.py:50
  11.6 12.8 %collective-permute-start.3 = (f32[4,64,256]{2,1,0:T(8,128)}, f32[4,64,256]{2,1,0:T(8,128)S(1)}, u32[]{:S(2)}, u32[]{:S(2)}) collective-permute-start(f32[4,64,256]{2,1,0:T(8,128)} %get-tuple-element.29), channel_id=1, source_target_pairs={{8,0},{16,8},{24,16},{9,1},{17,9},{25,17},{10,2},{18,10},{26,18},{... | collective-permute-start | bytes 786440 | tf_op jit(solution)/shard_map/ppermute | solution.py:50
  14.9 10.7 %copy-start = (f32[4,128,128]{2,1,0:T(8,128)}, f32[4,128,128]{2,1,0:T(8,128)S(1)}, u32[]{:S(2)}) copy-start(f32[4,128,128]{2,1,0:T(8,128)S(1)} %collective-permute-done.from_left) | copy-start | bytes 786436
  15.3 10.3 %copy-start.1 = (f32[4,128,128]{2,1,0:T(8,128)}, f32[4,128,128]{2,1,0:T(8,128)S(1)}, u32[]{:S(2)}) copy-start(f32[4,128,128]{2,1,0:T(8,128)S(1)} %collective-permute-done.1.from_right) | copy-start | bytes 786436
  15.4 9.1 %collective-permute-start.5 = (f32[4,64,128]{2,1,0:T(8,128)S(1)}, f32[4,64,128]{2,1,0:T(8,128)S(1)}, u32[]{:S(2)}, u32[]{:S(2)}) collective-permute-start(f32[4,64,128]{2,1,0:T(8,128)S(1)} %get-tuple-element.47), channel_id=1, source_target_pairs={{8,0},{16,8},{24,16},{9,1},{17,9},{25,17},{10,2},{18,10},{26,18},{... | collective-permute-start | bytes 393224 | tf_op jit(solution)/shard_map/ppermute | solution.py:50
  20.7 5.0 %collective-permute-start.4 = (f32[4,64,128]{2,1,0:T(8,128)S(1)}, f32[4,64,128]{2,1,0:T(8,128)S(1)}, u32[]{:S(2)}, u32[]{:S(2)}) collective-permute-start(f32[4,64,128]{2,1,0:T(8,128)S(1)} %get-tuple-element.48), channel_id=1, source_target_pairs={{0,8},{8,16},{16,24},{1,9},{9,17},{17,25},{2,10},{10,18},{18,26},{... | collective-permute-start | bytes 393224 | tf_op jit(solution)/shard_map/ppermute | solution.py:50
  24.3 1.3 copy-start.10
  24.3 1.3 copy-start.11
  43.6 6.9 %collective-permute-start.6 = (f32[4,3,64,128]{3,2,1,0:T(8,128)}, f32[4,3,64,128]{3,2,1,0:T(8,128)S(1)}, u32[]{:S(2)}, u32[]{:S(2)}) collective-permute-start(f32[4,3,64,128]{3,2,1,0:T(8,128)} %get-tuple-element.32), channel_id=1, source_target_pairs={{0,8},{8,16},{16,24},{1,9},{9,17},{17,25},{2,10},{10,18},{18,26},{... | collective-permute-start | bytes 1179656 | tf_op jit(solution)/shard_map/ppermute | solution.py:50
  45.5 9.3 %collective-permute-start.7 = (f32[4,3,64,128]{3,2,1,0:T(8,128)}, f32[4,3,64,128]{3,2,1,0:T(8,128)S(1)}, u32[]{:S(2)}, u32[]{:S(2)}) collective-permute-start(f32[4,3,64,128]{3,2,1,0:T(8,128)} %get-tuple-element.33), channel_id=1, source_target_pairs={{8,0},{16,8},{24,16},{9,1},{17,9},{25,17},{10,2},{18,10},{26,18},{... | collective-permute-start | bytes 1179656 | tf_op jit(solution)/shard_map/ppermute | solution.py:50
  50.5 4.3 %copy-start.6 = (f32[4,3,64,128]{3,2,1,0:T(8,128)}, f32[4,3,64,128]{3,2,1,0:T(8,128)S(1)}, u32[]{:S(2)}) copy-start(f32[4,3,64,128]{3,2,1,0:T(8,128)S(1)} %collective-permute-done.6.from_up) | copy-start | bytes 1179652
  58.4 15.6 %collective-permute-start.9 = (f32[4,256,128]{2,1,0:T(8,128)}, f32[4,256,128]{2,1,0:T(8,128)S(1)}, u32[]{:S(2)}, u32[]{:S(2)}) collective-permute-start(f32[4,256,128]{2,1,0:T(8,128)} %get-tuple-element.34.left_ref), channel_id=1, source_target_pairs={{1,0},{2,1},{3,2},{4,3},{5,4},{6,5},{7,6},{9,8},{10,9},{11,10},{12... | collective-permute-start | bytes 1572872 | tf_op jit(solution)/shard_map/ppermute | solution.py:50
  59.6 26.4 %collective-permute-start.8 = (f32[4,256,128]{2,1,0:T(8,128)}, f32[4,256,128]{2,1,0:T(8,128)S(1)}, u32[]{:S(2)}, u32[]{:S(2)}) collective-permute-start(f32[4,256,128]{2,1,0:T(8,128)} %get-tuple-element.36.right_ref), channel_id=1, source_target_pairs={{0,1},{1,2},{2,3},{3,4},{4,5},{5,6},{6,7},{8,9},{9,10},{10,11},{11... | collective-permute-start | bytes 1572872 | tf_op jit(solution)/shard_map/ppermute | solution.py:50
  74.0 12.1 %copy-start.2 = (f32[4,256,128]{2,1,0:T(8,128)}, f32[4,256,128]{2,1,0:T(8,128)S(1)}, u32[]{:S(2)}) copy-start(f32[4,256,128]{2,1,0:T(8,128)S(1)} %collective-permute-done.9.from_right) | copy-start | bytes 1572868
  90.0 6.9 %collective-permute-start.10 = (f32[4,3,64,128]{3,2,1,0:T(8,128)}, f32[4,3,64,128]{3,2,1,0:T(8,128)S(1)}, u32[]{:S(2)}, u32[]{:S(2)}) collective-permute-start(f32[4,3,64,128]{3,2,1,0:T(8,128)} %get-tuple-element.38), channel_id=1, source_target_pairs={{0,8},{8,16},{16,24},{1,9},{9,17},{17,25},{2,10},{10,18},{18,26},{... | collective-permute-start | bytes 1179656 | tf_op jit(solution)/shard_map/ppermute | solution.py:50
  91.9 9.3 %collective-permute-start.11 = (f32[4,3,64,128]{3,2,1,0:T(8,128)}, f32[4,3,64,128]{3,2,1,0:T(8,128)S(1)}, u32[]{:S(2)}, u32[]{:S(2)}) collective-permute-start(f32[4,3,64,128]{3,2,1,0:T(8,128)} %get-tuple-element.39), channel_id=1, source_target_pairs={{8,0},{16,8},{24,16},{9,1},{17,9},{25,17},{10,2},{18,10},{26,18},{... | collective-permute-start | bytes 1179656 | tf_op jit(solution)/shard_map/ppermute | solution.py:50
  97.0 4.3 %copy-start.4 = (f32[4,3,64,128]{3,2,1,0:T(8,128)}, f32[4,3,64,128]{3,2,1,0:T(8,128)S(1)}, u32[]{:S(2)}) copy-start(f32[4,3,64,128]{3,2,1,0:T(8,128)S(1)} %collective-permute-done.10.from_up) | copy-start | bytes 1179652
  119.7 6.9 %collective-permute-start.12 = (f32[4,3,64,128]{3,2,1,0:T(8,128)}, f32[4,3,64,128]{3,2,1,0:T(8,128)S(1)}, u32[]{:S(2)}, u32[]{:S(2)}) collective-permute-start(f32[4,3,64,128]{3,2,1,0:T(8,128)} %get-tuple-element.42), channel_id=1, source_target_pairs={{0,8},{8,16},{16,24},{1,9},{9,17},{17,25},{2,10},{10,18},{18,26},{... | collective-permute-start | bytes 1179656 | tf_op jit(solution)/shard_map/ppermute | solution.py:50
  121.6 9.3 %collective-permute-start.13 = (f32[4,3,64,128]{3,2,1,0:T(8,128)}, f32[4,3,64,128]{3,2,1,0:T(8,128)S(1)}, u32[]{:S(2)}, u32[]{:S(2)}) collective-permute-start(f32[4,3,64,128]{3,2,1,0:T(8,128)} %get-tuple-element.43), channel_id=1, source_target_pairs={{8,0},{16,8},{24,16},{9,1},{17,9},{25,17},{10,2},{18,10},{26,18},{... | collective-permute-start | bytes 1179656 | tf_op jit(solution)/shard_map/ppermute | solution.py:50
  126.7 4.3 %copy-start.7 = (f32[4,3,64,128]{3,2,1,0:T(8,128)}, f32[4,3,64,128]{3,2,1,0:T(8,128)S(1)}, u32[]{:S(2)}) copy-start(f32[4,3,64,128]{3,2,1,0:T(8,128)S(1)} %collective-permute-done.12.from_up) | copy-start | bytes 1179652
  134.8 17.1 %collective-permute-start.14 = (f32[4,128,128]{2,1,0:T(8,128)}, f32[4,128,128]{2,1,0:T(8,128)S(1)}, u32[]{:S(2)}, u32[]{:S(2)}) collective-permute-start(f32[4,128,128]{2,1,0:T(8,128)} %get-tuple-element.45), channel_id=1, source_target_pairs={{0,1},{1,2},{2,3},{3,4},{4,5},{5,6},{6,7},{8,9},{9,10},{10,11},{11... | collective-permute-start | bytes 786440 | tf_op jit(solution)/shard_map/ppermute | solution.py:50
  142.7 9.3 %collective-permute-start.15 = (f32[4,128,128]{2,1,0:T(8,128)}, f32[4,128,128]{2,1,0:T(8,128)S(1)}, u32[]{:S(2)}, u32[]{:S(2)}) collective-permute-start(f32[4,128,128]{2,1,0:T(8,128)} %get-tuple-element.46), channel_id=1, source_target_pairs={{1,0},{2,1},{3,2},{4,3},{5,4},{6,5},{7,6},{9,8},{10,9},{11,10},{12... | collective-permute-start | bytes 786440 | tf_op jit(solution)/shard_map/ppermute | solution.py:50
  (8 other events, 6.5 us)

commit v2 on v1

--- a/solution.py
+++ b/solution.py
@@ -331,7 +331,15 @@
 
 
 def f32(*shape):
-    return jax.ShapeDtypeStruct(shape, jnp.float32)
+    return pltpu.VMEM(shape, jnp.float32)
+
+
+def on_chip(*arrays):
+    return [pltpu.with_memory_space_constraint(array, pltpu.VMEM) for array in arrays]
+
+
+def limit(mib):
+    return pltpu.CompilerParams(vmem_limit_bytes=mib << 20)
 
 
 def body(object_slices, probe, amplitudes, scan_pos, scan_count):
@@ -365,7 +373,8 @@
         out_shape=[f32(planes, tile_r // 2, LANES)] * 2 + [f32(planes, rim, tile_c)] * 2,
         in_specs=[vmem()],
         out_specs=[vmem()] * 4,
-    )(tile)
+        compiler_params=limit(4),
+    )(*on_chip(tile))
     from_left = neighbour(right, "col", 1)
     from_right = neighbour(left, "col", -1)
     from_up = neighbour(down, "row", 1)
@@ -390,7 +399,14 @@
         in_specs=[smem()] + [vmem()] * 10,
         out_specs=[vmem()] * 4,
         scratch_shapes=work,
-    )(pos, tile, from_left, from_right, from_up, from_down, corner_up, corner_down, amps, probe, tables)
+        compiler_params=limit(20),
+    )(
+        pos,
+        *on_chip(
+            tile, from_left, from_right, from_up, from_down, corner_up, corner_down,
+            amps, probe, tables,
+        ),
+    )
 
     for iteration in range(1, ITERS):
         from_up = neighbour(bottom, "row", 1)
@@ -404,7 +420,8 @@
             ],
             in_specs=[vmem()] * 3,
             out_specs=[vmem()] * 3,
-        )(own, from_up, from_down)
+            compiler_params=limit(4),
+        )(*on_chip(own, from_up, from_down))
         from_left = neighbour(right, "col", 1)
         from_right = neighbour(left, "col", -1)
         total, up, down = pl.pallas_call(
@@ -416,7 +433,8 @@
             ],
             in_specs=[vmem()] * 5,
             out_specs=[vmem()] * 3,
-        )(left, mid, right, from_left, from_right)
+            compiler_params=limit(4),
+        )(*on_chip(left, mid, right, from_left, from_right))
         from_up = neighbour(down, "row", 1)
         from_down = neighbour(up, "row", -1)
         field, top, own, bottom = pl.pallas_call(
@@ -425,7 +443,8 @@
             in_specs=[smem()] + [vmem()] * 7,
             out_specs=[vmem()] * 4,
             scratch_shapes=work,
-        )(pos, field, total, from_up, from_down, amps, probe, tables)
+            compiler_params=limit(20),
+        )(pos, *on_chip(field, total, from_up, from_down, amps, probe, tables))
 
     from_up = neighbour(bottom, "row", 1)
     from_down = neighbour(top, "row", -1)
@@ -438,15 +457,17 @@
         ],
         in_specs=[vmem()] * 3,
         out_specs=[vmem()] * 3,
-    )(own, from_up, from_down)
+            compiler_params=limit(4),
+    )(*on_chip(own, from_up, from_down))
     from_left = neighbour(right, "col", 1)
     from_right = neighbour(left, "col", -1)
     out = pl.pallas_call(
         finish_kernel,
-        out_shape=f32(planes, tile_r, tile_c),
+        out_shape=jax.ShapeDtypeStruct((planes, tile_r, tile_c), jnp.float32),
         in_specs=[vmem()] * 4,
         out_specs=vmem(),
-    )(field, folded, from_left, from_right)
+        compiler_params=limit(8),
+    )(*on_chip(field, folded, from_left, from_right))
     return out.reshape(object_slices.shape)
 
 

time: 158 us -> 135 us (0.85)
  Pallas kernels: 50.5 us -> 29.6 us
  waiting for transfers between devices: 48 us -> 45.8 us
  starting transfers between devices: 51.6 us -> 53.3 us
    pallas_call x1, Pallas kernels: 17.7 us -> 13.3 us  [body(): pl.pallas_call(next_kernel, out_shape=outs, in_specs=[smem()] + [vmem()]...]
    pallas_call x1, Pallas kernels: 17.3 us -> 13.6 us  [body(): pl.pallas_call(first_kernel, out_shape=outs, in_specs=[smem()] + [vmem()]...]
    pallas_call x1, Pallas kernels: 3.19 us -> 0.16 us  [body(): pl.pallas_call(total_kernel, out_shape=[f32(planes, blocks, tile_r, LANES...]
    pallas_call x1, Pallas kernels: 3.09 us -> 0.23 us  [body(): pl.pallas_call(last_fold_kernel, out_shape=[f32(planes, blocks, tile_r, L...]
    pallas_call x1, Pallas kernels: 2.77 us -> 0.13 us  [body(): pl.pallas_call(fold_kernel, out_shape=[f32(planes, tile_r, LANES), f32(pl...]
    ppermute x16, waiting for transfers between devices: 48 us -> 45.8 us  [neighbour(): return lax.ppermute(values, axis, pairs)]
    pallas_call x1, Pallas kernels: 4.14 us -> 1.94 us  [body(): pl.pallas_call(finish_kernel, out_shape=jax.ShapeDtypeStruct((planes, til...]
    pallas_call x1, Pallas kernels: 2.34 us -> 0.2 us  [body(): pl.pallas_call(pack_kernel, out_shape=[f32(planes, tile_r // 2, LANES)] *...]
where the time goes in v2:
time: 135 us; the launch traced here: 134 us
  starting transfers between devices  53.3 us (39%)
  waiting for transfers between devices  45.8 us (34%)
  Pallas kernels  29.6 us (22%)
  local copies, waits for them, and re-layouts  3.78 us (3%)
    ppermute x16, starting transfers between devices, neighbour(): return lax.ppermute(values, axis, pairs)  53.3 us
    ppermute x16, waiting for transfers between devices, neighbour(): return lax.ppermute(values, axis, pairs)  45.8 us
    pallas_call x1, Pallas kernels, body(): pl.pallas_call(first_kernel, out_shape=outs, in_specs=[smem()] + [vmem()]...  13.6 us
    pallas_call x1, Pallas kernels, body(): pl.pallas_call(next_kernel, out_shape=outs, in_specs=[smem()] + [vmem()]...  13.3 us
    unnamed x12, local copies, waits for them, and re-layouts  3.78 us
  transfers between devices with their start and end apart: 16, of which 12 were waited for; matrix products, arithmetic and copies ran while one was open for 1% of the time, Pallas kernels for 0%

profile of v2, /device:TPU:1, one launch (start us, length us, event | category | flops | bytes accessed | tf_op | source)
XLA Modules:
  0.0 134.1 jit_solution(6267295651201257442)
XLA Ops:
  1.5 4.0 %collective-permute-start = (f32[4,128,128]{2,1,0:T(8,128)S(1)}, f32[4,128,128]{2,1,0:T(8,128)S(1)}, u32[]{:S(2)}, u32[]{:S(2)}) collective-permute-start(f32[4,128,128]{2,1,0:T(8,128)S(1)} %get-tuple-element.26), channel_id=1, source_target_pairs={{0,1},{1,2},{2,3},{3,4},{4,5},{5,6},{6,7},{8,9},{9,10},{10,11},{11... | collective-permute-start | bytes 786440 | tf_op jit(solution)/shard_map/ppermute | solution.py:50
  6.8 4.0 %collective-permute-start.2 = (f32[4,64,256]{2,1,0:T(8,128)S(1)}, f32[4,64,256]{2,1,0:T(8,128)S(1)}, u32[]{:S(2)}, u32[]{:S(2)}) collective-permute-start(f32[4,64,256]{2,1,0:T(8,128)S(1)} %get-tuple-element.28), channel_id=1, source_target_pairs={{0,8},{8,16},{16,24},{1,9},{9,17},{17,25},{2,10},{10,18},{18,26},{... | collective-permute-start | bytes 786440 | tf_op jit(solution)/shard_map/ppermute | solution.py:50
  10.8 1.9 %collective-permute-start.3 = (f32[4,64,256]{2,1,0:T(8,128)S(1)}, f32[4,64,256]{2,1,0:T(8,128)S(1)}, u32[]{:S(2)}, u32[]{:S(2)}) collective-permute-start(f32[4,64,256]{2,1,0:T(8,128)S(1)} %get-tuple-element.29), channel_id=1, source_target_pairs={{8,0},{16,8},{24,16},{9,1},{17,9},{25,17},{10,2},{18,10},{26,18},{... | collective-permute-start | bytes 786440 | tf_op jit(solution)/shard_map/ppermute | solution.py:50
  14.3 5.2 %collective-permute-start.5 = (f32[4,64,128]{2,1,0:T(8,128)S(1)}, f32[4,64,128]{2,1,0:T(8,128)S(1)}, u32[]{:S(2)}, u32[]{:S(2)}) collective-permute-start(f32[4,64,128]{2,1,0:T(8,128)S(1)} %get-tuple-element.47), channel_id=1, source_target_pairs={{8,0},{16,8},{24,16},{9,1},{17,9},{25,17},{10,2},{18,10},{26,18},{... | collective-permute-start | bytes 393224 | tf_op jit(solution)/shard_map/ppermute | solution.py:50
  19.6 3.0 %collective-permute-start.4 = (f32[4,64,128]{2,1,0:T(8,128)S(1)}, f32[4,64,128]{2,1,0:T(8,128)S(1)}, u32[]{:S(2)}, u32[]{:S(2)}) collective-permute-start(f32[4,64,128]{2,1,0:T(8,128)S(1)} %get-tuple-element.48), channel_id=1, source_target_pairs={{0,8},{8,16},{16,24},{1,9},{9,17},{17,25},{2,10},{10,18},{18,26},{... | collective-permute-start | bytes 393224 | tf_op jit(solution)/shard_map/ppermute | solution.py:50
  27.0 13.6 %shard_map.65 = (f32[4,3,384,128]{3,2,1,0:T(8,128)S(1)}, f32[4,3,64,128]{3,2,1,0:T(8,128)S(1)}, f32[4,3,256,128]{3,2,1,0:T(8,128)S(1)}, f32[4,3,64,128]{3,2,1,0:T(8,128)S(1)}) custom-call(s32[3,16]{1,0:T(4,128)S(1)} %pad_add_fusion.pos_ref, f32[4,256,256]{2,1,0:T(8,128)S(1)} %bitcast.16, f32[4,128,128]{2,1,0:T(8,128)S(1)} %collective-permute-done.from_left, ...), custom_call_target="tpu_custom_call" | custom-call | tf_op jit(solution)/shard_map/pallas_call | solution.py:396
  40.6 1.9 %collective-permute-start.6 = (f32[4,3,64,128]{3,2,1,0:T(8,128)S(1)}, f32[4,3,64,128]{3,2,1,0:T(8,128)S(1)}, u32[]{:S(2)}, u32[]{:S(2)}) collective-permute-start(f32[4,3,64,128]{3,2,1,0:T(8,128)S(1)} %get-tuple-element.32), channel_id=1, source_target_pairs={{0,8},{8,16},{16,24},{1,9},{9,17},{17,25},{2,10},{10,18},{18,26},{... | collective-permute-start | bytes 1179656 | tf_op jit(solution)/shard_map/ppermute | solution.py:50
  42.5 3.8 %collective-permute-start.7 = (f32[4,3,64,128]{3,2,1,0:T(8,128)S(1)}, f32[4,3,64,128]{3,2,1,0:T(8,128)S(1)}, u32[]{:S(2)}, u32[]{:S(2)}) collective-permute-start(f32[4,3,64,128]{3,2,1,0:T(8,128)S(1)} %get-tuple-element.33), channel_id=1, source_target_pairs={{8,0},{16,8},{24,16},{9,1},{17,9},{25,17},{10,2},{18,10},{26,18},{... | collective-permute-start | bytes 1179656 | tf_op jit(solution)/shard_map/ppermute | solution.py:50
  47.2 4.4 %collective-permute-done.7.from_down = f32[4,3,64,128]{3,2,1,0:T(8,128)S(1)} collective-permute-done((f32[4,3,64,128]{3,2,1,0:T(8,128)S(1)}, f32[4,3,64,128]{3,2,1,0:T(8,128)S(1)}, u32[]{:S(2)}, u32[]{:S(2)}) %collective-permute-start.7) | collective-permute-done | bytes 393248 | tf_op jit(solution)/shard_map/ppermute | solution.py:50
  53.2 8.8 %collective-permute-start.8 = (f32[4,256,128]{2,1,0:T(8,128)S(1)}, f32[4,256,128]{2,1,0:T(8,128)S(1)}, u32[]{:S(2)}, u32[]{:S(2)}) collective-permute-start(f32[4,256,128]{2,1,0:T(8,128)S(1)} %get-tuple-element.36.right_ref), channel_id=1, source_target_pairs={{0,1},{1,2},{2,3},{3,4},{4,5},{5,6},{6,7},{8,9},{9,10},{10,11},{11... | collective-permute-start | bytes 1572872 | tf_op jit(solution)/shard_map/ppermute | solution.py:50
  62.0 5.4 %collective-permute-done.9.from_right = f32[4,256,128]{2,1,0:T(8,128)S(1)} collective-permute-done((f32[4,256,128]{2,1,0:T(8,128)S(1)}, f32[4,256,128]{2,1,0:T(8,128)S(1)}, u32[]{:S(2)}, u32[]{:S(2)}) %collective-permute-start.9) | collective-permute-done | bytes 524320 | tf_op jit(solution)/shard_map/ppermute | solution.py:50
  67.5 12.1 %collective-permute-done.8.from_left = f32[4,256,128]{2,1,0:T(8,128)S(1)} collective-permute-done((f32[4,256,128]{2,1,0:T(8,128)S(1)}, f32[4,256,128]{2,1,0:T(8,128)S(1)}, u32[]{:S(2)}, u32[]{:S(2)}) %collective-permute-start.8) | collective-permute-done | bytes 524320 | tf_op jit(solution)/shard_map/ppermute | solution.py:50
  79.7 1.9 %collective-permute-start.10 = (f32[4,3,64,128]{3,2,1,0:T(8,128)S(1)}, f32[4,3,64,128]{3,2,1,0:T(8,128)S(1)}, u32[]{:S(2)}, u32[]{:S(2)}) collective-permute-start(f32[4,3,64,128]{3,2,1,0:T(8,128)S(1)} %get-tuple-element.38), channel_id=1, source_target_pairs={{0,8},{8,16},{16,24},{1,9},{9,17},{17,25},{2,10},{10,18},{18,26},{... | collective-permute-start | bytes 1179656 | tf_op jit(solution)/shard_map/ppermute | solution.py:50
  81.6 2.4 %collective-permute-start.11 = (f32[4,3,64,128]{3,2,1,0:T(8,128)S(1)}, f32[4,3,64,128]{3,2,1,0:T(8,128)S(1)}, u32[]{:S(2)}, u32[]{:S(2)}) collective-permute-start(f32[4,3,64,128]{3,2,1,0:T(8,128)S(1)} %get-tuple-element.39), channel_id=1, source_target_pairs={{8,0},{16,8},{24,16},{9,1},{17,9},{25,17},{10,2},{18,10},{26,18},{... | collective-permute-start | bytes 1179656 | tf_op jit(solution)/shard_map/ppermute | solution.py:50
  84.1 2.3 %collective-permute-done.10.from_up = f32[4,3,64,128]{3,2,1,0:T(8,128)S(1)} collective-permute-done((f32[4,3,64,128]{3,2,1,0:T(8,128)S(1)}, f32[4,3,64,128]{3,2,1,0:T(8,128)S(1)}, u32[]{:S(2)}, u32[]{:S(2)}) %collective-permute-start.10) | collective-permute-done | bytes 393248 | tf_op jit(solution)/shard_map/ppermute | solution.py:50
  86.3 4.4 %collective-permute-done.11.from_down = f32[4,3,64,128]{3,2,1,0:T(8,128)S(1)} collective-permute-done((f32[4,3,64,128]{3,2,1,0:T(8,128)S(1)}, f32[4,3,64,128]{3,2,1,0:T(8,128)S(1)}, u32[]{:S(2)}, u32[]{:S(2)}) %collective-permute-start.11) | collective-permute-done | bytes 393248 | tf_op jit(solution)/shard_map/ppermute | solution.py:50
  90.7 13.3 %shard_map.68 = (f32[4,3,384,128]{3,2,1,0:T(8,128)S(1)}, f32[4,3,64,128]{3,2,1,0:T(8,128)S(1)}, f32[4,3,256,128]{3,2,1,0:T(8,128)S(1)}, f32[4,3,64,128]{3,2,1,0:T(8,128)S(1)}) custom-call(s32[3,16]{1,0:T(4,128)S(1)} %pad_add_fusion.pos_ref, f32[4,3,384,128]{3,2,1,0:T(8,128)S(1)} %get-tuple-element.30.old_ref, ...), custom_call_target="tpu_custom_call" | custom-call | tf_op jit(solution)/shard_map/pallas_call | solution.py:440
  104.0 1.9 %collective-permute-start.12 = (f32[4,3,64,128]{3,2,1,0:T(8,128)S(1)}, f32[4,3,64,128]{3,2,1,0:T(8,128)S(1)}, u32[]{:S(2)}, u32[]{:S(2)}) collective-permute-start(f32[4,3,64,128]{3,2,1,0:T(8,128)S(1)} %get-tuple-element.42), channel_id=1, source_target_pairs={{0,8},{8,16},{16,24},{1,9},{9,17},{17,25},{2,10},{10,18},{18,26},{... | collective-permute-start | bytes 1179656 | tf_op jit(solution)/shard_map/ppermute | solution.py:50
  106.0 2.4 %collective-permute-start.13 = (f32[4,3,64,128]{3,2,1,0:T(8,128)S(1)}, f32[4,3,64,128]{3,2,1,0:T(8,128)S(1)}, u32[]{:S(2)}, u32[]{:S(2)}) collective-permute-start(f32[4,3,64,128]{3,2,1,0:T(8,128)S(1)} %get-tuple-element.43), channel_id=1, source_target_pairs={{8,0},{16,8},{24,16},{9,1},{17,9},{25,17},{10,2},{18,10},{26,18},{... | collective-permute-start | bytes 1179656 | tf_op jit(solution)/shard_map/ppermute | solution.py:50
  108.4 2.3 %collective-permute-done.12.from_up = f32[4,3,64,128]{3,2,1,0:T(8,128)S(1)} collective-permute-done((f32[4,3,64,128]{3,2,1,0:T(8,128)S(1)}, f32[4,3,64,128]{3,2,1,0:T(8,128)S(1)}, u32[]{:S(2)}, u32[]{:S(2)}) %collective-permute-start.12) | collective-permute-done | bytes 393248 | tf_op jit(solution)/shard_map/ppermute | solution.py:50
  110.7 4.4 %collective-permute-done.13.from_down = f32[4,3,64,128]{3,2,1,0:T(8,128)S(1)} collective-permute-done((f32[4,3,64,128]{3,2,1,0:T(8,128)S(1)}, f32[4,3,64,128]{3,2,1,0:T(8,128)S(1)}, u32[]{:S(2)}, u32[]{:S(2)}) %collective-permute-start.13) | collective-permute-done | bytes 393248 | tf_op jit(solution)/shard_map/ppermute | solution.py:50
  115.3 8.0 %collective-permute-start.14 = (f32[4,128,128]{2,1,0:T(8,128)S(1)}, f32[4,128,128]{2,1,0:T(8,128)S(1)}, u32[]{:S(2)}, u32[]{:S(2)}) collective-permute-start(f32[4,128,128]{2,1,0:T(8,128)S(1)} %get-tuple-element.45), channel_id=1, source_target_pairs={{0,1},{1,2},{2,3},{3,4},{4,5},{5,6},{6,7},{8,9},{9,10},{10,11},{11... | collective-permute-start | bytes 786440 | tf_op jit(solution)/shard_map/ppermute | solution.py:50
  124.6 7.6 %collective-permute-done.14.from_left = f32[4,128,128]{2,1,0:T(8,128)S(1)} collective-permute-done((f32[4,128,128]{2,1,0:T(8,128)S(1)}, f32[4,128,128]{2,1,0:T(8,128)S(1)}, u32[]{:S(2)}, u32[]{:S(2)}) %collective-permute-start.14) | collective-permute-done | bytes 262176 | tf_op jit(solution)/shard_map/ppermute | solution.py:50
  132.2 1.9 %shard_map.70 = f32[4,256,256]{2,1,0:T(8,128)} custom-call(f32[4,3,384,128]{3,2,1,0:T(8,128)S(1)} %get-tuple-element.40.field_ref, f32[4,3,256,128]{3,2,1,0:T(8,128)S(1)} %get-tuple-element.44.folded_ref, f32[4,128,128]{2,1,0:T(8,128)S(1)} %collective-permute-done.14.from_left, f32[4,128,128]{2,1,0:T(8,128)S(1)} %collective-permute-done.15.from_right), custom_call_target="tpu_custom_call" | custom-call | tf_op jit(solution)/shard_map/pallas_call | solution.py:464
  (33 shorter events, 12.3 us)
Async XLA Ops:
  0.0 24.5 %copy-start = (f32[1,1,16,128,128]{4,3,2,1,0:T(8,128)S(1)}, f32[1,1,16,128,128]{4,3,2,1,0:T(8,128)}, u32[]{:S(2)}) copy-start(f32[1,1,16,128,128]{4,3,2,1,0:T(8,128)} %param.8) | copy-start | bytes 3145732
  0.0 1.3 copy-start.3
  1.3 23.2 %copy-start.5 = (f32[2,128,128]{2,1,0:T(8,128)S(1)}, f32[2,128,128]{2,1,0:T(8,128)}, u32[]{:S(2)}) copy-start(f32[2,128,128]{2,1,0:T(8,128)} %probe_ref.3) | copy-start | bytes 393220
  1.5 12.6 %collective-permute-start = (f32[4,128,128]{2,1,0:T(8,128)S(1)}, f32[4,128,128]{2,1,0:T(8,128)S(1)}, u32[]{:S(2)}, u32[]{:S(2)}) collective-permute-start(f32[4,128,128]{2,1,0:T(8,128)S(1)} %get-tuple-element.26), channel_id=1, source_target_pairs={{0,1},{1,2},{2,3},{3,4},{4,5},{5,6},{6,7},{8,9},{9,10},{10,11},{11... | collective-permute-start | bytes 786440 | tf_op jit(solution)/shard_map/ppermute | solution.py:50
  5.5 8.8 %collective-permute-start.1 = (f32[4,128,128]{2,1,0:T(8,128)S(1)}, f32[4,128,128]{2,1,0:T(8,128)S(1)}, u32[]{:S(2)}, u32[]{:S(2)}) collective-permute-start(f32[4,128,128]{2,1,0:T(8,128)S(1)} %get-tuple-element.27), channel_id=1, source_target_pairs={{1,0},{2,1},{3,2},{4,3},{5,4},{6,5},{7,6},{9,8},{10,9},{11,10},{12... | collective-permute-start | bytes 786440 | tf_op jit(solution)/shard_map/ppermute | solution.py:50
  6.8 15.8 %collective-permute-start.2 = (f32[4,64,256]{2,1,0:T(8,128)S(1)}, f32[4,64,256]{2,1,0:T(8,128)S(1)}, u32[]{:S(2)}, u32[]{:S(2)}) collective-permute-start(f32[4,64,256]{2,1,0:T(8,128)S(1)} %get-tuple-element.28), channel_id=1, source_target_pairs={{0,8},{8,16},{16,24},{1,9},{9,17},{17,25},{2,10},{10,18},{18,26},{... | collective-permute-start | bytes 786440 | tf_op jit(solution)/shard_map/ppermute | solution.py:50
  10.8 11.9 %collective-permute-start.3 = (f32[4,64,256]{2,1,0:T(8,128)S(1)}, f32[4,64,256]{2,1,0:T(8,128)S(1)}, u32[]{:S(2)}, u32[]{:S(2)}) collective-permute-start(f32[4,64,256]{2,1,0:T(8,128)S(1)} %get-tuple-element.29), channel_id=1, source_target_pairs={{8,0},{16,8},{24,16},{9,1},{17,9},{25,17},{10,2},{18,10},{26,18},{... | collective-permute-start | bytes 786440 | tf_op jit(solution)/shard_map/ppermute | solution.py:50
  14.3 9.0 %collective-permute-start.5 = (f32[4,64,128]{2,1,0:T(8,128)S(1)}, f32[4,64,128]{2,1,0:T(8,128)S(1)}, u32[]{:S(2)}, u32[]{:S(2)}) collective-permute-start(f32[4,64,128]{2,1,0:T(8,128)S(1)} %get-tuple-element.47), channel_id=1, source_target_pairs={{8,0},{16,8},{24,16},{9,1},{17,9},{25,17},{10,2},{18,10},{26,18},{... | collective-permute-start | bytes 393224 | tf_op jit(solution)/shard_map/ppermute | solution.py:50
  19.6 5.0 %collective-permute-start.4 = (f32[4,64,128]{2,1,0:T(8,128)S(1)}, f32[4,64,128]{2,1,0:T(8,128)S(1)}, u32[]{:S(2)}, u32[]{:S(2)}) collective-permute-start(f32[4,64,128]{2,1,0:T(8,128)S(1)} %get-tuple-element.48), channel_id=1, source_target_pairs={{0,8},{8,16},{16,24},{1,9},{9,17},{17,25},{2,10},{10,18},{18,26},{... | collective-permute-start | bytes 393224 | tf_op jit(solution)/shard_map/ppermute | solution.py:50
  24.5 1.2 copy-start.1
  25.7 1.2 copy-start.4
  40.6 6.6 %collective-permute-start.6 = (f32[4,3,64,128]{3,2,1,0:T(8,128)S(1)}, f32[4,3,64,128]{3,2,1,0:T(8,128)S(1)}, u32[]{:S(2)}, u32[]{:S(2)}) collective-permute-start(f32[4,3,64,128]{3,2,1,0:T(8,128)S(1)} %get-tuple-element.32), channel_id=1, source_target_pairs={{0,8},{8,16},{16,24},{1,9},{9,17},{17,25},{2,10},{10,18},{18,26},{... | collective-permute-start | bytes 1179656 | tf_op jit(solution)/shard_map/ppermute | solution.py:50
  42.5 9.1 %collective-permute-start.7 = (f32[4,3,64,128]{3,2,1,0:T(8,128)S(1)}, f32[4,3,64,128]{3,2,1,0:T(8,128)S(1)}, u32[]{:S(2)}, u32[]{:S(2)}) collective-permute-start(f32[4,3,64,128]{3,2,1,0:T(8,128)S(1)} %get-tuple-element.33), channel_id=1, source_target_pairs={{8,0},{16,8},{24,16},{9,1},{17,9},{25,17},{10,2},{18,10},{26,18},{... | collective-permute-start | bytes 1179656 | tf_op jit(solution)/shard_map/ppermute | solution.py:50
  51.8 38.9 %copy-start.2 = (bf16[8,256,256]{2,1,0:T(8,128)(2,1)S(1)}, bf16[8,256,256]{2,1,0:T(8,128)(2,1)}, u32[]{:S(2)}) copy-start(bf16[8,256,256]{2,1,0:T(8,128)(2,1)} %constant.18.clone.tables_ref) | copy-start | bytes 3145732
  51.8 15.7 %collective-permute-start.9 = (f32[4,256,128]{2,1,0:T(8,128)S(1)}, f32[4,256,128]{2,1,0:T(8,128)S(1)}, u32[]{:S(2)}, u32[]{:S(2)}) collective-permute-start(f32[4,256,128]{2,1,0:T(8,128)S(1)} %get-tuple-element.34.left_ref), channel_id=1, source_target_pairs={{1,0},{2,1},{3,2},{4,3},{5,4},{6,5},{7,6},{9,8},{10,9},{11,10},{12... | collective-permute-start | bytes 1572872 | tf_op jit(solution)/shard_map/ppermute | solution.py:50
  53.2 26.3 %collective-permute-start.8 = (f32[4,256,128]{2,1,0:T(8,128)S(1)}, f32[4,256,128]{2,1,0:T(8,128)S(1)}, u32[]{:S(2)}, u32[]{:S(2)}) collective-permute-start(f32[4,256,128]{2,1,0:T(8,128)S(1)} %get-tuple-element.36.right_ref), channel_id=1, source_target_pairs={{0,1},{1,2},{2,3},{3,4},{4,5},{5,6},{6,7},{8,9},{9,10},{10,11},{11... | collective-permute-start | bytes 1572872 | tf_op jit(solution)/shard_map/ppermute | solution.py:50
  79.7 6.6 %collective-permute-start.10 = (f32[4,3,64,128]{3,2,1,0:T(8,128)S(1)}, f32[4,3,64,128]{3,2,1,0:T(8,128)S(1)}, u32[]{:S(2)}, u32[]{:S(2)}) collective-permute-start(f32[4,3,64,128]{3,2,1,0:T(8,128)S(1)} %get-tuple-element.38), channel_id=1, source_target_pairs={{0,8},{8,16},{16,24},{1,9},{9,17},{17,25},{2,10},{10,18},{18,26},{... | collective-permute-start | bytes 1179656 | tf_op jit(solution)/shard_map/ppermute | solution.py:50
  81.6 9.1 %collective-permute-start.11 = (f32[4,3,64,128]{3,2,1,0:T(8,128)S(1)}, f32[4,3,64,128]{3,2,1,0:T(8,128)S(1)}, u32[]{:S(2)}, u32[]{:S(2)}) collective-permute-start(f32[4,3,64,128]{3,2,1,0:T(8,128)S(1)} %get-tuple-element.39), channel_id=1, source_target_pairs={{8,0},{16,8},{24,16},{9,1},{17,9},{25,17},{10,2},{18,10},{26,18},{... | collective-permute-start | bytes 1179656 | tf_op jit(solution)/shard_map/ppermute | solution.py:50
  104.0 6.6 %collective-permute-start.12 = (f32[4,3,64,128]{3,2,1,0:T(8,128)S(1)}, f32[4,3,64,128]{3,2,1,0:T(8,128)S(1)}, u32[]{:S(2)}, u32[]{:S(2)}) collective-permute-start(f32[4,3,64,128]{3,2,1,0:T(8,128)S(1)} %get-tuple-element.42), channel_id=1, source_target_pairs={{0,8},{8,16},{16,24},{1,9},{9,17},{17,25},{2,10},{10,18},{18,26},{... | collective-permute-start | bytes 1179656 | tf_op jit(solution)/shard_map/ppermute | solution.py:50
  106.0 9.1 %collective-permute-start.13 = (f32[4,3,64,128]{3,2,1,0:T(8,128)S(1)}, f32[4,3,64,128]{3,2,1,0:T(8,128)S(1)}, u32[]{:S(2)}, u32[]{:S(2)}) collective-permute-start(f32[4,3,64,128]{3,2,1,0:T(8,128)S(1)} %get-tuple-element.43), channel_id=1, source_target_pairs={{8,0},{16,8},{24,16},{9,1},{17,9},{25,17},{10,2},{18,10},{26,18},{... | collective-permute-start | bytes 1179656 | tf_op jit(solution)/shard_map/ppermute | solution.py:50
  115.3 16.9 %collective-permute-start.14 = (f32[4,128,128]{2,1,0:T(8,128)S(1)}, f32[4,128,128]{2,1,0:T(8,128)S(1)}, u32[]{:S(2)}, u32[]{:S(2)}) collective-permute-start(f32[4,128,128]{2,1,0:T(8,128)S(1)} %get-tuple-element.45), channel_id=1, source_target_pairs={{0,1},{1,2},{2,3},{3,4},{4,5},{5,6},{6,7},{8,9},{9,10},{10,11},{11... | collective-permute-start | bytes 786440 | tf_op jit(solution)/shard_map/ppermute | solution.py:50
  123.3 8.9 %collective-permute-start.15 = (f32[4,128,128]{2,1,0:T(8,128)S(1)}, f32[4,128,128]{2,1,0:T(8,128)S(1)}, u32[]{:S(2)}, u32[]{:S(2)}) collective-permute-start(f32[4,128,128]{2,1,0:T(8,128)S(1)} %get-tuple-element.46), channel_id=1, source_target_pairs={{1,0},{2,1},{3,2},{4,3},{5,4},{6,5},{7,6},{9,8},{10,9},{11,10},{12... | collective-permute-start | bytes 786440 | tf_op jit(solution)/shard_map/ppermute | solution.py:50

commit v3 on v1

v3 whole, which is shorter than its diff:
```python
import math

import jax
import jax.numpy as jnp
import ml_dtypes
import numpy as np
from jax import lax
from jax.experimental import pallas as pl
from jax.experimental.pallas import tpu as pltpu
from jax.sharding import PartitionSpec as P

ITERS = 2
LANES = 128
GROUP = 4

modulus_offset = 0.5
fresnel_scale = 0.9


def split_table(table):
    high = table.astype(np.float32).astype(ml_dtypes.bfloat16)
    low = (table - high.astype(np.float64)).astype(np.float32).astype(ml_dtypes.bfloat16)
    return high, low


def transform_tables(frame_size):
    positions = np.arange(frame_size)
    dft = np.exp(-2j * math.pi * (positions[:, None] * positions[None, :] % frame_size) / frame_size)
    dft = dft / math.sqrt(frame_size)
    frequency = np.where(positions < frame_size // 2, positions, positions - frame_size)
    phase = np.exp(1j * math.pi * fresnel_scale * frequency.astype(np.float64) ** 2 / frame_size)
    hop = (np.conj(dft) * phase[None, :]) @ dft
    tables = []
    for matrix in (dft, hop):
        re, im = matrix.real, matrix.imag
        right = np.block([[re, im], [-im, re]])
        left = np.block([[re, -im], [im, re]])
        for table in (right, left):
            tables.extend(split_table(table))
    return np.stack(tables)


DFT_RIGHT, DFT_LEFT, HOP_RIGHT, HOP_LEFT = 0, 2, 4, 6


def neighbour(values, axis, step):
    count = lax.axis_size(axis)
    pairs = [(i, i + step) for i in range(count) if 0 <= i + step < count]
    return lax.ppermute(values, axis, pairs)


def lane_ids(shape):
    return lax.broadcasted_iota(jnp.int32, shape, len(shape) - 1)


def swap_halves(values):
    return pltpu.roll(values, LANES // 2, values.ndim - 1)


def vmem():
    return pl.BlockSpec(memory_space=pltpu.VMEM)


def smem():
    return pl.BlockSpec(memory_space=pltpu.SMEM)


def split(values):
    high = values.astype(jnp.bfloat16)
    return high, (values - high.astype(jnp.float32)).astype(jnp.bfloat16)


def dot(a, b):
    return jnp.dot(a, b, preferred_element_type=jnp.float32)


def blend(first, second):
    return jnp.where(lane_ids(first.shape) < LANES // 2, first, second)


def segments(rows, rim):
    half = rows // 2
    return ((slice(0, rim), slice(rows - rim, rows)), (slice(rim, half), slice(half, rows - rim)))


def pack_kernel(object_ref, turned_ref, left_edge, right_edge, left_mid, right_mid):
    planes, rows, cols = object_ref.shape
    tiles = cols // LANES
    pieces = segments(rows, left_edge.shape[1])
    for plane in range(planes):
        for (upper, lower), left_ref, right_ref in zip(
            pieces, (left_edge, left_mid), (right_edge, right_mid)
        ):
            left_ref[plane] = blend(
                object_ref[plane, lower, 0:LANES], swap_halves(object_ref[plane, upper, 0:LANES])
            )
            right_ref[plane] = blend(
                swap_halves(object_ref[plane, upper, cols - LANES : cols]),
                object_ref[plane, lower, cols - LANES : cols],
            )
    for plane in range(planes):
        for tile in range(tiles):
            turned_ref[plane, tile] = swap_halves(
                object_ref[plane, :, tile * LANES : (tile + 1) * LANES]
            )


def lay(turned_ref, plane, rows, left, right, put):
    tiles = turned_ref.shape[1]
    parts = [left] + [turned_ref[plane, tile, rows, :] for tile in range(tiles)] + [right]
    for block in range(tiles + 1):
        put(block, blend(parts[block], parts[block + 1]))


def rows_kernel(turned_ref, from_left, from_right, tables_hbm, up_ref, down_ref, tables_ref, sem):
    copy = pltpu.make_async_copy(tables_hbm, tables_ref, sem)
    copy.start()
    planes, _, rows, _ = turned_ref.shape
    rim = up_ref.shape[2]
    (upper, lower), _ = segments(rows, rim)
    for plane in range(planes):

        def put_up(block, values):
            up_ref[plane, block] = values

        def put_down(block, values):
            down_ref[plane, block] = values

        left, right = from_left[plane], from_right[plane]
        lay(turned_ref, plane, upper, left, right, put_up)
        lay(turned_ref, plane, lower, swap_halves(left), swap_halves(right), put_down)
    copy.wait()


def gradients(pos_ref, amps_ref, probe_ref, tables_ref, field_ref, grad_ref, work):
    frame = probe_ref.shape[-1]
    o0, o1, inc, wave = work
    count = pos_ref[2, 0]
    lanes = lane_ids((frame, LANES))

    grad_ref[...] = jnp.zeros_like(grad_ref)

    def right(source, index):
        table_high, table_low = tables_ref[index], tables_ref[index + 1]
        high, low = split(source)
        return dot(high, table_high) + (dot(low, table_high) + dot(high, table_low))

    def left(source, index):
        table_high, table_low = tables_ref[index], tables_ref[index + 1]
        high, low = split(source)
        return dot(table_high, high) + (dot(table_high, low) + dot(table_low, high))

    def two_sided(zs, right_index, left_index):
        result = []
        for pair in range(0, len(zs), 2):
            rows = jnp.concatenate([jnp.concatenate(z, axis=1) for z in zs[pair : pair + 2]], axis=0)
            out = right(rows, right_index)
            mixed = left(
                jnp.concatenate(
                    [
                        jnp.concatenate([out[:frame, :frame], out[frame:, :frame]], axis=1),
                        jnp.concatenate([out[:frame, frame:], out[frame:, frame:]], axis=1),
                    ],
                    axis=0,
                ),
                left_index,
            )
            for k in range(2):
                cols = slice(k * frame, (k + 1) * frame)
                result.append((mixed[:frame, cols], mixed[frame:, cols]))
        return result

    def group_step(group, carry):
        base = group * GROUP
        where = []
        for k in range(GROUP):
            row_at, col_at = pos_ref[0, base + k], pos_ref[1, base + k]
            block = lax.shift_right_logical(col_at, 7)
            shift = jnp.bitwise_and(col_at, LANES - 1)
            where.append((pl.ds(row_at, frame), block, shift))
            for plane in range(4):
                near = field_ref[plane, block, pl.ds(row_at, frame), :]
                far = field_ref[plane, block + 1, pl.ds(row_at, frame), :]
                joined = jnp.where(lanes >= shift, near, far)
                target = o0 if plane < 2 else o1
                target[k, plane % 2] = pltpu.roll(
                    joined, jnp.bitwise_and(LANES - shift, LANES - 1), 1
                )
        probe_re, probe_im = probe_ref[0], probe_ref[1]
        zs = []
        for k in range(GROUP):
            a, b = o0[k, 0], o0[k, 1]
            zs.append((probe_re * a - probe_im * b, probe_re * b + probe_im * a))
        for k, (re, im) in enumerate(two_sided(zs, HOP_RIGHT, HOP_LEFT)):
            inc[k, 0] = re
            inc[k, 1] = im
        zs = []
        for k in range(GROUP):
            a, b, c, d = inc[k, 0], inc[k, 1], o1[k, 0], o1[k, 1]
            zs.append((a * c - b * d, a * d + b * c))
        for k, (re, im) in enumerate(two_sided(zs, DFT_RIGHT, DFT_LEFT)):
            live = jnp.where(base + k < count, 1.0, 0.0)
            factor = (1.0 - amps_ref[base + k] * lax.rsqrt(re * re + im * im + modulus_offset)) * live
            wave[k, 0] = re * factor
            wave[k, 1] = im * factor
        zs = [(wave[k, 0], wave[k, 1]) for k in range(GROUP)]

        def place(k, first_plane, values):
            rows, block, shift = where[k]
            for part in range(2):
                moved = pltpu.roll(values[part], shift, 1)
                near = jnp.where(lanes >= shift, moved, 0.0)
                far = jnp.where(lanes >= shift, 0.0, moved)
                grad_ref[first_plane + part, block, rows, :] += near
                grad_ref[first_plane + part, block + 1, rows, :] += far

        for k, (re, im) in enumerate(two_sided(zs, DFT_LEFT, DFT_RIGHT)):
            wave[k, 0] = re
            wave[k, 1] = im
        zs = []
        for k in range(GROUP):
            re, im = wave[k, 0], wave[k, 1]
            a, b, c, d = inc[k, 0], inc[k, 1], o1[k, 0], o1[k, 1]
            place(k, 2, (a * re + b * im, a * im - b * re))
            zs.append((c * re + d * im, c * im - d * re))
        for k, (re, im) in enumerate(two_sided(zs, HOP_LEFT, HOP_RIGHT)):
            place(k, 0, (probe_re * re + probe_im * im, probe_re * im - probe_im * re))
        return carry

    lax.fori_loop(0, (count + GROUP - 1) // GROUP, group_step, 0)


def write_grad(grad_ref, pieces, packed):
    top, bottom, edges, left, mid, right = pieces
    _, blocks, all_rows, _ = grad_ref.shape
    rim = top.shape[2]
    rows = all_rows - 2 * rim
    top[...] = grad_ref[:, :, 0:rim, :]
    bottom[...] = grad_ref[:, :, rim + rows : all_rows, :]
    edges[:, :, 0:rim, :] = grad_ref[:, :, rim : 2 * rim, :]
    edges[:, :, rim : 2 * rim, :] = grad_ref[:, :, rows : rim + rows, :]
    left[...] = grad_ref[:, 0, 2 * rim : rows, :]
    mid[...] = grad_ref[:, 1 : blocks - 1, 2 * rim : rows, :]
    right[...] = grad_ref[:, blocks - 1, 2 * rim : rows, :]
    if packed:
        half = (rows - 2 * rim) // 2
        upper, lower = slice(2 * rim, 2 * rim + half), slice(2 * rim + half, rows)
        pack_bands(grad_ref, packed, upper, lower)


def pack_bands(ref, packed, upper, lower):
    blocks = ref.shape[1]
    for plane in range(ref.shape[0]):
        packed[0][plane] = blend(ref[plane, 0, upper, :], swap_halves(ref[plane, 0, lower, :]))
        packed[1][plane] = blend(
            swap_halves(ref[plane, blocks - 1, lower, :]), ref[plane, blocks - 1, upper, :]
        )


def first_kernel(
    pos_ref, turned_ref, up_ref, down_ref, from_left, from_right, from_up, from_down,
    amps_ref, probe_ref, tables_ref, field_ref, *rest,
):
    pieces, (grad_ref, *work) = rest[:-5], rest[-5:]
    planes, _, rows, _ = turned_ref.shape
    rim = up_ref.shape[2]
    _, (upper, lower) = segments(rows, rim)
    field_ref[:, :, 0:rim, :] = from_up[...]
    field_ref[:, :, rim : 2 * rim, :] = up_ref[...]
    field_ref[:, :, rows : rows + rim, :] = down_ref[...]
    field_ref[:, :, rows + rim : rows + 2 * rim, :] = from_down[...]
    for plane in range(planes):

        def put_upper(block, values):
            field_ref[plane, block, rim + upper.start : rim + upper.stop, :] = values

        def put_lower(block, values):
            field_ref[plane, block, rim + lower.start : rim + lower.stop, :] = values

        left, right = from_left[plane], from_right[plane]
        lay(turned_ref, plane, upper, left, right, put_upper)
        lay(turned_ref, plane, lower, swap_halves(left), swap_halves(right), put_lower)
    gradients(pos_ref, amps_ref, probe_ref, tables_ref, field_ref, grad_ref, work)
    write_grad(grad_ref, pieces[:6], pieces[6:])


def folded(edges, from_up, from_down, plane, block):
    rim = from_up.shape[2]
    return (
        edges[plane, block, 0:rim, :] + from_up[plane, block],
        edges[plane, block, rim : 2 * rim, :] + from_down[plane, block],
    )


def fold_kernel(edges, from_up, from_down, left_ref, mid_ref, right_ref):
    planes, blocks = edges.shape[:2]
    rim = from_up.shape[2]
    for plane in range(planes):
        for block in range(blocks):
            upper, lower = folded(edges, from_up, from_down, plane, block)
            target = mid_ref.at[plane, block - 1]
            if block == 0:
                target = left_ref.at[plane]
            elif block == blocks - 1:
                target = right_ref.at[plane]
            target[0:rim, :] = upper
            target[rim : 2 * rim, :] = lower


def total_kernel(left_ref, mid_ref, right_ref, from_left, from_right, up_ref, down_ref):
    planes, blocks, rim, _ = up_ref.shape
    for plane in range(planes):
        for block in range(blocks):
            if block == 0:
                values = left_ref[plane] + from_left[plane]
            elif block == blocks - 1:
                values = right_ref[plane] + from_right[plane]
            else:
                values = mid_ref[plane, block - 1]
            up_ref[plane, block] = values[0:rim]
            down_ref[plane, block] = values[rim : 2 * rim]


def next_kernel(
    pos_ref, old_ref, up_ref, down_ref, left_ref, mid_ref, right_ref,
    from_left, from_right, from_up, from_down, amps_ref, probe_ref, tables_ref, field_ref, *rest,
):
    pieces, (grad_ref, *work) = rest[:-5], rest[-5:]
    _, blocks, all_rows, _ = old_ref.shape
    rim = up_ref.shape[2]
    rows = all_rows - 2 * rim
    for block in range(blocks):
        lane = lane_ids((1, 1, LANES))
        inside = lane >= 0
        middle = mid_ref[:, block - 1] if 0 < block < blocks - 1 else None
        if block == 0:
            inside = lane >= pos_ref[2, 1] * (LANES // 2)
            middle = left_ref[...] + from_left[...]
        if block == blocks - 1:
            inside = lane < LANES - pos_ref[2, 2] * (LANES // 2)
            middle = right_ref[...] + from_right[...]
        for lo, hi, values in (
            (0, rim, from_up[:, block]),
            (rim, 2 * rim, up_ref[:, block]),
            (2 * rim, rows, middle),
            (rows, rows + rim, down_ref[:, block]),
            (rows + rim, all_rows, from_down[:, block]),
        ):
            updated = old_ref[:, block, lo:hi, :] - values
            field_ref[:, block, lo:hi, :] = jnp.where(inside, updated, 0.0)
    gradients(pos_ref, amps_ref, probe_ref, tables_ref, field_ref, grad_ref, work)
    write_grad(grad_ref, pieces[:6], pieces[6:])


def last_fold_kernel(edges, from_up, from_down, folded_ref, left_ref, right_ref):
    planes, blocks = edges.shape[:2]
    rim = from_up.shape[2]
    for plane in range(planes):
        for block in range(blocks):
            upper, lower = folded(edges, from_up, from_down, plane, block)
            folded_ref[plane, block, 0:rim, :] = upper
            folded_ref[plane, block, rim : 2 * rim, :] = lower
    pack_bands(folded_ref, (left_ref, right_ref), slice(0, rim), slice(rim, 2 * rim))


def finish_kernel(
    field_ref, edges, left_ref, mid_ref, right_ref,
    mid_left, mid_right, edge_left, edge_right, out_ref,
):
    planes, blocks, _, _ = field_ref.shape
    rows = out_ref.shape[1]
    rim = edge_left.shape[1]
    (first, last), (upper, lower) = segments(rows, rim)
    half = upper.stop - upper.start

    def whole(plane, part, edge):
        size = rim if edge else half
        at = slice(part * size, (part + 1) * size)
        values = [
            edges[plane, block, at, :] if edge
            else left_ref[plane, at, :] if block == 0
            else right_ref[plane, at, :] if block == blocks - 1
            else mid_ref[plane, block - 1, at, :]
            for block in range(blocks)
        ]
        extras = [edge_left[plane], edge_right[plane]] if edge else [mid_left[plane], mid_right[plane]]
        if part == 1:
            extras = [swap_halves(extra) for extra in extras]
        values[0] += extras[0]
        values[-1] += extras[1]
        return values

    for plane in range(planes):
        for part, edge, at in ((0, True, first), (0, False, upper), (1, False, lower), (1, True, last)):
            values = whole(plane, part, edge)
            turned = [
                swap_halves(field_ref[plane, block, rim + at.start : rim + at.stop, :] - values[block])
                for block in range(blocks)
            ]
            for block in range(blocks - 1):
                out_ref[plane, at, block * LANES : (block + 1) * LANES] = blend(
                    turned[block], turned[block + 1]
                )


def f32(*shape):
    return pltpu.VMEM(shape, jnp.float32)


def on_chip(*arrays):
    return [pltpu.with_memory_space_constraint(array, pltpu.VMEM) for array in arrays]


def body(object_slices, probe, amplitudes, scan_pos, scan_count):
    layers, _, tile_r, tile_c = object_slices.shape
    planes = layers * 2
    frame = probe.shape[-1]
    rim = frame // 2
    blocks = tile_c // LANES + 1
    slots = amplitudes.shape[2]
    row_id, col_id = lax.axis_index("row"), lax.axis_index("col")
    amps = amplitudes[0, 0]
    flags = jnp.stack(
        [
            scan_count[0, 0],
            (col_id == 0).astype(jnp.int32),
            (col_id == lax.axis_size("col") - 1).astype(jnp.int32),
        ]
    )
    pos = jnp.stack(
        [
            scan_pos[0, 0, 0] - row_id * tile_r,
            scan_pos[1, 0, 0] - col_id * tile_c,
            jnp.pad(flags, (0, slots - 3)),
        ]
    )
    tables = jnp.asarray(transform_tables(frame))
    tile = object_slices.reshape(planes, tile_r, tile_c)

    band = tile_r - 2 * rim

    def call(kernel, outs, mib, scratch=(), scalars=(), raw=()):
        def run(*arrays):
            return pl.pallas_call(
                kernel,
                out_shape=outs,
                in_specs=[smem()] * len(scalars) + [vmem()] * len(arrays)
                + [pl.BlockSpec(memory_space=pltpu.HBM)] * len(raw),
                out_specs=[vmem()] * len(outs),
                scratch_shapes=list(scratch),
                compiler_params=pltpu.CompilerParams(vmem_limit_bytes=mib << 20),
            )(
                *scalars,
                *on_chip(*arrays),
                *[pltpu.with_memory_space_constraint(array, pltpu.HBM) for array in raw],
            )

        return run

    strip = f32(planes, blocks, rim, LANES)
    packed_edge = f32(planes, rim, LANES)
    packed_mid = f32(planes, band // 2, LANES)
    turned, left_edge, right_edge, left_mid, right_mid = call(
        pack_kernel,
        [f32(planes, blocks - 1, tile_r, LANES)] + [packed_edge] * 2 + [packed_mid] * 2,
        4,
    )(tile)
    from_left = neighbour(right_edge, "col", 1)
    from_right = neighbour(left_edge, "col", -1)
    mid_left = neighbour(right_mid, "col", 1)
    mid_right = neighbour(left_mid, "col", -1)
    up, down, tables = call(
        rows_kernel,
        [strip, strip, pltpu.VMEM(tables.shape, tables.dtype)],
        4,
        scratch=[pltpu.SemaphoreType.DMA(())],
        raw=[tables],
    )(turned, from_left, from_right)
    from_up = neighbour(down, "row", 1)
    from_down = neighbour(up, "row", -1)

    field_shape = f32(planes, blocks, tile_r + frame, LANES)
    work = [field_shape] + [pltpu.VMEM((GROUP, 2, frame, frame), jnp.float32)] * 4
    pieces = [
        strip,
        strip,
        f32(planes, blocks, 2 * rim, LANES),
        f32(planes, band, LANES),
        f32(planes, blocks - 2, band, LANES),
        f32(planes, band, LANES),
    ]
    field, top, bottom, edges, left, mid, right = call(
        first_kernel, [field_shape] + pieces, 20, scratch=work, scalars=[pos]
    )(turned, up, down, mid_left, mid_right, from_up, from_down, amps, probe, tables)

    for iteration in range(1, ITERS):
        mid_left = neighbour(right, "col", 1)
        mid_right = neighbour(left, "col", -1)
        from_up = neighbour(bottom, "row", 1)
        from_down = neighbour(top, "row", -1)
        edge_parts = call(
            fold_kernel,
            [
                f32(planes, 2 * rim, LANES),
                f32(planes, blocks - 2, 2 * rim, LANES),
                f32(planes, 2 * rim, LANES),
            ],
            4,
        )(edges, from_up, from_down)
        from_left = neighbour(edge_parts[2], "col", 1)
        from_right = neighbour(edge_parts[0], "col", -1)
        up, down = call(total_kernel, [strip, strip], 4)(*edge_parts, from_left, from_right)
        from_up = neighbour(down, "row", 1)
        from_down = neighbour(up, "row", -1)
        last = iteration == ITERS - 1
        field, top, bottom, edges, left, mid, right, *packed = call(
            next_kernel,
            [field_shape] + pieces + [packed_mid] * (2 * last),
            20,
            scratch=work,
            scalars=[pos],
        )(
            field, up, down, left, mid, right, mid_left, mid_right, from_up, from_down,
            amps, probe, tables,
        )

    mid_left = neighbour(packed[1], "col", 1)
    mid_right = neighbour(packed[0], "col", -1)
    from_up = neighbour(bottom, "row", 1)
    from_down = neighbour(top, "row", -1)
    edges, edge_left, edge_right = call(
        last_fold_kernel, [f32(planes, blocks, 2 * rim, LANES)] + [packed_edge] * 2, 4
    )(edges, from_up, from_down)
    edge_left, edge_right = neighbour(edge_right, "col", 1), neighbour(edge_left, "col", -1)
    (out,) = call(finish_kernel, [jax.ShapeDtypeStruct((planes, tile_r, tile_c), jnp.float32)], 8)(
        field, edges, left, mid, right, mid_left, mid_right, edge_left, edge_right
    )
    return out.reshape(object_slices.shape)


def solution(mesh):
    in_specs = (
        P(None, None, "row", "col"),
        P(),
        P("row", "col", None, None, None),
        P(None, "row", "col", None),
        P("row", "col"),
    )
    out_specs = P(None, None, "row", "col")

    return jax.shard_map(body, mesh=mesh, in_specs=in_specs, out_specs=out_specs, check_vma=False)
```

time: 158 us -> 125 us (0.79)
  the two profiles are of different devices: /device:TPU:1 before, /device:TPU:13 now
where the time goes in v3:
time: 125 us; the launch traced here: 124 us
  starting transfers between devices  73.8 us (59%)
  waiting for transfers between devices  28.8 us (23%)
  Pallas kernels  19 us (15%)
  local copies, waits for them, and re-layouts  1.33 us (1%)
    ppermute x20, starting transfers between devices, neighbour(): return lax.ppermute(values, axis, pairs)  73.8 us
    ppermute x20, waiting for transfers between devices, neighbour(): return lax.ppermute(values, axis, pairs)  28.8 us
    pallas_call x8, Pallas kernels, run(): pl.pallas_call(kernel, out_shape=outs, in_specs=[smem()] * len(scalars) +...  19 us
  transfers between devices with their start and end apart: 20, of which 10 were waited for; matrix products, arithmetic and copies ran while one was open for 0% of the time, Pallas kernels for 1%

profile of v3, /device:TPU:13, one launch (start us, length us, event | category | flops | bytes accessed | tf_op | source)
XLA Modules:
  0.0 123.9 jit_solution(13458449368024096289)
XLA Ops:
  1.8 3.1 %collective-permute-start = (f32[4,64,128]{2,1,0:T(8,128)S(1)}, f32[4,64,128]{2,1,0:T(8,128)S(1)}, u32[]{:S(2)}, u32[]{:S(2)}) collective-permute-start(f32[4,64,128]{2,1,0:T(8,128)S(1)} %get-tuple-element.38), channel_id=1, source_target_pairs={{0,1},{1,2},{2,3},{3,4},{4,5},{5,6},{6,7},{8,9},{9,10},{10,11},{11... | collective-permute-start | bytes 393224 | tf_op jit(solution)/shard_map/ppermute | solution.py:49
  4.9 2.1 %collective-permute-start.1 = (f32[4,64,128]{2,1,0:T(8,128)S(1)}, f32[4,64,128]{2,1,0:T(8,128)S(1)}, u32[]{:S(2)}, u32[]{:S(2)}) collective-permute-start(f32[4,64,128]{2,1,0:T(8,128)S(1)} %get-tuple-element.39), channel_id=1, source_target_pairs={{1,0},{2,1},{3,2},{4,3},{5,4},{6,5},{7,6},{9,8},{10,9},{11,10},{12... | collective-permute-start | bytes 393224 | tf_op jit(solution)/shard_map/ppermute | solution.py:49
  7.1 4.0 %collective-permute-start.2 = (f32[4,64,128]{2,1,0:T(8,128)S(1)}, f32[4,64,128]{2,1,0:T(8,128)S(1)}, u32[]{:S(2)}, u32[]{:S(2)}) collective-permute-start(f32[4,64,128]{2,1,0:T(8,128)S(1)} %get-tuple-element.42), channel_id=1, source_target_pairs={{0,1},{1,2},{2,3},{3,4},{4,5},{5,6},{6,7},{8,9},{9,10},{10,11},{11... | collective-permute-start | bytes 393224 | tf_op jit(solution)/shard_map/ppermute | solution.py:49
  15.1 3.4 %collective-permute-start.5 = (f32[4,3,64,128]{3,2,1,0:T(8,128)S(1)}, f32[4,3,64,128]{3,2,1,0:T(8,128)S(1)}, u32[]{:S(2)}, u32[]{:S(2)}) collective-permute-start(f32[4,3,64,128]{3,2,1,0:T(8,128)S(1)} %get-tuple-element.40.up_ref), channel_id=1, source_target_pairs={{8,0},{16,8},{24,16},{9,1},{17,9},{25,17},{10,2},{18,10},{26,18},{... | collective-permute-start | bytes 1179656 | tf_op jit(solution)/shard_map/ppermute | solution.py:49
  18.5 3.0 %collective-permute-start.4 = (f32[4,3,64,128]{3,2,1,0:T(8,128)S(1)}, f32[4,3,64,128]{3,2,1,0:T(8,128)S(1)}, u32[]{:S(2)}, u32[]{:S(2)}) collective-permute-start(f32[4,3,64,128]{3,2,1,0:T(8,128)S(1)} %get-tuple-element.41.down_ref), channel_id=1, source_target_pairs={{0,8},{8,16},{16,24},{1,9},{9,17},{17,25},{2,10},{10,18},{18,26},{... | collective-permute-start | bytes 1179656 | tf_op jit(solution)/shard_map/ppermute | solution.py:49
  21.6 3.4 %collective-permute-done.5.from_down = f32[4,3,64,128]{3,2,1,0:T(8,128)S(1)} collective-permute-done((f32[4,3,64,128]{3,2,1,0:T(8,128)S(1)}, f32[4,3,64,128]{3,2,1,0:T(8,128)S(1)}, u32[]{:S(2)}, u32[]{:S(2)}) %collective-permute-start.5) | collective-permute-done | bytes 393248 | tf_op jit(solution)/shard_map/ppermute | solution.py:49
  26.3 7.4 %shard_map.66 = (f32[4,3,384,128]{3,2,1,0:T(8,128)S(1)}, f32[4,3,64,128]{3,2,1,0:T(8,128)S(1)}, f32[4,3,64,128]{3,2,1,0:T(8,128)S(1)}, f32[4,3,128,128]{3,2,1,0:...) custom-call(s32[3,16]{1,0:T(4,128)S(1)} %pad_add_fusion.pos_ref, ...), custom_call_target="tpu_custom_call" | custom-call | tf_op jit(solution)/shard_map/pallas_call | solution.py:444
  33.7 1.9 %collective-permute-start.6 = (f32[4,3,64,128]{3,2,1,0:T(8,128)S(1)}, f32[4,3,64,128]{3,2,1,0:T(8,128)S(1)}, u32[]{:S(2)}, u32[]{:S(2)}) collective-permute-start(f32[4,3,64,128]{3,2,1,0:T(8,128)S(1)} %get-tuple-element.47), channel_id=1, source_target_pairs={{0,8},{8,16},{16,24},{1,9},{9,17},{17,25},{2,10},{10,18},{18,26},{... | collective-permute-start | bytes 1179656 | tf_op jit(solution)/shard_map/ppermute | solution.py:49
  35.6 3.7 %collective-permute-start.7 = (f32[4,3,64,128]{3,2,1,0:T(8,128)S(1)}, f32[4,3,64,128]{3,2,1,0:T(8,128)S(1)}, u32[]{:S(2)}, u32[]{:S(2)}) collective-permute-start(f32[4,3,64,128]{3,2,1,0:T(8,128)S(1)} %get-tuple-element.48), channel_id=1, source_target_pairs={{8,0},{16,8},{24,16},{9,1},{17,9},{25,17},{10,2},{18,10},{26,18},{... | collective-permute-start | bytes 1179656 | tf_op jit(solution)/shard_map/ppermute | solution.py:49
  40.3 4.4 %collective-permute-done.7.from_down = f32[4,3,64,128]{3,2,1,0:T(8,128)S(1)} collective-permute-done((f32[4,3,64,128]{3,2,1,0:T(8,128)S(1)}, f32[4,3,64,128]{3,2,1,0:T(8,128)S(1)}, u32[]{:S(2)}, u32[]{:S(2)}) %collective-permute-start.7) | collective-permute-done | bytes 393248 | tf_op jit(solution)/shard_map/ppermute | solution.py:49
  44.8 3.1 %collective-permute-start.9 = (f32[4,128,128]{2,1,0:T(8,128)S(1)}, f32[4,128,128]{2,1,0:T(8,128)S(1)}, u32[]{:S(2)}, u32[]{:S(2)}) collective-permute-start(f32[4,128,128]{2,1,0:T(8,128)S(1)} %get-tuple-element.49.left_ref), channel_id=1, source_target_pairs={{1,0},{2,1},{3,2},{4,3},{5,4},{6,5},{7,6},{9,8},{10,9},{11,10},{12... | collective-permute-start | bytes 786440 | tf_op jit(solution)/shard_map/ppermute | solution.py:49
  47.9 12.5 %collective-permute-start.8 = (f32[4,128,128]{2,1,0:T(8,128)S(1)}, f32[4,128,128]{2,1,0:T(8,128)S(1)}, u32[]{:S(2)}, u32[]{:S(2)}) collective-permute-start(f32[4,128,128]{2,1,0:T(8,128)S(1)} %get-tuple-element.51.right_ref), channel_id=1, source_target_pairs={{0,1},{1,2},{2,3},{3,4},{4,5},{5,6},{6,7},{8,9},{9,10},{10,11},{11... | collective-permute-start | bytes 786440 | tf_op jit(solution)/shard_map/ppermute | solution.py:49
  65.7 3.6 %collective-permute-start.12 = (f32[4,3,64,128]{3,2,1,0:T(8,128)S(1)}, f32[4,3,64,128]{3,2,1,0:T(8,128)S(1)}, u32[]{:S(2)}, u32[]{:S(2)}) collective-permute-start(f32[4,3,64,128]{3,2,1,0:T(8,128)S(1)} %get-tuple-element.53.down_ref), channel_id=1, source_target_pairs={{0,8},{8,16},{16,24},{1,9},{9,17},{17,25},{2,10},{10,18},{18,26},{... | collective-permute-start | bytes 1179656 | tf_op jit(solution)/shard_map/ppermute | solution.py:49
  71.3 5.0 %collective-permute-start.10 = (f32[4,128,128]{2,1,0:T(8,128)S(1)}, f32[4,128,128]{2,1,0:T(8,128)S(1)}, u32[]{:S(2)}, u32[]{:S(2)}) collective-permute-start(f32[4,128,128]{2,1,0:T(8,128)S(1)} %get-tuple-element.56.right_ref), channel_id=1, source_target_pairs={{0,1},{1,2},{2,3},{3,4},{4,5},{5,6},{6,7},{8,9},{9,10},{10,11},{11... | collective-permute-start | bytes 786440 | tf_op jit(solution)/shard_map/ppermute | solution.py:49
  76.3 5.7 %collective-permute-done.11.from_right = f32[4,128,128]{2,1,0:T(8,128)S(1)} collective-permute-done((f32[4,128,128]{2,1,0:T(8,128)S(1)}, f32[4,128,128]{2,1,0:T(8,128)S(1)}, u32[]{:S(2)}, u32[]{:S(2)}) %collective-permute-start.11) | collective-permute-done | bytes 262176 | tf_op jit(solution)/shard_map/ppermute | solution.py:49
  82.0 3.7 %collective-permute-done.10.from_left = f32[4,128,128]{2,1,0:T(8,128)S(1)} collective-permute-done((f32[4,128,128]{2,1,0:T(8,128)S(1)}, f32[4,128,128]{2,1,0:T(8,128)S(1)}, u32[]{:S(2)}, u32[]{:S(2)}) %collective-permute-start.10) | collective-permute-done | bytes 262176 | tf_op jit(solution)/shard_map/ppermute | solution.py:49
  85.8 7.6 %shard_map.69 = (f32[4,3,384,128]{3,2,1,0:T(8,128)S(1)}, f32[4,3,64,128]{3,2,1,0:T(8,128)S(1)}, f32[4,3,64,128]{3,2,1,0:T(8,128)S(1)}, f32[4,3,128,128]{3,2,1,0:...) custom-call(s32[3,16]{1,0:T(4,128)S(1)} %pad_add_fusion.pos_ref, ...), custom_call_target="tpu_custom_call" | custom-call | tf_op jit(solution)/shard_map/pallas_call | solution.py:444
  95.3 8.0 %collective-permute-start.15 = (f32[4,3,64,128]{3,2,1,0:T(8,128)S(1)}, f32[4,3,64,128]{3,2,1,0:T(8,128)S(1)}, u32[]{:S(2)}, u32[]{:S(2)}) collective-permute-start(f32[4,3,64,128]{3,2,1,0:T(8,128)S(1)} %get-tuple-element.60), channel_id=1, source_target_pairs={{8,0},{16,8},{24,16},{9,1},{17,9},{25,17},{10,2},{18,10},{26,18},{... | collective-permute-start | bytes 1179656 | tf_op jit(solution)/shard_map/ppermute | solution.py:49
  103.3 3.2 %collective-permute-start.16 = (f32[4,64,128]{2,1,0:T(8,128)S(1)}, f32[4,64,128]{2,1,0:T(8,128)S(1)}, u32[]{:S(2)}, u32[]{:S(2)}) collective-permute-start(f32[4,64,128]{2,1,0:T(8,128)S(1)} %get-tuple-element.65), channel_id=1, source_target_pairs={{0,1},{1,2},{2,3},{3,4},{4,5},{5,6},{6,7},{8,9},{9,10},{10,11},{11... | collective-permute-start | bytes 393224 | tf_op jit(solution)/shard_map/ppermute | solution.py:49
  106.5 2.1 %collective-permute-start.17 = (f32[4,64,128]{2,1,0:T(8,128)S(1)}, f32[4,64,128]{2,1,0:T(8,128)S(1)}, u32[]{:S(2)}, u32[]{:S(2)}) collective-permute-start(f32[4,64,128]{2,1,0:T(8,128)S(1)} %get-tuple-element.66), channel_id=1, source_target_pairs={{1,0},{2,1},{3,2},{4,3},{5,4},{6,5},{7,6},{9,8},{10,9},{11,10},{12... | collective-permute-start | bytes 393224 | tf_op jit(solution)/shard_map/ppermute | solution.py:49
  108.8 5.3 %collective-permute-start.18 = (f32[4,64,128]{2,1,0:T(8,128)S(1)}, f32[4,64,128]{2,1,0:T(8,128)S(1)}, u32[]{:S(2)}, u32[]{:S(2)}) collective-permute-start(f32[4,64,128]{2,1,0:T(8,128)S(1)} %get-tuple-element.67), channel_id=1, source_target_pairs={{0,1},{1,2},{2,3},{3,4},{4,5},{5,6},{6,7},{8,9},{9,10},{10,11},{11... | collective-permute-start | bytes 393224 | tf_op jit(solution)/shard_map/ppermute | solution.py:49
  116.1 2.0 %collective-permute-done.18.edge_left = f32[4,64,128]{2,1,0:T(8,128)S(1)} collective-permute-done((f32[4,64,128]{2,1,0:T(8,128)S(1)}, f32[4,64,128]{2,1,0:T(8,128)S(1)}, u32[]{:S(2)}, u32[]{:S(2)}) %collective-permute-start.18) | collective-permute-done | bytes 131104 | tf_op jit(solution)/shard_map/ppermute | solution.py:49
  118.1 3.9 %collective-permute-done.19.edge_right = f32[4,64,128]{2,1,0:T(8,128)S(1)} collective-permute-done((f32[4,64,128]{2,1,0:T(8,128)S(1)}, f32[4,64,128]{2,1,0:T(8,128)S(1)}, u32[]{:S(2)}, u32[]{:S(2)}) %collective-permute-start.19) | collective-permute-done | bytes 131104 | tf_op jit(solution)/shard_map/ppermute | solution.py:49
  122.0 1.9 %shard_map.71 = f32[4,256,256]{2,1,0:T(8,128)} custom-call(f32[4,3,384,128]{3,2,1,0:T(8,128)S(1)} %get-tuple-element.57.field_ref, f32[4,3,128,128]{3,2,1,0:T(8,128)S(1)} %get-tuple-element.61.edges, f32[4,128,128]{2,1,0:T(8,128)S(1)} %get-tuple-element.62.left_ref, f32[4,1,128,128]{3,2,1,0:T(8,128)S(1)} %get-tuple-element.63.mid_ref, ...), custom_call_target="tpu_custom_call" | custom-call | tf_op jit(solution)/shard_map/pallas_call | solution.py:444
  (36 shorter events, 18.7 us)
Async XLA Ops:
  0.0 26.3 %copy-start = (f32[1,1,16,128,128]{4,3,2,1,0:T(8,128)S(1)}, f32[1,1,16,128,128]{4,3,2,1,0:T(8,128)}, u32[]{:S(2)}) copy-start(f32[1,1,16,128,128]{4,3,2,1,0:T(8,128)} %param.8) | copy-start | bytes 3145732
  0.0 1.3 %copy-start.1 = (f32[2,2,256,256]{3,2,1,0:T(8,128)S(1)}, f32[2,2,256,256]{3,2,1,0:T(8,128)}, u32[]{:S(2)}) copy-start(f32[2,2,256,256]{3,2,1,0:T(8,128)} %param.6) | copy-start | bytes 3145732
  1.3 20.2 %copy-start.3 = (s32[2,1,1,16]{3,2,1,0:T(1,128)S(1)}, s32[2,1,1,16]{3,2,1,0:T(1,128)}, u32[]{:S(2)}) copy-start(s32[2,1,1,16]{3,2,1,0:T(1,128)} %param.9) | copy-start | bytes 388
  1.3 24.9 %copy-start.2 = (f32[2,128,128]{2,1,0:T(8,128)S(1)}, f32[2,128,128]{2,1,0:T(8,128)}, u32[]{:S(2)}) copy-start(f32[2,128,128]{2,1,0:T(8,128)} %probe_ref.3) | copy-start | bytes 393220
  1.8 12.0 %collective-permute-start = (f32[4,64,128]{2,1,0:T(8,128)S(1)}, f32[4,64,128]{2,1,0:T(8,128)S(1)}, u32[]{:S(2)}, u32[]{:S(2)}) collective-permute-start(f32[4,64,128]{2,1,0:T(8,128)S(1)} %get-tuple-element.38), channel_id=1, source_target_pairs={{0,1},{1,2},{2,3},{3,4},{4,5},{5,6},{6,7},{8,9},{9,10},{10,11},{11... | collective-permute-start | bytes 393224 | tf_op jit(solution)/shard_map/ppermute | solution.py:49
  4.9 8.9 %collective-permute-start.1 = (f32[4,64,128]{2,1,0:T(8,128)S(1)}, f32[4,64,128]{2,1,0:T(8,128)S(1)}, u32[]{:S(2)}, u32[]{:S(2)}) collective-permute-start(f32[4,64,128]{2,1,0:T(8,128)S(1)} %get-tuple-element.39), channel_id=1, source_target_pairs={{1,0},{2,1},{3,2},{4,3},{5,4},{6,5},{7,6},{9,8},{10,9},{11,10},{12... | collective-permute-start | bytes 393224 | tf_op jit(solution)/shard_map/ppermute | solution.py:49
  7.1 14.5 %collective-permute-start.2 = (f32[4,64,128]{2,1,0:T(8,128)S(1)}, f32[4,64,128]{2,1,0:T(8,128)S(1)}, u32[]{:S(2)}, u32[]{:S(2)}) collective-permute-start(f32[4,64,128]{2,1,0:T(8,128)S(1)} %get-tuple-element.42), channel_id=1, source_target_pairs={{0,1},{1,2},{2,3},{3,4},{4,5},{5,6},{6,7},{8,9},{9,10},{10,11},{11... | collective-permute-start | bytes 393224 | tf_op jit(solution)/shard_map/ppermute | solution.py:49
  11.1 10.5 %collective-permute-start.3 = (f32[4,64,128]{2,1,0:T(8,128)S(1)}, f32[4,64,128]{2,1,0:T(8,128)S(1)}, u32[]{:S(2)}, u32[]{:S(2)}) collective-permute-start(f32[4,64,128]{2,1,0:T(8,128)S(1)} %get-tuple-element.43), channel_id=1, source_target_pairs={{1,0},{2,1},{3,2},{4,3},{5,4},{6,5},{7,6},{9,8},{10,9},{11,10},{12... | collective-permute-start | bytes 393224 | tf_op jit(solution)/shard_map/ppermute | solution.py:49
  15.1 10.0 %collective-permute-start.5 = (f32[4,3,64,128]{3,2,1,0:T(8,128)S(1)}, f32[4,3,64,128]{3,2,1,0:T(8,128)S(1)}, u32[]{:S(2)}, u32[]{:S(2)}) collective-permute-start(f32[4,3,64,128]{3,2,1,0:T(8,128)S(1)} %get-tuple-element.40.up_ref), channel_id=1, source_target_pairs={{8,0},{16,8},{24,16},{9,1},{17,9},{25,17},{10,2},{18,10},{26,18},{... | collective-permute-start | bytes 1179656 | tf_op jit(solution)/shard_map/ppermute | solution.py:49
  18.5 7.7 %collective-permute-start.4 = (f32[4,3,64,128]{3,2,1,0:T(8,128)S(1)}, f32[4,3,64,128]{3,2,1,0:T(8,128)S(1)}, u32[]{:S(2)}, u32[]{:S(2)}) collective-permute-start(f32[4,3,64,128]{3,2,1,0:T(8,128)S(1)} %get-tuple-element.41.down_ref), channel_id=1, source_target_pairs={{0,8},{8,16},{16,24},{1,9},{9,17},{17,25},{2,10},{10,18},{18,26},{... | collective-permute-start | bytes 1179656 | tf_op jit(solution)/shard_map/ppermute | solution.py:49
  33.7 6.6 %collective-permute-start.6 = (f32[4,3,64,128]{3,2,1,0:T(8,128)S(1)}, f32[4,3,64,128]{3,2,1,0:T(8,128)S(1)}, u32[]{:S(2)}, u32[]{:S(2)}) collective-permute-start(f32[4,3,64,128]{3,2,1,0:T(8,128)S(1)} %get-tuple-element.47), channel_id=1, source_target_pairs={{0,8},{8,16},{16,24},{1,9},{9,17},{17,25},{2,10},{10,18},{18,26},{... | collective-permute-start | bytes 1179656 | tf_op jit(solution)/shard_map/ppermute | solution.py:49
  35.6 9.1 %collective-permute-start.7 = (f32[4,3,64,128]{3,2,1,0:T(8,128)S(1)}, f32[4,3,64,128]{3,2,1,0:T(8,128)S(1)}, u32[]{:S(2)}, u32[]{:S(2)}) collective-permute-start(f32[4,3,64,128]{3,2,1,0:T(8,128)S(1)} %get-tuple-element.48), channel_id=1, source_target_pairs={{8,0},{16,8},{24,16},{9,1},{17,9},{25,17},{10,2},{18,10},{26,18},{... | collective-permute-start | bytes 1179656 | tf_op jit(solution)/shard_map/ppermute | solution.py:49
  44.8 17.4 %collective-permute-start.9 = (f32[4,128,128]{2,1,0:T(8,128)S(1)}, f32[4,128,128]{2,1,0:T(8,128)S(1)}, u32[]{:S(2)}, u32[]{:S(2)}) collective-permute-start(f32[4,128,128]{2,1,0:T(8,128)S(1)} %get-tuple-element.49.left_ref), channel_id=1, source_target_pairs={{1,0},{2,1},{3,2},{4,3},{5,4},{6,5},{7,6},{9,8},{10,9},{11,10},{12... | collective-permute-start | bytes 786440 | tf_op jit(solution)/shard_map/ppermute | solution.py:49
  47.9 15.8 %collective-permute-start.8 = (f32[4,128,128]{2,1,0:T(8,128)S(1)}, f32[4,128,128]{2,1,0:T(8,128)S(1)}, u32[]{:S(2)}, u32[]{:S(2)}) collective-permute-start(f32[4,128,128]{2,1,0:T(8,128)S(1)} %get-tuple-element.51.right_ref), channel_id=1, source_target_pairs={{0,1},{1,2},{2,3},{3,4},{4,5},{5,6},{6,7},{8,9},{9,10},{10,11},{11... | collective-permute-start | bytes 786440 | tf_op jit(solution)/shard_map/ppermute | solution.py:49
  63.8 21.9 %collective-permute-start.13 = (f32[4,3,64,128]{3,2,1,0:T(8,128)S(1)}, f32[4,3,64,128]{3,2,1,0:T(8,128)S(1)}, u32[]{:S(2)}, u32[]{:S(2)}) collective-permute-start(f32[4,3,64,128]{3,2,1,0:T(8,128)S(1)} %get-tuple-element.52.up_ref), channel_id=1, source_target_pairs={{8,0},{16,8},{24,16},{9,1},{17,9},{25,17},{10,2},{18,10},{26,18},{... | collective-permute-start | bytes 1179656 | tf_op jit(solution)/shard_map/ppermute | solution.py:49
  65.7 20.0 %collective-permute-start.12 = (f32[4,3,64,128]{3,2,1,0:T(8,128)S(1)}, f32[4,3,64,128]{3,2,1,0:T(8,128)S(1)}, u32[]{:S(2)}, u32[]{:S(2)}) collective-permute-start(f32[4,3,64,128]{3,2,1,0:T(8,128)S(1)} %get-tuple-element.53.down_ref), channel_id=1, source_target_pairs={{0,8},{8,16},{16,24},{1,9},{9,17},{17,25},{2,10},{10,18},{18,26},{... | collective-permute-start | bytes 1179656 | tf_op jit(solution)/shard_map/ppermute | solution.py:49
  69.4 12.6 %collective-permute-start.11 = (f32[4,128,128]{2,1,0:T(8,128)S(1)}, f32[4,128,128]{2,1,0:T(8,128)S(1)}, u32[]{:S(2)}, u32[]{:S(2)}) collective-permute-start(f32[4,128,128]{2,1,0:T(8,128)S(1)} %get-tuple-element.54.left_ref), channel_id=1, source_target_pairs={{1,0},{2,1},{3,2},{4,3},{5,4},{6,5},{7,6},{9,8},{10,9},{11,10},{12... | collective-permute-start | bytes 786440 | tf_op jit(solution)/shard_map/ppermute | solution.py:49
  71.3 14.4 %collective-permute-start.10 = (f32[4,128,128]{2,1,0:T(8,128)S(1)}, f32[4,128,128]{2,1,0:T(8,128)S(1)}, u32[]{:S(2)}, u32[]{:S(2)}) collective-permute-start(f32[4,128,128]{2,1,0:T(8,128)S(1)} %get-tuple-element.56.right_ref), channel_id=1, source_target_pairs={{0,1},{1,2},{2,3},{3,4},{4,5},{5,6},{6,7},{8,9},{9,10},{10,11},{11... | collective-permute-start | bytes 786440 | tf_op jit(solution)/shard_map/ppermute | solution.py:49
  93.4 15.3 %collective-permute-start.14 = (f32[4,3,64,128]{3,2,1,0:T(8,128)S(1)}, f32[4,3,64,128]{3,2,1,0:T(8,128)S(1)}, u32[]{:S(2)}, u32[]{:S(2)}) collective-permute-start(f32[4,3,64,128]{3,2,1,0:T(8,128)S(1)} %get-tuple-element.59), channel_id=1, source_target_pairs={{0,8},{8,16},{16,24},{1,9},{9,17},{17,25},{2,10},{10,18},{18,26},{... | collective-permute-start | bytes 1179656 | tf_op jit(solution)/shard_map/ppermute | solution.py:49
  95.3 13.3 %collective-permute-start.15 = (f32[4,3,64,128]{3,2,1,0:T(8,128)S(1)}, f32[4,3,64,128]{3,2,1,0:T(8,128)S(1)}, u32[]{:S(2)}, u32[]{:S(2)}) collective-permute-start(f32[4,3,64,128]{3,2,1,0:T(8,128)S(1)} %get-tuple-element.60), channel_id=1, source_target_pairs={{8,0},{16,8},{24,16},{9,1},{17,9},{25,17},{10,2},{18,10},{26,18},{... | collective-permute-start | bytes 1179656 | tf_op jit(solution)/shard_map/ppermute | solution.py:49
  103.3 12.7 %collective-permute-start.16 = (f32[4,64,128]{2,1,0:T(8,128)S(1)}, f32[4,64,128]{2,1,0:T(8,128)S(1)}, u32[]{:S(2)}, u32[]{:S(2)}) collective-permute-start(f32[4,64,128]{2,1,0:T(8,128)S(1)} %get-tuple-element.65), channel_id=1, source_target_pairs={{0,1},{1,2},{2,3},{3,4},{4,5},{5,6},{6,7},{8,9},{9,10},{10,11},{11... | collective-permute-start | bytes 393224 | tf_op jit(solution)/shard_map/ppermute | solution.py:49
  106.5 9.5 %collective-permute-start.17 = (f32[4,64,128]{2,1,0:T(8,128)S(1)}, f32[4,64,128]{2,1,0:T(8,128)S(1)}, u32[]{:S(2)}, u32[]{:S(2)}) collective-permute-start(f32[4,64,128]{2,1,0:T(8,128)S(1)} %get-tuple-element.66), channel_id=1, source_target_pairs={{1,0},{2,1},{3,2},{4,3},{5,4},{6,5},{7,6},{9,8},{10,9},{11,10},{12... | collective-permute-start | bytes 393224 | tf_op jit(solution)/shard_map/ppermute | solution.py:49
  108.8 9.2 %collective-permute-start.18 = (f32[4,64,128]{2,1,0:T(8,128)S(1)}, f32[4,64,128]{2,1,0:T(8,128)S(1)}, u32[]{:S(2)}, u32[]{:S(2)}) collective-permute-start(f32[4,64,128]{2,1,0:T(8,128)S(1)} %get-tuple-element.67), channel_id=1, source_target_pairs={{0,1},{1,2},{2,3},{3,4},{4,5},{5,6},{6,7},{8,9},{9,10},{10,11},{11... | collective-permute-start | bytes 393224 | tf_op jit(solution)/shard_map/ppermute | solution.py:49
  114.1 7.9 %collective-permute-start.19 = (f32[4,64,128]{2,1,0:T(8,128)S(1)}, f32[4,64,128]{2,1,0:T(8,128)S(1)}, u32[]{:S(2)}, u32[]{:S(2)}) collective-permute-start(f32[4,64,128]{2,1,0:T(8,128)S(1)} %get-tuple-element.68), channel_id=1, source_target_pairs={{1,0},{2,1},{3,2},{4,3},{5,4},{6,5},{7,6},{9,8},{10,9},{11,10},{12... | collective-permute-start | bytes 393224 | tf_op jit(solution)/shard_map/ppermute | solution.py:49

commit v4 on v3

--- a/solution.py
+++ b/solution.py
@@ -43,10 +43,19 @@
 DFT_RIGHT, DFT_LEFT, HOP_RIGHT, HOP_LEFT = 0, 2, 4, 6
 
 
-def neighbour(values, axis, step):
+def exchange(odd_values, even_values, axis):
     count = lax.axis_size(axis)
-    pairs = [(i, i + step) for i in range(count) if 0 <= i + step < count]
-    return lax.ppermute(values, axis, pairs)
+    received = []
+    for values, first in ((odd_values, 1), (even_values, 0)):
+        lower = range(first, count - 1, 2)
+        pairs = [(i, i + 1) for i in lower] + [(i + 1, i) for i in lower]
+        received.append(lax.ppermute(values, axis, pairs))
+    return received
+
+
+def paired(axis, before, after):
+    even = lax.rem(lax.axis_index(axis), 2) == 0
+    return jnp.where(even, before, after), jnp.where(even, after, before)
 
 
 def lane_ids(shape):
@@ -83,21 +92,22 @@
     return ((slice(0, rim), slice(rows - rim, rows)), (slice(rim, half), slice(half, rows - rim)))
 
 
-def pack_kernel(object_ref, turned_ref, left_edge, right_edge, left_mid, right_mid):
+def pack_kernel(object_ref, turned_ref, odd_edge, even_edge, odd_mid, even_mid):
     planes, rows, cols = object_ref.shape
     tiles = cols // LANES
-    pieces = segments(rows, left_edge.shape[1])
-    for plane in range(planes):
-        for (upper, lower), left_ref, right_ref in zip(
-            pieces, (left_edge, left_mid), (right_edge, right_mid)
+    pieces = segments(rows, odd_edge.shape[1])
+    for plane in range(planes):
+        for (upper, lower), odd_ref, even_ref in zip(
+            pieces, (odd_edge, odd_mid), (even_edge, even_mid)
         ):
-            left_ref[plane] = blend(
+            left = blend(
                 object_ref[plane, lower, 0:LANES], swap_halves(object_ref[plane, upper, 0:LANES])
             )
-            right_ref[plane] = blend(
+            right = blend(
                 swap_halves(object_ref[plane, upper, cols - LANES : cols]),
                 object_ref[plane, lower, cols - LANES : cols],
             )
+            odd_ref[plane], even_ref[plane] = paired("col", left, right)
     for plane in range(planes):
         for tile in range(tiles):
             turned_ref[plane, tile] = swap_halves(
@@ -112,7 +122,9 @@
         put(block, blend(parts[block], parts[block + 1]))
 
 
-def rows_kernel(turned_ref, from_left, from_right, tables_hbm, up_ref, down_ref, tables_ref, sem):
+def rows_kernel(
+    turned_ref, from_odd, from_even, tables_hbm, up_ref, down_ref, odd_ref, even_ref, tables_ref, sem
+):
     copy = pltpu.make_async_copy(tables_hbm, tables_ref, sem)
     copy.start()
     planes, _, rows, _ = turned_ref.shape
@@ -126,9 +138,10 @@
         def put_down(block, values):
             down_ref[plane, block] = values
 
-        left, right = from_left[plane], from_right[plane]
+        left, right = paired("col", from_odd[plane], from_even[plane])
         lay(turned_ref, plane, upper, left, right, put_up)
         lay(turned_ref, plane, lower, swap_halves(left), swap_halves(right), put_down)
+    odd_ref[...], even_ref[...] = paired("row", up_ref[...], down_ref[...])
     copy.wait()
 
 
@@ -230,45 +243,50 @@
     lax.fori_loop(0, (count + GROUP - 1) // GROUP, group_step, 0)
 
 
-def write_grad(grad_ref, pieces, packed):
-    top, bottom, edges, left, mid, right = pieces
+def write_grad(grad_ref, pieces):
+    row_odd, row_even, edges, left, mid, right, band_odd, band_even = pieces
     _, blocks, all_rows, _ = grad_ref.shape
-    rim = top.shape[2]
+    rim = row_odd.shape[2]
     rows = all_rows - 2 * rim
-    top[...] = grad_ref[:, :, 0:rim, :]
-    bottom[...] = grad_ref[:, :, rim + rows : all_rows, :]
+    row_odd[...], row_even[...] = paired(
+        "row", grad_ref[:, :, 0:rim, :], grad_ref[:, :, rim + rows : all_rows, :]
+    )
     edges[:, :, 0:rim, :] = grad_ref[:, :, rim : 2 * rim, :]
     edges[:, :, rim : 2 * rim, :] = grad_ref[:, :, rows : rim + rows, :]
     left[...] = grad_ref[:, 0, 2 * rim : rows, :]
     mid[...] = grad_ref[:, 1 : blocks - 1, 2 * rim : rows, :]
     right[...] = grad_ref[:, blocks - 1, 2 * rim : rows, :]
-    if packed:
+    if band_odd.shape[1] == rows - 2 * rim:
+        band_odd[...], band_even[...] = paired("col", left[...], right[...])
+    else:
         half = (rows - 2 * rim) // 2
         upper, lower = slice(2 * rim, 2 * rim + half), slice(2 * rim + half, rows)
-        pack_bands(grad_ref, packed, upper, lower)
+        pack_bands(grad_ref, (band_odd, band_even), upper, lower)
 
 
 def pack_bands(ref, packed, upper, lower):
-    blocks = ref.shape[1]
+    last = ref.shape[1] - 1
     for plane in range(ref.shape[0]):
-        packed[0][plane] = blend(ref[plane, 0, upper, :], swap_halves(ref[plane, 0, lower, :]))
-        packed[1][plane] = blend(
-            swap_halves(ref[plane, blocks - 1, lower, :]), ref[plane, blocks - 1, upper, :]
+        packed[0][plane], packed[1][plane] = paired(
+            "col",
+            blend(ref[plane, 0, upper, :], swap_halves(ref[plane, 0, lower, :])),
+            blend(swap_halves(ref[plane, last, lower, :]), ref[plane, last, upper, :]),
         )
 
 
 def first_kernel(
-    pos_ref, turned_ref, up_ref, down_ref, from_left, from_right, from_up, from_down,
+    pos_ref, turned_ref, up_ref, down_ref, from_odd, from_even, row_odd, row_even,
     amps_ref, probe_ref, tables_ref, field_ref, *rest,
 ):
     pieces, (grad_ref, *work) = rest[:-5], rest[-5:]
     planes, _, rows, _ = turned_ref.shape
     rim = up_ref.shape[2]
     _, (upper, lower) = segments(rows, rim)
-    field_ref[:, :, 0:rim, :] = from_up[...]
+    field_ref[:, :, 0:rim, :], field_ref[:, :, rows + rim : rows + 2 * rim, :] = paired(
+        "row", row_odd[...], row_even[...]
+    )
     field_ref[:, :, rim : 2 * rim, :] = up_ref[...]
     field_ref[:, :, rows : rows + rim, :] = down_ref[...]
-    field_ref[:, :, rows + rim : rows + 2 * rim, :] = from_down[...]
     for plane in range(planes):
 
         def put_upper(block, values):
@@ -277,99 +295,90 @@
         def put_lower(block, values):
             field_ref[plane, block, rim + lower.start : rim + lower.stop, :] = values
 
-        left, right = from_left[plane], from_right[plane]
+        left, right = paired("col", from_odd[plane], from_even[plane])
         lay(turned_ref, plane, upper, left, right, put_upper)
         lay(turned_ref, plane, lower, swap_halves(left), swap_halves(right), put_lower)
     gradients(pos_ref, amps_ref, probe_ref, tables_ref, field_ref, grad_ref, work)
-    write_grad(grad_ref, pieces[:6], pieces[6:])
-
-
-def folded(edges, from_up, from_down, plane, block):
-    rim = from_up.shape[2]
+    write_grad(grad_ref, pieces)
+
+
+def folded(edges, row_odd, row_even, plane, block):
+    rim = row_odd.shape[2]
+    from_up, from_down = paired("row", row_odd[plane, block], row_even[plane, block])
     return (
-        edges[plane, block, 0:rim, :] + from_up[plane, block],
-        edges[plane, block, rim : 2 * rim, :] + from_down[plane, block],
-    )
-
-
-def fold_kernel(edges, from_up, from_down, left_ref, mid_ref, right_ref):
+        edges[plane, block, 0:rim, :] + from_up, edges[plane, block, rim : 2 * rim, :] + from_down
+    )
+
+
+def fold_kernel(edges, row_odd, row_even, folded_ref, odd_ref, even_ref):
     planes, blocks = edges.shape[:2]
-    rim = from_up.shape[2]
+    rim = row_odd.shape[2]
     for plane in range(planes):
         for block in range(blocks):
-            upper, lower = folded(edges, from_up, from_down, plane, block)
-            target = mid_ref.at[plane, block - 1]
+            upper, lower = folded(edges, row_odd, row_even, plane, block)
+            folded_ref[plane, block, 0:rim, :] = upper
+            folded_ref[plane, block, rim : 2 * rim, :] = lower
+    if odd_ref.shape[1] == 2 * rim:
+        odd_ref[...], even_ref[...] = paired("col", folded_ref[:, 0], folded_ref[:, blocks - 1])
+    else:
+        pack_bands(folded_ref, (odd_ref, even_ref), slice(0, rim), slice(rim, 2 * rim))
+
+
+def total_kernel(folded_ref, from_odd, from_even, up_ref, down_ref, odd_ref, even_ref):
+    planes, blocks, rim, _ = up_ref.shape
+    for plane in range(planes):
+        left, right = paired("col", from_odd[plane], from_even[plane])
+        for block in range(blocks):
+            values = folded_ref[plane, block]
             if block == 0:
-                target = left_ref.at[plane]
-            elif block == blocks - 1:
-                target = right_ref.at[plane]
-            target[0:rim, :] = upper
-            target[rim : 2 * rim, :] = lower
-
-
-def total_kernel(left_ref, mid_ref, right_ref, from_left, from_right, up_ref, down_ref):
-    planes, blocks, rim, _ = up_ref.shape
-    for plane in range(planes):
-        for block in range(blocks):
-            if block == 0:
-                values = left_ref[plane] + from_left[plane]
-            elif block == blocks - 1:
-                values = right_ref[plane] + from_right[plane]
-            else:
-                values = mid_ref[plane, block - 1]
+                values += left
+            if block == blocks - 1:
+                values += right
             up_ref[plane, block] = values[0:rim]
             down_ref[plane, block] = values[rim : 2 * rim]
+    odd_ref[...], even_ref[...] = paired("row", up_ref[...], down_ref[...])
 
 
 def next_kernel(
     pos_ref, old_ref, up_ref, down_ref, left_ref, mid_ref, right_ref,
-    from_left, from_right, from_up, from_down, amps_ref, probe_ref, tables_ref, field_ref, *rest,
+    from_odd, from_even, row_odd, row_even, amps_ref, probe_ref, tables_ref, field_ref, *rest,
 ):
     pieces, (grad_ref, *work) = rest[:-5], rest[-5:]
     _, blocks, all_rows, _ = old_ref.shape
     rim = up_ref.shape[2]
     rows = all_rows - 2 * rim
+    from_left, from_right = paired("col", from_odd[...], from_even[...])
     for block in range(blocks):
         lane = lane_ids((1, 1, LANES))
+        from_up, from_down = paired("row", row_odd[:, block], row_even[:, block])
         inside = lane >= 0
         middle = mid_ref[:, block - 1] if 0 < block < blocks - 1 else None
         if block == 0:
             inside = lane >= pos_ref[2, 1] * (LANES // 2)
-            middle = left_ref[...] + from_left[...]
+            middle = left_ref[...] + from_left
         if block == blocks - 1:
             inside = lane < LANES - pos_ref[2, 2] * (LANES // 2)
-            middle = right_ref[...] + from_right[...]
+            middle = right_ref[...] + from_right
         for lo, hi, values in (
-            (0, rim, from_up[:, block]),
+            (0, rim, from_up),
             (rim, 2 * rim, up_ref[:, block]),
             (2 * rim, rows, middle),
             (rows, rows + rim, down_ref[:, block]),
-            (rows + rim, all_rows, from_down[:, block]),
+            (rows + rim, all_rows, from_down),
         ):
             updated = old_ref[:, block, lo:hi, :] - values
             field_ref[:, block, lo:hi, :] = jnp.where(inside, updated, 0.0)
     gradients(pos_ref, amps_ref, probe_ref, tables_ref, field_ref, grad_ref, work)
-    write_grad(grad_ref, pieces[:6], pieces[6:])
-
-
-def last_fold_kernel(edges, from_up, from_down, folded_ref, left_ref, right_ref):
-    planes, blocks = edges.shape[:2]
-    rim = from_up.shape[2]
-    for plane in range(planes):
-        for block in range(blocks):
-            upper, lower = folded(edges, from_up, from_down, plane, block)
-            folded_ref[plane, block, 0:rim, :] = upper
-            folded_ref[plane, block, rim : 2 * rim, :] = lower
-    pack_bands(folded_ref, (left_ref, right_ref), slice(0, rim), slice(rim, 2 * rim))
+    write_grad(grad_ref, pieces)
 
 
 def finish_kernel(
     field_ref, edges, left_ref, mid_ref, right_ref,
-    mid_left, mid_right, edge_left, edge_right, out_ref,
+    mid_odd, mid_even, edge_odd, edge_even, out_ref,
 ):
     planes, blocks, _, _ = field_ref.shape
     rows = out_ref.shape[1]
-    rim = edge_left.shape[1]
+    rim = edge_odd.shape[1]
     (first, last), (upper, lower) = segments(rows, rim)
     half = upper.stop - upper.start
 
@@ -383,7 +392,8 @@
             else mid_ref[plane, block - 1, at, :]
             for block in range(blocks)
         ]
-        extras = [edge_left[plane], edge_right[plane]] if edge else [mid_left[plane], mid_right[plane]]
+        odd, even = (edge_odd, edge_even) if edge else (mid_odd, mid_even)
+        extras = paired("col", odd[plane], even[plane])
         if part == 1:
             extras = [swap_halves(extra) for extra in extras]
         values[0] += extras[0]
@@ -460,80 +470,61 @@
     strip = f32(planes, blocks, rim, LANES)
     packed_edge = f32(planes, rim, LANES)
     packed_mid = f32(planes, band // 2, LANES)
-    turned, left_edge, right_edge, left_mid, right_mid = call(
+    packed_both = [packed_edge] * 2
+    turned, odd_edge, even_edge, odd_mid, even_mid = call(
         pack_kernel,
-        [f32(planes, blocks - 1, tile_r, LANES)] + [packed_edge] * 2 + [packed_mid] * 2,
+        [f32(planes, blocks - 1, tile_r, LANES)] + packed_both + [packed_mid] * 2,
         4,
     )(tile)
-    from_left = neighbour(right_edge, "col", 1)
-    from_right = neighbour(left_edge, "col", -1)
-    mid_left = neighbour(right_mid, "col", 1)
-    mid_right = neighbour(left_mid, "col", -1)
-    up, down, tables = call(
+    edge_strips = exchange(odd_edge, even_edge, "col")
+    mid_strips = exchange(odd_mid, even_mid, "col")
+    up, down, odd, even, tables = call(
         rows_kernel,
-        [strip, strip, pltpu.VMEM(tables.shape, tables.dtype)],
+        [strip] * 4 + [pltpu.VMEM(tables.shape, tables.dtype)],
         4,
         scratch=[pltpu.SemaphoreType.DMA(())],
         raw=[tables],
-    )(turned, from_left, from_right)
-    from_up = neighbour(down, "row", 1)
-    from_down = neighbour(up, "row", -1)
+    )(turned, *edge_strips)
+    row_strips = exchange(odd, even, "row")
 
     field_shape = f32(planes, blocks, tile_r + frame, LANES)
     work = [field_shape] + [pltpu.VMEM((GROUP, 2, frame, frame), jnp.float32)] * 4
+    edge_rows = f32(planes, blocks, 2 * rim, LANES)
     pieces = [
         strip,
         strip,
-        f32(planes, blocks, 2 * rim, LANES),
+        edge_rows,
         f32(planes, band, LANES),
         f32(planes, blocks - 2, band, LANES),
         f32(planes, band, LANES),
     ]
-    field, top, bottom, edges, left, mid, right = call(
-        first_kernel, [field_shape] + pieces, 20, scratch=work, scalars=[pos]
-    )(turned, up, down, mid_left, mid_right, from_up, from_down, amps, probe, tables)
+    field, *grads = call(
+        first_kernel, [field_shape] + pieces + [f32(planes, band, LANES)] * 2, 20,
+        scratch=work, scalars=[pos],
+    )(turned, up, down, *mid_strips, *row_strips, amps, probe, tables)
 
     for iteration in range(1, ITERS):
-        mid_left = neighbour(right, "col", 1)
-        mid_right = neighbour(left, "col", -1)
-        from_up = neighbour(bottom, "row", 1)
-        from_down = neighbour(top, "row", -1)
-        edge_parts = call(
-            fold_kernel,
-            [
-                f32(planes, 2 * rim, LANES),
-                f32(planes, blocks - 2, 2 * rim, LANES),
-                f32(planes, 2 * rim, LANES),
-            ],
-            4,
-        )(edges, from_up, from_down)
-        from_left = neighbour(edge_parts[2], "col", 1)
-        from_right = neighbour(edge_parts[0], "col", -1)
-        up, down = call(total_kernel, [strip, strip], 4)(*edge_parts, from_left, from_right)
-        from_up = neighbour(down, "row", 1)
-        from_down = neighbour(up, "row", -1)
-        last = iteration == ITERS - 1
-        field, top, bottom, edges, left, mid, right, *packed = call(
-            next_kernel,
-            [field_shape] + pieces + [packed_mid] * (2 * last),
-            20,
-            scratch=work,
-            scalars=[pos],
-        )(
-            field, up, down, left, mid, right, mid_left, mid_right, from_up, from_down,
-            amps, probe, tables,
-        )
-
-    mid_left = neighbour(packed[1], "col", 1)
-    mid_right = neighbour(packed[0], "col", -1)
-    from_up = neighbour(bottom, "row", 1)
-    from_down = neighbour(top, "row", -1)
-    edges, edge_left, edge_right = call(
-        last_fold_kernel, [f32(planes, blocks, 2 * rim, LANES)] + [packed_edge] * 2, 4
-    )(edges, from_up, from_down)
-    edge_left, edge_right = neighbour(edge_right, "col", 1), neighbour(edge_left, "col", -1)
+        odd, even, edges, left, mid, right, band_odd, band_even = grads
+        row_strips = exchange(odd, even, "row")
+        mid_strips = exchange(band_odd, band_even, "col")
+        edges, odd, even = call(
+            fold_kernel, [edge_rows] + [f32(planes, 2 * rim, LANES)] * 2, 4
+        )(edges, *row_strips)
+        edge_strips = exchange(odd, even, "col")
+        up, down, odd, even = call(total_kernel, [strip] * 4, 4)(edges, *edge_strips)
+        row_strips = exchange(odd, even, "row")
+        bands = [f32(planes, band, LANES)] * 2 if iteration < ITERS - 1 else [packed_mid] * 2
+        field, *grads = call(
+            next_kernel, [field_shape] + pieces + bands, 20, scratch=work, scalars=[pos]
+        )(field, up, down, left, mid, right, *mid_strips, *row_strips, amps, probe, tables)
+
+    odd, even, edges, left, mid, right, band_odd, band_even = grads
+    row_strips = exchange(odd, even, "row")
+    mid_strips = exchange(band_odd, band_even, "col")
+    edges, odd, even = call(fold_kernel, [edge_rows] + packed_both, 4)(edges, *row_strips)
+    edge_strips = exchange(odd, even, "col")
     (out,) = call(finish_kernel, [jax.ShapeDtypeStruct((planes, tile_r, tile_c), jnp.float32)], 8)(
-        field, edges, left, mid, right, mid_left, mid_right, edge_left, edge_right
+        field, edges, left, mid, right, *mid_strips, *edge_strips
     )
     return out.reshape(object_slices.shape)
 

time: 125 us -> 117 us (0.936)
  the two profiles are of different devices: /device:TPU:13 before, /device:TPU:23 now
where the time goes in v4:
time: 117 us
  starting transfers between devices  63.9 us (55%)
  waiting for transfers between devices  43.7 us (37%)
  Pallas kernels  6.73 us (6%)
  local copies, waits for them, and re-layouts  1.33 us (1%)
    ppermute x20, starting transfers between devices, exchange(): received.append(lax.ppermute(values, axis, pairs))  63.9 us
    ppermute x20, waiting for transfers between devices, exchange(): received.append(lax.ppermute(values, axis, pairs))  43.7 us
    pallas_call x8, Pallas kernels, run(): pl.pallas_call(kernel, out_shape=outs, in_specs=[smem()] * len(scalars) +...  6.73 us
  transfers between devices with their start and end apart: 20, of which 10 were waited for; matrix products, arithmetic and copies ran while one was open for 0% of the time, Pallas kernels for 1%

profile of v4, /device:TPU:23, one launch (start us, length us, event | category | flops | bytes accessed | tf_op | source)
XLA Modules:
  0.0 116.6 jit_solution(6160947338696342574)
XLA Ops:
  0.0 1.3 %copy-done.1 = f32[2,2,256,256]{3,2,1,0:T(8,128)S(1)} copy-done((f32[2,2,256,256]{3,2,1,0:T(8,128)S(1)}, f32[2,2,256,256]{3,2,1,0:T(8,128)}, u32[]{:S(2)}) %copy-start.1) | copy-done | bytes 1048600
  1.8 3.1 %collective-permute-start = (f32[4,64,128]{2,1,0:T(8,128)S(1)}, f32[4,64,128]{2,1,0:T(8,128)S(1)}, u32[]{:S(2)}, u32[]{:S(2)}) collective-permute-start(f32[4,64,128]{2,1,0:T(8,128)S(1)} %get-tuple-element.44), channel_id=1, source_target_pairs={{1,2},{3,4},{5,6},{2,1},{4,3},{6,5},{9,10},{11,12},{13,14},{10,9},... | collective-permute-start | bytes 393224 | tf_op jit(solution)/shard_map/ppermute | solution.py:52
  5.1 2.9 %collective-permute-start.2 = (f32[4,64,128]{2,1,0:T(8,128)S(1)}, f32[4,64,128]{2,1,0:T(8,128)S(1)}, u32[]{:S(2)}, u32[]{:S(2)}) collective-permute-start(f32[4,64,128]{2,1,0:T(8,128)S(1)} %get-tuple-element.48), channel_id=1, source_target_pairs={{1,2},{3,4},{5,6},{2,1},{4,3},{6,5},{9,10},{11,12},{13,14},{10,9},... | collective-permute-start | bytes 393224 | tf_op jit(solution)/shard_map/ppermute | solution.py:52
  9.2 6.4 %collective-permute-done.1.from_even = f32[4,64,128]{2,1,0:T(8,128)S(1)} collective-permute-done((f32[4,64,128]{2,1,0:T(8,128)S(1)}, f32[4,64,128]{2,1,0:T(8,128)S(1)}, u32[]{:S(2)}, u32[]{:S(2)}) %collective-permute-start.1) | collective-permute-done | bytes 131104 | tf_op jit(solution)/shard_map/ppermute | solution.py:52
  15.6 1.2 %shard_map.65 = (f32[4,3,64,128]{3,2,1,0:T(8,128)S(1)}, f32[4,3,64,128]{3,2,1,0:T(8,128)S(1)}, f32[4,3,64,128]{3,2,1,0:T(8,128)S(1)}, f32[4,3,64,128]{3,2,1,0:T(8,128)S(1)}, bf16[8,256,256]{2,1,0:T(8,128)(2,1)S(1)}) custom-call(f32[4,2,256,128]{3,2,1,0:T(8,128)S(1)} %get-tuple-element.43.turned_ref, f32[4,64,128]{2,1,0:T(8,128)S(1)} %collective-permute-done.from_odd, ...), custom_call_target="tpu_custom_call" | custom-call | tf_op jit(solution)/shard_map/pallas_call | solution.py:454
  17.6 1.9 %collective-permute-start.5 = (f32[4,3,64,128]{3,2,1,0:T(8,128)S(1)}, f32[4,3,64,128]{3,2,1,0:T(8,128)S(1)}, u32[]{:S(2)}, u32[]{:S(2)}) collective-permute-start(f32[4,3,64,128]{3,2,1,0:T(8,128)S(1)} %get-tuple-element.51), channel_id=1, source_target_pairs={{0,8},{16,24},{8,0},{24,16},{1,9},{17,25},{9,1},{25,17},{2,10},{18... | collective-permute-start | bytes 1179656 | tf_op jit(solution)/shard_map/ppermute | solution.py:52
  19.6 1.3 %collective-permute-done.5.row_even = f32[4,3,64,128]{3,2,1,0:T(8,128)S(1)} collective-permute-done((f32[4,3,64,128]{3,2,1,0:T(8,128)S(1)}, f32[4,3,64,128]{3,2,1,0:T(8,128)S(1)}, u32[]{:S(2)}, u32[]{:S(2)}) %collective-permute-start.5) | collective-permute-done | bytes 393248 | tf_op jit(solution)/shard_map/ppermute | solution.py:52
  20.9 1.2 %shard_map.66 = (f32[4,3,384,128]{3,2,1,0:T(8,128)S(1)}, f32[4,3,64,128]{3,2,1,0:T(8,128)S(1)}, f32[4,3,64,128]{3,2,1,0:T(8,128)S(1)}, f32[4,3,128,128]{3,2,1,0:...) custom-call(s32[3,16]{1,0:T(4,128)S(1)} %pad_add_fusion.pos_ref, ...), custom_call_target="tpu_custom_call" | custom-call | tf_op jit(solution)/shard_map/pallas_call | solution.py:454
  22.7 19.9 %collective-permute-start.7 = (f32[4,3,64,128]{3,2,1,0:T(8,128)S(1)}, f32[4,3,64,128]{3,2,1,0:T(8,128)S(1)}, u32[]{:S(2)}, u32[]{:S(2)}) collective-permute-start(f32[4,3,64,128]{3,2,1,0:T(8,128)S(1)} %get-tuple-element.56), channel_id=1, source_target_pairs={{0,8},{16,24},{8,0},{24,16},{1,9},{17,25},{9,1},{25,17},{2,10},{18... | collective-permute-start | bytes 1179656 | tf_op jit(solution)/shard_map/ppermute | solution.py:52
  42.6 1.3 %collective-permute-done.7.row_even = f32[4,3,64,128]{3,2,1,0:T(8,128)S(1)} collective-permute-done((f32[4,3,64,128]{3,2,1,0:T(8,128)S(1)}, f32[4,3,64,128]{3,2,1,0:T(8,128)S(1)}, u32[]{:S(2)}, u32[]{:S(2)}) %collective-permute-start.7) | collective-permute-done | bytes 393248 | tf_op jit(solution)/shard_map/ppermute | solution.py:52
  44.1 3.1 %collective-permute-start.8 = (f32[4,128,128]{2,1,0:T(8,128)S(1)}, f32[4,128,128]{2,1,0:T(8,128)S(1)}, u32[]{:S(2)}, u32[]{:S(2)}) collective-permute-start(f32[4,128,128]{2,1,0:T(8,128)S(1)} %get-tuple-element.58), channel_id=1, source_target_pairs={{1,2},{3,4},{5,6},{2,1},{4,3},{6,5},{9,10},{11,12},{13,14},{10,9},... | collective-permute-start | bytes 786440 | tf_op jit(solution)/shard_map/ppermute | solution.py:52
  47.3 4.9 %collective-permute-done.8.from_odd = f32[4,128,128]{2,1,0:T(8,128)S(1)} collective-permute-done((f32[4,128,128]{2,1,0:T(8,128)S(1)}, f32[4,128,128]{2,1,0:T(8,128)S(1)}, u32[]{:S(2)}, u32[]{:S(2)}) %collective-permute-start.8) | collective-permute-done | bytes 262176 | tf_op jit(solution)/shard_map/ppermute | solution.py:52
  52.2 6.8 %collective-permute-done.9.from_even = f32[4,128,128]{2,1,0:T(8,128)S(1)} collective-permute-done((f32[4,128,128]{2,1,0:T(8,128)S(1)}, f32[4,128,128]{2,1,0:T(8,128)S(1)}, u32[]{:S(2)}, u32[]{:S(2)}) %collective-permute-start.9) | collective-permute-done | bytes 262176 | tf_op jit(solution)/shard_map/ppermute | solution.py:52
  59.9 3.8 %collective-permute-start.13 = (f32[4,3,64,128]{3,2,1,0:T(8,128)S(1)}, f32[4,3,64,128]{3,2,1,0:T(8,128)S(1)}, u32[]{:S(2)}, u32[]{:S(2)}) collective-permute-start(f32[4,3,64,128]{3,2,1,0:T(8,128)S(1)} %get-tuple-element.68), channel_id=1, source_target_pairs={{0,8},{16,24},{8,0},{24,16},{1,9},{17,25},{9,1},{25,17},{2,10},{18... | collective-permute-start | bytes 1179656 | tf_op jit(solution)/shard_map/ppermute | solution.py:52
  63.6 3.1 %collective-permute-start.10 = (f32[4,128,128]{2,1,0:T(8,128)S(1)}, f32[4,128,128]{2,1,0:T(8,128)S(1)}, u32[]{:S(2)}, u32[]{:S(2)}) collective-permute-start(f32[4,128,128]{2,1,0:T(8,128)S(1)} %get-tuple-element.65), channel_id=1, source_target_pairs={{1,2},{3,4},{5,6},{2,1},{4,3},{6,5},{9,10},{11,12},{13,14},{10,9},... | collective-permute-start | bytes 786440 | tf_op jit(solution)/shard_map/ppermute | solution.py:52
  67.2 7.1 %collective-permute-done.10.from_odd = f32[4,128,128]{2,1,0:T(8,128)S(1)} collective-permute-done((f32[4,128,128]{2,1,0:T(8,128)S(1)}, f32[4,128,128]{2,1,0:T(8,128)S(1)}, u32[]{:S(2)}, u32[]{:S(2)}) %collective-permute-start.10) | collective-permute-done | bytes 262176 | tf_op jit(solution)/shard_map/ppermute | solution.py:52
  74.3 6.0 %collective-permute-done.11.from_even = f32[4,128,128]{2,1,0:T(8,128)S(1)} collective-permute-done((f32[4,128,128]{2,1,0:T(8,128)S(1)}, f32[4,128,128]{2,1,0:T(8,128)S(1)}, u32[]{:S(2)}, u32[]{:S(2)}) %collective-permute-start.11) | collective-permute-done | bytes 262176 | tf_op jit(solution)/shard_map/ppermute | solution.py:52
  80.3 1.4 %shard_map.69 = (f32[4,3,384,128]{3,2,1,0:T(8,128)S(1)}, f32[4,3,64,128]{3,2,1,0:T(8,128)S(1)}, f32[4,3,64,128]{3,2,1,0:T(8,128)S(1)}, f32[4,3,128,128]{3,2,1,0:...) custom-call(s32[3,16]{1,0:T(4,128)S(1)} %pad_add_fusion.pos_ref, ...), custom_call_target="tpu_custom_call" | custom-call | tf_op jit(solution)/shard_map/pallas_call | solution.py:454
  82.4 15.6 %collective-permute-start.15 = (f32[4,3,64,128]{3,2,1,0:T(8,128)S(1)}, f32[4,3,64,128]{3,2,1,0:T(8,128)S(1)}, u32[]{:S(2)}, u32[]{:S(2)}) collective-permute-start(f32[4,3,64,128]{3,2,1,0:T(8,128)S(1)} %get-tuple-element.72), channel_id=1, source_target_pairs={{0,8},{16,24},{8,0},{24,16},{1,9},{17,25},{9,1},{25,17},{2,10},{18... | collective-permute-start | bytes 1179656 | tf_op jit(solution)/shard_map/ppermute | solution.py:52
  98.0 3.1 %collective-permute-start.16 = (f32[4,64,128]{2,1,0:T(8,128)S(1)}, f32[4,64,128]{2,1,0:T(8,128)S(1)}, u32[]{:S(2)}, u32[]{:S(2)}) collective-permute-start(f32[4,64,128]{2,1,0:T(8,128)S(1)} %get-tuple-element.77), channel_id=1, source_target_pairs={{1,2},{3,4},{5,6},{2,1},{4,3},{6,5},{9,10},{11,12},{13,14},{10,9},... | collective-permute-start | bytes 393224 | tf_op jit(solution)/shard_map/ppermute | solution.py:52
  101.4 3.1 %collective-permute-start.18 = (f32[4,64,128]{2,1,0:T(8,128)S(1)}, f32[4,64,128]{2,1,0:T(8,128)S(1)}, u32[]{:S(2)}, u32[]{:S(2)}) collective-permute-start(f32[4,64,128]{2,1,0:T(8,128)S(1)} %get-tuple-element.79), channel_id=1, source_target_pairs={{1,2},{3,4},{5,6},{2,1},{4,3},{6,5},{9,10},{11,12},{13,14},{10,9},... | collective-permute-start | bytes 393224 | tf_op jit(solution)/shard_map/ppermute | solution.py:52
  105.8 6.0 %collective-permute-done.17.mid_even = f32[4,64,128]{2,1,0:T(8,128)S(1)} collective-permute-done((f32[4,64,128]{2,1,0:T(8,128)S(1)}, f32[4,64,128]{2,1,0:T(8,128)S(1)}, u32[]{:S(2)}, u32[]{:S(2)}) %collective-permute-start.17) | collective-permute-done | bytes 131104 | tf_op jit(solution)/shard_map/ppermute | solution.py:52
  111.8 2.8 %collective-permute-done.19.edge_even = f32[4,64,128]{2,1,0:T(8,128)S(1)} collective-permute-done((f32[4,64,128]{2,1,0:T(8,128)S(1)}, f32[4,64,128]{2,1,0:T(8,128)S(1)}, u32[]{:S(2)}, u32[]{:S(2)}) %collective-permute-start.19) | collective-permute-done | bytes 131104 | tf_op jit(solution)/shard_map/ppermute | solution.py:52
  114.6 1.9 %shard_map.71 = f32[4,256,256]{2,1,0:T(8,128)} custom-call(f32[4,3,384,128]{3,2,1,0:T(8,128)S(1)} %get-tuple-element.69.field_ref, f32[4,3,128,128]{3,2,1,0:T(8,128)S(1)} %get-tuple-element.73.edges, f32[4,128,128]{2,1,0:T(8,128)S(1)} %get-tuple-element.74.left_ref, f32[4,1,128,128]{3,2,1,0:T(8,128)S(1)} %get-tuple-element.75.mid_ref, ...), custom_call_target="tpu_custom_call" | custom-call | tf_op jit(solution)/shard_map/pallas_call | solution.py:454
  (36 shorter events, 6.3 us)
Async XLA Ops:
  0.0 20.9 %copy-start = (f32[1,1,16,128,128]{4,3,2,1,0:T(8,128)S(1)}, f32[1,1,16,128,128]{4,3,2,1,0:T(8,128)}, u32[]{:S(2)}) copy-start(f32[1,1,16,128,128]{4,3,2,1,0:T(8,128)} %param.8) | copy-start | bytes 3145732
  0.0 1.3 %copy-start.1 = (f32[2,2,256,256]{3,2,1,0:T(8,128)S(1)}, f32[2,2,256,256]{3,2,1,0:T(8,128)}, u32[]{:S(2)}) copy-start(f32[2,2,256,256]{3,2,1,0:T(8,128)} %param.6) | copy-start | bytes 3145732
  1.3 18.2 %copy-start.3 = (s32[2,1,1,16]{3,2,1,0:T(1,128)S(1)}, s32[2,1,1,16]{3,2,1,0:T(1,128)}, u32[]{:S(2)}) copy-start(s32[2,1,1,16]{3,2,1,0:T(1,128)} %param.9) | copy-start | bytes 388
  1.3 19.5 %copy-start.2 = (f32[2,128,128]{2,1,0:T(8,128)S(1)}, f32[2,128,128]{2,1,0:T(8,128)}, u32[]{:S(2)}) copy-start(f32[2,128,128]{2,1,0:T(8,128)} %probe_ref.3) | copy-start | bytes 393220
  1.8 7.4 %collective-permute-start = (f32[4,64,128]{2,1,0:T(8,128)S(1)}, f32[4,64,128]{2,1,0:T(8,128)S(1)}, u32[]{:S(2)}, u32[]{:S(2)}) collective-permute-start(f32[4,64,128]{2,1,0:T(8,128)S(1)} %get-tuple-element.44), channel_id=1, source_target_pairs={{1,2},{3,4},{5,6},{2,1},{4,3},{6,5},{9,10},{11,12},{13,14},{10,9},... | collective-permute-start | bytes 393224 | tf_op jit(solution)/shard_map/ppermute | solution.py:52
  4.9 10.7 %collective-permute-start.1 = (f32[4,64,128]{2,1,0:T(8,128)S(1)}, f32[4,64,128]{2,1,0:T(8,128)S(1)}, u32[]{:S(2)}, u32[]{:S(2)}) collective-permute-start(f32[4,64,128]{2,1,0:T(8,128)S(1)} %get-tuple-element.45), channel_id=1, source_target_pairs={{0,1},{2,3},{4,5},{6,7},{1,0},{3,2},{5,4},{7,6},{8,9},{10,11},{12,... | collective-permute-start | bytes 393224 | tf_op jit(solution)/shard_map/ppermute | solution.py:52
  5.1 14.4 %collective-permute-start.2 = (f32[4,64,128]{2,1,0:T(8,128)S(1)}, f32[4,64,128]{2,1,0:T(8,128)S(1)}, u32[]{:S(2)}, u32[]{:S(2)}) collective-permute-start(f32[4,64,128]{2,1,0:T(8,128)S(1)} %get-tuple-element.48), channel_id=1, source_target_pairs={{1,2},{3,4},{5,6},{2,1},{4,3},{6,5},{9,10},{11,12},{13,14},{10,9},... | collective-permute-start | bytes 393224 | tf_op jit(solution)/shard_map/ppermute | solution.py:52
  8.1 11.5 %collective-permute-start.3 = (f32[4,64,128]{2,1,0:T(8,128)S(1)}, f32[4,64,128]{2,1,0:T(8,128)S(1)}, u32[]{:S(2)}, u32[]{:S(2)}) collective-permute-start(f32[4,64,128]{2,1,0:T(8,128)S(1)} %get-tuple-element.49), channel_id=1, source_target_pairs={{0,1},{2,3},{4,5},{6,7},{1,0},{3,2},{5,4},{7,6},{8,9},{10,11},{12,... | collective-permute-start | bytes 393224 | tf_op jit(solution)/shard_map/ppermute | solution.py:52
  16.9 2.7 %collective-permute-start.4 = (f32[4,3,64,128]{3,2,1,0:T(8,128)S(1)}, f32[4,3,64,128]{3,2,1,0:T(8,128)S(1)}, u32[]{:S(2)}, u32[]{:S(2)}) collective-permute-start(f32[4,3,64,128]{3,2,1,0:T(8,128)S(1)} %get-tuple-element.50), channel_id=1, source_target_pairs={{8,16},{16,8},{9,17},{17,9},{10,18},{18,10},{11,19},{19,11},{12,20... | collective-permute-start | bytes 1179656 | tf_op jit(solution)/shard_map/ppermute | solution.py:52
  17.6 3.3 %collective-permute-start.5 = (f32[4,3,64,128]{3,2,1,0:T(8,128)S(1)}, f32[4,3,64,128]{3,2,1,0:T(8,128)S(1)}, u32[]{:S(2)}, u32[]{:S(2)}) collective-permute-start(f32[4,3,64,128]{3,2,1,0:T(8,128)S(1)} %get-tuple-element.51), channel_id=1, source_target_pairs={{0,8},{16,24},{8,0},{24,16},{1,9},{17,25},{9,1},{25,17},{2,10},{18... | collective-permute-start | bytes 1179656 | tf_op jit(solution)/shard_map/ppermute | solution.py:52
  22.0 20.6 %collective-permute-start.6 = (f32[4,3,64,128]{3,2,1,0:T(8,128)S(1)}, f32[4,3,64,128]{3,2,1,0:T(8,128)S(1)}, u32[]{:S(2)}, u32[]{:S(2)}) collective-permute-start(f32[4,3,64,128]{3,2,1,0:T(8,128)S(1)} %get-tuple-element.55), channel_id=1, source_target_pairs={{8,16},{16,8},{9,17},{17,9},{10,18},{18,10},{11,19},{19,11},{12,20... | collective-permute-start | bytes 1179656 | tf_op jit(solution)/shard_map/ppermute | solution.py:52
  22.7 21.2 %collective-permute-start.7 = (f32[4,3,64,128]{3,2,1,0:T(8,128)S(1)}, f32[4,3,64,128]{3,2,1,0:T(8,128)S(1)}, u32[]{:S(2)}, u32[]{:S(2)}) collective-permute-start(f32[4,3,64,128]{3,2,1,0:T(8,128)S(1)} %get-tuple-element.56), channel_id=1, source_target_pairs={{0,8},{16,24},{8,0},{24,16},{1,9},{17,25},{9,1},{25,17},{2,10},{18... | collective-permute-start | bytes 1179656 | tf_op jit(solution)/shard_map/ppermute | solution.py:52
  44.1 8.1 %collective-permute-start.8 = (f32[4,128,128]{2,1,0:T(8,128)S(1)}, f32[4,128,128]{2,1,0:T(8,128)S(1)}, u32[]{:S(2)}, u32[]{:S(2)}) collective-permute-start(f32[4,128,128]{2,1,0:T(8,128)S(1)} %get-tuple-element.58), channel_id=1, source_target_pairs={{1,2},{3,4},{5,6},{2,1},{4,3},{6,5},{9,10},{11,12},{13,14},{10,9},... | collective-permute-start | bytes 786440 | tf_op jit(solution)/shard_map/ppermute | solution.py:52
  47.2 11.8 %collective-permute-start.9 = (f32[4,128,128]{2,1,0:T(8,128)S(1)}, f32[4,128,128]{2,1,0:T(8,128)S(1)}, u32[]{:S(2)}, u32[]{:S(2)}) collective-permute-start(f32[4,128,128]{2,1,0:T(8,128)S(1)} %get-tuple-element.59), channel_id=1, source_target_pairs={{0,1},{2,3},{4,5},{6,7},{1,0},{3,2},{5,4},{7,6},{8,9},{10,11},{12,... | collective-permute-start | bytes 786440 | tf_op jit(solution)/shard_map/ppermute | solution.py:52
  59.2 21.1 %collective-permute-start.12 = (f32[4,3,64,128]{3,2,1,0:T(8,128)S(1)}, f32[4,3,64,128]{3,2,1,0:T(8,128)S(1)}, u32[]{:S(2)}, u32[]{:S(2)}) collective-permute-start(f32[4,3,64,128]{3,2,1,0:T(8,128)S(1)} %get-tuple-element.67), channel_id=1, source_target_pairs={{8,16},{16,8},{9,17},{17,9},{10,18},{18,10},{11,19},{19,11},{12,20... | collective-permute-start | bytes 1179656 | tf_op jit(solution)/shard_map/ppermute | solution.py:52
  59.9 20.4 %collective-permute-start.13 = (f32[4,3,64,128]{3,2,1,0:T(8,128)S(1)}, f32[4,3,64,128]{3,2,1,0:T(8,128)S(1)}, u32[]{:S(2)}, u32[]{:S(2)}) collective-permute-start(f32[4,3,64,128]{3,2,1,0:T(8,128)S(1)} %get-tuple-element.68), channel_id=1, source_target_pairs={{0,8},{16,24},{8,0},{24,16},{1,9},{17,25},{9,1},{25,17},{2,10},{18... | collective-permute-start | bytes 1179656 | tf_op jit(solution)/shard_map/ppermute | solution.py:52
  63.6 10.7 %collective-permute-start.10 = (f32[4,128,128]{2,1,0:T(8,128)S(1)}, f32[4,128,128]{2,1,0:T(8,128)S(1)}, u32[]{:S(2)}, u32[]{:S(2)}) collective-permute-start(f32[4,128,128]{2,1,0:T(8,128)S(1)} %get-tuple-element.65), channel_id=1, source_target_pairs={{1,2},{3,4},{5,6},{2,1},{4,3},{6,5},{9,10},{11,12},{13,14},{10,9},... | collective-permute-start | bytes 786440 | tf_op jit(solution)/shard_map/ppermute | solution.py:52
  66.8 13.5 %collective-permute-start.11 = (f32[4,128,128]{2,1,0:T(8,128)S(1)}, f32[4,128,128]{2,1,0:T(8,128)S(1)}, u32[]{:S(2)}, u32[]{:S(2)}) collective-permute-start(f32[4,128,128]{2,1,0:T(8,128)S(1)} %get-tuple-element.66), channel_id=1, source_target_pairs={{0,1},{2,3},{4,5},{6,7},{1,0},{3,2},{5,4},{7,6},{8,9},{10,11},{12,... | collective-permute-start | bytes 786440 | tf_op jit(solution)/shard_map/ppermute | solution.py:52
  81.7 19.4 %collective-permute-start.14 = (f32[4,3,64,128]{3,2,1,0:T(8,128)S(1)}, f32[4,3,64,128]{3,2,1,0:T(8,128)S(1)}, u32[]{:S(2)}, u32[]{:S(2)}) collective-permute-start(f32[4,3,64,128]{3,2,1,0:T(8,128)S(1)} %get-tuple-element.71), channel_id=1, source_target_pairs={{8,16},{16,8},{9,17},{17,9},{10,18},{18,10},{11,19},{19,11},{12,20... | collective-permute-start | bytes 1179656 | tf_op jit(solution)/shard_map/ppermute | solution.py:52
  82.4 18.7 %collective-permute-start.15 = (f32[4,3,64,128]{3,2,1,0:T(8,128)S(1)}, f32[4,3,64,128]{3,2,1,0:T(8,128)S(1)}, u32[]{:S(2)}, u32[]{:S(2)}) collective-permute-start(f32[4,3,64,128]{3,2,1,0:T(8,128)S(1)} %get-tuple-element.72), channel_id=1, source_target_pairs={{0,8},{16,24},{8,0},{24,16},{1,9},{17,25},{9,1},{25,17},{2,10},{18... | collective-permute-start | bytes 1179656 | tf_op jit(solution)/shard_map/ppermute | solution.py:52
  98.0 7.9 %collective-permute-start.16 = (f32[4,64,128]{2,1,0:T(8,128)S(1)}, f32[4,64,128]{2,1,0:T(8,128)S(1)}, u32[]{:S(2)}, u32[]{:S(2)}) collective-permute-start(f32[4,64,128]{2,1,0:T(8,128)S(1)} %get-tuple-element.77), channel_id=1, source_target_pairs={{1,2},{3,4},{5,6},{2,1},{4,3},{6,5},{9,10},{11,12},{13,14},{10,9},... | collective-permute-start | bytes 393224 | tf_op jit(solution)/shard_map/ppermute | solution.py:52
  101.1 10.7 %collective-permute-start.17 = (f32[4,64,128]{2,1,0:T(8,128)S(1)}, f32[4,64,128]{2,1,0:T(8,128)S(1)}, u32[]{:S(2)}, u32[]{:S(2)}) collective-permute-start(f32[4,64,128]{2,1,0:T(8,128)S(1)} %get-tuple-element.78), channel_id=1, source_target_pairs={{0,1},{2,3},{4,5},{6,7},{1,0},{3,2},{5,4},{7,6},{8,9},{10,11},{12,... | collective-permute-start | bytes 393224 | tf_op jit(solution)/shard_map/ppermute | solution.py:52
  101.4 10.4 %collective-permute-start.18 = (f32[4,64,128]{2,1,0:T(8,128)S(1)}, f32[4,64,128]{2,1,0:T(8,128)S(1)}, u32[]{:S(2)}, u32[]{:S(2)}) collective-permute-start(f32[4,64,128]{2,1,0:T(8,128)S(1)} %get-tuple-element.79), channel_id=1, source_target_pairs={{1,2},{3,4},{5,6},{2,1},{4,3},{6,5},{9,10},{11,12},{13,14},{10,9},... | collective-permute-start | bytes 393224 | tf_op jit(solution)/shard_map/ppermute | solution.py:52
  104.5 10.2 %collective-permute-start.19 = (f32[4,64,128]{2,1,0:T(8,128)S(1)}, f32[4,64,128]{2,1,0:T(8,128)S(1)}, u32[]{:S(2)}, u32[]{:S(2)}) collective-permute-start(f32[4,64,128]{2,1,0:T(8,128)S(1)} %get-tuple-element.80), channel_id=1, source_target_pairs={{0,1},{2,3},{4,5},{6,7},{1,0},{3,2},{5,4},{7,6},{8,9},{10,11},{12,... | collective-permute-start | bytes 393224 | tf_op jit(solution)/shard_map/ppermute | solution.py:52

commit v5 on v4

--- a/solution.py
+++ b/solution.py
@@ -11,7 +11,7 @@
 
 ITERS = 2
 LANES = 128
-GROUP = 4
+GROUP = 8
 
 modulus_offset = 0.5
 fresnel_scale = 0.9
@@ -122,11 +122,13 @@
         put(block, blend(parts[block], parts[block + 1]))
 
 
-def rows_kernel(
-    turned_ref, from_odd, from_even, tables_hbm, up_ref, down_ref, odd_ref, even_ref, tables_ref, sem
-):
-    copy = pltpu.make_async_copy(tables_hbm, tables_ref, sem)
+def load_kernel(source_hbm, target_ref, sem):
+    copy = pltpu.make_async_copy(source_hbm, target_ref, sem)
     copy.start()
+    copy.wait()
+
+
+def rows_kernel(turned_ref, from_odd, from_even, up_ref, down_ref, odd_ref, even_ref):
     planes, _, rows, _ = turned_ref.shape
     rim = up_ref.shape[2]
     (upper, lower), _ = segments(rows, rim)
@@ -142,7 +144,6 @@
         lay(turned_ref, plane, upper, left, right, put_up)
         lay(turned_ref, plane, lower, swap_halves(left), swap_halves(right), put_down)
     odd_ref[...], even_ref[...] = paired("row", up_ref[...], down_ref[...])
-    copy.wait()
 
 
 def gradients(pos_ref, amps_ref, probe_ref, tables_ref, field_ref, grad_ref, work):
@@ -164,11 +165,15 @@
         return dot(table_high, high) + (dot(table_high, low) + dot(table_low, high))
 
     def two_sided(zs, right_index, left_index):
-        result = []
-        for pair in range(0, len(zs), 2):
-            rows = jnp.concatenate([jnp.concatenate(z, axis=1) for z in zs[pair : pair + 2]], axis=0)
-            out = right(rows, right_index)
-            mixed = left(
+        outs = [
+            right(
+                jnp.concatenate([jnp.concatenate(z, axis=1) for z in zs[pair : pair + 2]], axis=0),
+                right_index,
+            )
+            for pair in range(0, len(zs), 2)
+        ]
+        mixes = [
+            left(
                 jnp.concatenate(
                     [
                         jnp.concatenate([out[:frame, :frame], out[frame:, :frame]], axis=1),
@@ -178,6 +183,10 @@
                 ),
                 left_index,
             )
+            for out in outs
+        ]
+        result = []
+        for mixed in mixes:
             for k in range(2):
                 cols = slice(k * frame, (k + 1) * frame)
                 result.append((mixed[:frame, cols], mixed[frame:, cols]))
@@ -478,13 +487,14 @@
     )(tile)
     edge_strips = exchange(odd_edge, even_edge, "col")
     mid_strips = exchange(odd_mid, even_mid, "col")
-    up, down, odd, even, tables = call(
-        rows_kernel,
-        [strip] * 4 + [pltpu.VMEM(tables.shape, tables.dtype)],
+    up, down, odd, even = call(rows_kernel, [strip] * 4, 4)(turned, *edge_strips)
+    (tables,) = call(
+        load_kernel,
+        [pltpu.VMEM(tables.shape, tables.dtype)],
         4,
         scratch=[pltpu.SemaphoreType.DMA(())],
         raw=[tables],
-    )(turned, *edge_strips)
+    )()
     row_strips = exchange(odd, even, "row")
 
     field_shape = f32(planes, blocks, tile_r + frame, LANES)

time: 117 us -> 111 us (0.949)
  the two profiles are of different devices: /device:TPU:23 before, /device:TPU:1 now
where the time goes in v5:
time: 111 us; the launch traced here: 109 us
  waiting for transfers between devices  41.1 us (37%)
  starting transfers between devices  40 us (36%)
  Pallas kernels  25.6 us (23%)
  local copies, waits for them, and re-layouts  1.33 us (1%)
    ppermute x20, waiting for transfers between devices, exchange(): received.append(lax.ppermute(values, axis, pairs))  41.1 us
    ppermute x20, starting transfers between devices, exchange(): received.append(lax.ppermute(values, axis, pairs))  40 us
    pallas_call x9, Pallas kernels, run(): pl.pallas_call(kernel, out_shape=outs, in_specs=[smem()] * len(scalars) +...  25.6 us
  transfers between devices with their start and end apart: 20, of which 7 were waited for; matrix products, arithmetic and copies ran while one was open for 0% of the time, Pallas kernels for 1%

profile of v5, /device:TPU:1, one launch (start us, length us, event | category | flops | bytes accessed | tf_op | source)
XLA Modules:
  0.0 108.9 jit_solution(6964543420955961349)
XLA Ops:
  0.0 1.3 %copy-done.1 = f32[2,2,256,256]{3,2,1,0:T(8,128)S(1)} copy-done((f32[2,2,256,256]{3,2,1,0:T(8,128)S(1)}, f32[2,2,256,256]{3,2,1,0:T(8,128)}, u32[]{:S(2)}) %copy-start.1) | copy-done | bytes 1048600
  2.5 4.6 %collective-permute-start.1 = (f32[4,64,128]{2,1,0:T(8,128)S(1)}, f32[4,64,128]{2,1,0:T(8,128)S(1)}, u32[]{:S(2)}, u32[]{:S(2)}) collective-permute-start(f32[4,64,128]{2,1,0:T(8,128)S(1)} %get-tuple-element.44), channel_id=1, source_target_pairs={{0,1},{2,3},{4,5},{6,7},{1,0},{3,2},{5,4},{7,6},{8,9},{10,11},{12,... | collective-permute-start | bytes 393224 | tf_op jit(solution)/shard_map/ppermute | solution.py:52
  7.7 3.8 %collective-permute-start.3 = (f32[4,64,128]{2,1,0:T(8,128)S(1)}, f32[4,64,128]{2,1,0:T(8,128)S(1)}, u32[]{:S(2)}, u32[]{:S(2)}) collective-permute-start(f32[4,64,128]{2,1,0:T(8,128)S(1)} %get-tuple-element.48), channel_id=1, source_target_pairs={{0,1},{2,3},{4,5},{6,7},{1,0},{3,2},{5,4},{7,6},{8,9},{10,11},{12,... | collective-permute-start | bytes 393224 | tf_op jit(solution)/shard_map/ppermute | solution.py:52
  12.3 3.2 %collective-permute-done.1.from_even = f32[4,64,128]{2,1,0:T(8,128)S(1)} collective-permute-done((f32[4,64,128]{2,1,0:T(8,128)S(1)}, f32[4,64,128]{2,1,0:T(8,128)S(1)}, u32[]{:S(2)}, u32[]{:S(2)}) %collective-permute-start.1) | collective-permute-done | bytes 131104 | tf_op jit(solution)/shard_map/ppermute | solution.py:52
  15.6 3.6 %collective-permute-start.4 = (f32[4,3,64,128]{3,2,1,0:T(8,128)S(1)}, f32[4,3,64,128]{3,2,1,0:T(8,128)S(1)}, u32[]{:S(2)}, u32[]{:S(2)}) collective-permute-start(f32[4,3,64,128]{3,2,1,0:T(8,128)S(1)} %get-tuple-element.49), channel_id=1, source_target_pairs={{8,16},{16,8},{9,17},{17,9},{10,18},{18,10},{11,19},{19,11},{12,20... | collective-permute-start | bytes 1179656 | tf_op jit(solution)/shard_map/ppermute | solution.py:52
  19.4 1.2 %shard_map.66.tables_ref = bf16[8,256,256]{2,1,0:T(8,128)(2,1)S(1)} custom-call(bf16[8,256,256]{2,1,0:T(8,128)(2,1)} %constant.16.clone.source_hbm), custom_call_target="tpu_custom_call" | custom-call | tf_op jit(solution)/shard_map/pallas_call | solution.py:463
  20.6 4.1 %collective-permute-done.4.row_odd = f32[4,3,64,128]{3,2,1,0:T(8,128)S(1)} collective-permute-done((f32[4,3,64,128]{3,2,1,0:T(8,128)S(1)}, f32[4,3,64,128]{3,2,1,0:T(8,128)S(1)}, u32[]{:S(2)}, u32[]{:S(2)}) %collective-permute-start.4) | collective-permute-done | bytes 393248 | tf_op jit(solution)/shard_map/ppermute | solution.py:52
  24.7 10.5 %shard_map.67 = (f32[4,3,384,128]{3,2,1,0:T(8,128)S(1)}, f32[4,3,64,128]{3,2,1,0:T(8,128)S(1)}, f32[4,3,64,128]{3,2,1,0:T(8,128)S(1)}, f32[4,3,128,128]{3,2,1,0:...) custom-call(s32[3,16]{1,0:T(4,128)S(1)} %pad_add_fusion.pos_ref, ...), custom_call_target="tpu_custom_call" | custom-call | tf_op jit(solution)/shard_map/pallas_call | solution.py:463
  35.3 1.9 %collective-permute-start.6 = (f32[4,3,64,128]{3,2,1,0:T(8,128)S(1)}, f32[4,3,64,128]{3,2,1,0:T(8,128)S(1)}, u32[]{:S(2)}, u32[]{:S(2)}) collective-permute-start(f32[4,3,64,128]{3,2,1,0:T(8,128)S(1)} %get-tuple-element.53), channel_id=1, source_target_pairs={{8,16},{16,8},{9,17},{17,9},{10,18},{18,10},{11,19},{19,11},{12,20... | collective-permute-start | bytes 1179656 | tf_op jit(solution)/shard_map/ppermute | solution.py:52
  37.3 7.1 %collective-permute-done.6.row_odd = f32[4,3,64,128]{3,2,1,0:T(8,128)S(1)} collective-permute-done((f32[4,3,64,128]{3,2,1,0:T(8,128)S(1)}, f32[4,3,64,128]{3,2,1,0:T(8,128)S(1)}, u32[]{:S(2)}, u32[]{:S(2)}) %collective-permute-start.6) | collective-permute-done | bytes 393248 | tf_op jit(solution)/shard_map/ppermute | solution.py:52
  44.5 0.7 collective-permute-start.8
  45.2 3.8 %collective-permute-start.9 = (f32[4,128,128]{2,1,0:T(8,128)S(1)}, f32[4,128,128]{2,1,0:T(8,128)S(1)}, u32[]{:S(2)}, u32[]{:S(2)}) collective-permute-start(f32[4,128,128]{2,1,0:T(8,128)S(1)} %get-tuple-element.57), channel_id=1, source_target_pairs={{0,1},{2,3},{4,5},{6,7},{1,0},{3,2},{5,4},{7,6},{8,9},{10,11},{12,... | collective-permute-start | bytes 786440 | tf_op jit(solution)/shard_map/ppermute | solution.py:52
  49.0 6.7 %collective-permute-done.9.from_even = f32[4,128,128]{2,1,0:T(8,128)S(1)} collective-permute-done((f32[4,128,128]{2,1,0:T(8,128)S(1)}, f32[4,128,128]{2,1,0:T(8,128)S(1)}, u32[]{:S(2)}, u32[]{:S(2)}) %collective-permute-start.9) | collective-permute-done | bytes 262176 | tf_op jit(solution)/shard_map/ppermute | solution.py:52
  55.8 3.1 %collective-permute-start.12 = (f32[4,3,64,128]{3,2,1,0:T(8,128)S(1)}, f32[4,3,64,128]{3,2,1,0:T(8,128)S(1)}, u32[]{:S(2)}, u32[]{:S(2)}) collective-permute-start(f32[4,3,64,128]{3,2,1,0:T(8,128)S(1)} %get-tuple-element.65), channel_id=1, source_target_pairs={{8,16},{16,8},{9,17},{17,9},{10,18},{18,10},{11,19},{19,11},{12,20... | collective-permute-start | bytes 1179656 | tf_op jit(solution)/shard_map/ppermute | solution.py:52
  58.9 0.7 collective-permute-start.10
  59.6 4.3 %collective-permute-start.11 = (f32[4,128,128]{2,1,0:T(8,128)S(1)}, f32[4,128,128]{2,1,0:T(8,128)S(1)}, u32[]{:S(2)}, u32[]{:S(2)}) collective-permute-start(f32[4,128,128]{2,1,0:T(8,128)S(1)} %get-tuple-element.64), channel_id=1, source_target_pairs={{0,1},{2,3},{4,5},{6,7},{1,0},{3,2},{5,4},{7,6},{8,9},{10,11},{12,... | collective-permute-start | bytes 786440 | tf_op jit(solution)/shard_map/ppermute | solution.py:52
  63.9 11.6 %collective-permute-done.11.from_even = f32[4,128,128]{2,1,0:T(8,128)S(1)} collective-permute-done((f32[4,128,128]{2,1,0:T(8,128)S(1)}, f32[4,128,128]{2,1,0:T(8,128)S(1)}, u32[]{:S(2)}, u32[]{:S(2)}) %collective-permute-start.11) | collective-permute-done | bytes 262176 | tf_op jit(solution)/shard_map/ppermute | solution.py:52
  75.6 10.8 %shard_map.70 = (f32[4,3,384,128]{3,2,1,0:T(8,128)S(1)}, f32[4,3,64,128]{3,2,1,0:T(8,128)S(1)}, f32[4,3,64,128]{3,2,1,0:T(8,128)S(1)}, f32[4,3,128,128]{3,2,1,0:...) custom-call(s32[3,16]{1,0:T(4,128)S(1)} %pad_add_fusion.pos_ref, ...), custom_call_target="tpu_custom_call" | custom-call | tf_op jit(solution)/shard_map/pallas_call | solution.py:463
  86.4 1.9 %collective-permute-start.14 = (f32[4,3,64,128]{3,2,1,0:T(8,128)S(1)}, f32[4,3,64,128]{3,2,1,0:T(8,128)S(1)}, u32[]{:S(2)}, u32[]{:S(2)}) collective-permute-start(f32[4,3,64,128]{3,2,1,0:T(8,128)S(1)} %get-tuple-element.69), channel_id=1, source_target_pairs={{8,16},{16,8},{9,17},{17,9},{10,18},{18,10},{11,19},{19,11},{12,20... | collective-permute-start | bytes 1179656 | tf_op jit(solution)/shard_map/ppermute | solution.py:52
  89.1 3.5 %collective-permute-start.17 = (f32[4,64,128]{2,1,0:T(8,128)S(1)}, f32[4,64,128]{2,1,0:T(8,128)S(1)}, u32[]{:S(2)}, u32[]{:S(2)}) collective-permute-start(f32[4,64,128]{2,1,0:T(8,128)S(1)} %get-tuple-element.76), channel_id=1, source_target_pairs={{0,1},{2,3},{4,5},{6,7},{1,0},{3,2},{5,4},{7,6},{8,9},{10,11},{12,... | collective-permute-start | bytes 393224 | tf_op jit(solution)/shard_map/ppermute | solution.py:52
  92.6 3.2 %collective-permute-done.14.row_odd = f32[4,3,64,128]{3,2,1,0:T(8,128)S(1)} collective-permute-done((f32[4,3,64,128]{3,2,1,0:T(8,128)S(1)}, f32[4,3,64,128]{3,2,1,0:T(8,128)S(1)}, u32[]{:S(2)}, u32[]{:S(2)}) %collective-permute-start.14) | collective-permute-done | bytes 393248 | tf_op jit(solution)/shard_map/ppermute | solution.py:52
  96.7 5.2 %collective-permute-start.19 = (f32[4,64,128]{2,1,0:T(8,128)S(1)}, f32[4,64,128]{2,1,0:T(8,128)S(1)}, u32[]{:S(2)}, u32[]{:S(2)}) collective-permute-start(f32[4,64,128]{2,1,0:T(8,128)S(1)} %get-tuple-element.78), channel_id=1, source_target_pairs={{0,1},{2,3},{4,5},{6,7},{1,0},{3,2},{5,4},{7,6},{8,9},{10,11},{12,... | collective-permute-start | bytes 393224 | tf_op jit(solution)/shard_map/ppermute | solution.py:52
  101.9 5.1 %collective-permute-done.19.edge_even = f32[4,64,128]{2,1,0:T(8,128)S(1)} collective-permute-done((f32[4,64,128]{2,1,0:T(8,128)S(1)}, f32[4,64,128]{2,1,0:T(8,128)S(1)}, u32[]{:S(2)}, u32[]{:S(2)}) %collective-permute-start.19) | collective-permute-done | bytes 131104 | tf_op jit(solution)/shard_map/ppermute | solution.py:52
  107.0 1.9 %shard_map.72 = f32[4,256,256]{2,1,0:T(8,128)} custom-call(f32[4,3,384,128]{3,2,1,0:T(8,128)S(1)} %get-tuple-element.67.field_ref, f32[4,3,128,128]{3,2,1,0:T(8,128)S(1)} %get-tuple-element.71.edges, f32[4,128,128]{2,1,0:T(8,128)S(1)} %get-tuple-element.72.left_ref, f32[4,1,128,128]{3,2,1,0:T(8,128)S(1)} %get-tuple-element.73.mid_ref, ...), custom_call_target="tpu_custom_call" | custom-call | tf_op jit(solution)/shard_map/pallas_call | solution.py:463
  (37 shorter events, 4.2 us)
Async XLA Ops:
  0.0 24.7 %copy-start = (f32[1,1,16,128,128]{4,3,2,1,0:T(8,128)S(1)}, f32[1,1,16,128,128]{4,3,2,1,0:T(8,128)}, u32[]{:S(2)}) copy-start(f32[1,1,16,128,128]{4,3,2,1,0:T(8,128)} %param.8) | copy-start | bytes 3145732
  0.0 1.3 %copy-start.1 = (f32[2,2,256,256]{3,2,1,0:T(8,128)S(1)}, f32[2,2,256,256]{3,2,1,0:T(8,128)}, u32[]{:S(2)}) copy-start(f32[2,2,256,256]{3,2,1,0:T(8,128)} %param.6) | copy-start | bytes 3145732
  1.3 18.0 %copy-start.3 = (s32[2,1,1,16]{3,2,1,0:T(1,128)S(1)}, s32[2,1,1,16]{3,2,1,0:T(1,128)}, u32[]{:S(2)}) copy-start(s32[2,1,1,16]{3,2,1,0:T(1,128)} %param.9) | copy-start | bytes 388
  1.3 23.4 %copy-start.2 = (f32[2,128,128]{2,1,0:T(8,128)S(1)}, f32[2,128,128]{2,1,0:T(8,128)}, u32[]{:S(2)}) copy-start(f32[2,128,128]{2,1,0:T(8,128)} %probe_ref.3) | copy-start | bytes 393220
  1.8 10.5 %collective-permute-start = (f32[4,64,128]{2,1,0:T(8,128)S(1)}, f32[4,64,128]{2,1,0:T(8,128)S(1)}, u32[]{:S(2)}, u32[]{:S(2)}) collective-permute-start(f32[4,64,128]{2,1,0:T(8,128)S(1)} %get-tuple-element.43), channel_id=1, source_target_pairs={{1,2},{3,4},{5,6},{2,1},{4,3},{6,5},{9,10},{11,12},{13,14},{10,9},... | collective-permute-start | bytes 393224 | tf_op jit(solution)/shard_map/ppermute | solution.py:52
  2.5 13.0 %collective-permute-start.1 = (f32[4,64,128]{2,1,0:T(8,128)S(1)}, f32[4,64,128]{2,1,0:T(8,128)S(1)}, u32[]{:S(2)}, u32[]{:S(2)}) collective-permute-start(f32[4,64,128]{2,1,0:T(8,128)S(1)} %get-tuple-element.44), channel_id=1, source_target_pairs={{0,1},{2,3},{4,5},{6,7},{1,0},{3,2},{5,4},{7,6},{8,9},{10,11},{12,... | collective-permute-start | bytes 393224 | tf_op jit(solution)/shard_map/ppermute | solution.py:52
  7.1 13.5 %collective-permute-start.2 = (f32[4,64,128]{2,1,0:T(8,128)S(1)}, f32[4,64,128]{2,1,0:T(8,128)S(1)}, u32[]{:S(2)}, u32[]{:S(2)}) collective-permute-start(f32[4,64,128]{2,1,0:T(8,128)S(1)} %get-tuple-element.47), channel_id=1, source_target_pairs={{1,2},{3,4},{5,6},{2,1},{4,3},{6,5},{9,10},{11,12},{13,14},{10,9},... | collective-permute-start | bytes 393224 | tf_op jit(solution)/shard_map/ppermute | solution.py:52
  7.7 12.9 %collective-permute-start.3 = (f32[4,64,128]{2,1,0:T(8,128)S(1)}, f32[4,64,128]{2,1,0:T(8,128)S(1)}, u32[]{:S(2)}, u32[]{:S(2)}) collective-permute-start(f32[4,64,128]{2,1,0:T(8,128)S(1)} %get-tuple-element.48), channel_id=1, source_target_pairs={{0,1},{2,3},{4,5},{6,7},{1,0},{3,2},{5,4},{7,6},{8,9},{10,11},{12,... | collective-permute-start | bytes 393224 | tf_op jit(solution)/shard_map/ppermute | solution.py:52
  15.6 9.1 %collective-permute-start.4 = (f32[4,3,64,128]{3,2,1,0:T(8,128)S(1)}, f32[4,3,64,128]{3,2,1,0:T(8,128)S(1)}, u32[]{:S(2)}, u32[]{:S(2)}) collective-permute-start(f32[4,3,64,128]{3,2,1,0:T(8,128)S(1)} %get-tuple-element.49), channel_id=1, source_target_pairs={{8,16},{16,8},{9,17},{17,9},{10,18},{18,10},{11,19},{19,11},{12,20... | collective-permute-start | bytes 1179656 | tf_op jit(solution)/shard_map/ppermute | solution.py:52
  19.2 5.5 %collective-permute-start.5 = (f32[4,3,64,128]{3,2,1,0:T(8,128)S(1)}, f32[4,3,64,128]{3,2,1,0:T(8,128)S(1)}, u32[]{:S(2)}, u32[]{:S(2)}) collective-permute-start(f32[4,3,64,128]{3,2,1,0:T(8,128)S(1)} %get-tuple-element.50), channel_id=1, source_target_pairs={{0,8},{16,24},{8,0},{24,16},{1,9},{17,25},{9,1},{25,17},{2,10},{18... | collective-permute-start | bytes 1179656 | tf_op jit(solution)/shard_map/ppermute | solution.py:52
  35.3 9.1 %collective-permute-start.6 = (f32[4,3,64,128]{3,2,1,0:T(8,128)S(1)}, f32[4,3,64,128]{3,2,1,0:T(8,128)S(1)}, u32[]{:S(2)}, u32[]{:S(2)}) collective-permute-start(f32[4,3,64,128]{3,2,1,0:T(8,128)S(1)} %get-tuple-element.53), channel_id=1, source_target_pairs={{8,16},{16,8},{9,17},{17,9},{10,18},{18,10},{11,19},{19,11},{12,20... | collective-permute-start | bytes 1179656 | tf_op jit(solution)/shard_map/ppermute | solution.py:52
  37.2 7.2 %collective-permute-start.7 = (f32[4,3,64,128]{3,2,1,0:T(8,128)S(1)}, f32[4,3,64,128]{3,2,1,0:T(8,128)S(1)}, u32[]{:S(2)}, u32[]{:S(2)}) collective-permute-start(f32[4,3,64,128]{3,2,1,0:T(8,128)S(1)} %get-tuple-element.54), channel_id=1, source_target_pairs={{0,8},{16,24},{8,0},{24,16},{1,9},{17,25},{9,1},{25,17},{2,10},{18... | collective-permute-start | bytes 1179656 | tf_op jit(solution)/shard_map/ppermute | solution.py:52
  44.5 4.5 %collective-permute-start.8 = (f32[4,128,128]{2,1,0:T(8,128)S(1)}, f32[4,128,128]{2,1,0:T(8,128)S(1)}, u32[]{:S(2)}, u32[]{:S(2)}) collective-permute-start(f32[4,128,128]{2,1,0:T(8,128)S(1)} %get-tuple-element.56), channel_id=1, source_target_pairs={{1,2},{3,4},{5,6},{2,1},{4,3},{6,5},{9,10},{11,12},{13,14},{10,9},... | collective-permute-start | bytes 786440 | tf_op jit(solution)/shard_map/ppermute | solution.py:52
  45.2 10.4 %collective-permute-start.9 = (f32[4,128,128]{2,1,0:T(8,128)S(1)}, f32[4,128,128]{2,1,0:T(8,128)S(1)}, u32[]{:S(2)}, u32[]{:S(2)}) collective-permute-start(f32[4,128,128]{2,1,0:T(8,128)S(1)} %get-tuple-element.57), channel_id=1, source_target_pairs={{0,1},{2,3},{4,5},{6,7},{1,0},{3,2},{5,4},{7,6},{8,9},{10,11},{12,... | collective-permute-start | bytes 786440 | tf_op jit(solution)/shard_map/ppermute | solution.py:52
  55.8 19.8 %collective-permute-start.12 = (f32[4,3,64,128]{3,2,1,0:T(8,128)S(1)}, f32[4,3,64,128]{3,2,1,0:T(8,128)S(1)}, u32[]{:S(2)}, u32[]{:S(2)}) collective-permute-start(f32[4,3,64,128]{3,2,1,0:T(8,128)S(1)} %get-tuple-element.65), channel_id=1, source_target_pairs={{8,16},{16,8},{9,17},{17,9},{10,18},{18,10},{11,19},{19,11},{12,20... | collective-permute-start | bytes 1179656 | tf_op jit(solution)/shard_map/ppermute | solution.py:52
  58.9 16.7 %collective-permute-start.13 = (f32[4,3,64,128]{3,2,1,0:T(8,128)S(1)}, f32[4,3,64,128]{3,2,1,0:T(8,128)S(1)}, u32[]{:S(2)}, u32[]{:S(2)}) collective-permute-start(f32[4,3,64,128]{3,2,1,0:T(8,128)S(1)} %get-tuple-element.66), channel_id=1, source_target_pairs={{0,8},{16,24},{8,0},{24,16},{1,9},{17,25},{9,1},{25,17},{2,10},{18... | collective-permute-start | bytes 1179656 | tf_op jit(solution)/shard_map/ppermute | solution.py:52
  58.9 5.0 %collective-permute-start.10 = (f32[4,128,128]{2,1,0:T(8,128)S(1)}, f32[4,128,128]{2,1,0:T(8,128)S(1)}, u32[]{:S(2)}, u32[]{:S(2)}) collective-permute-start(f32[4,128,128]{2,1,0:T(8,128)S(1)} %get-tuple-element.63), channel_id=1, source_target_pairs={{1,2},{3,4},{5,6},{2,1},{4,3},{6,5},{9,10},{11,12},{13,14},{10,9},... | collective-permute-start | bytes 786440 | tf_op jit(solution)/shard_map/ppermute | solution.py:52
  59.6 16.0 %collective-permute-start.11 = (f32[4,128,128]{2,1,0:T(8,128)S(1)}, f32[4,128,128]{2,1,0:T(8,128)S(1)}, u32[]{:S(2)}, u32[]{:S(2)}) collective-permute-start(f32[4,128,128]{2,1,0:T(8,128)S(1)} %get-tuple-element.64), channel_id=1, source_target_pairs={{0,1},{2,3},{4,5},{6,7},{1,0},{3,2},{5,4},{7,6},{8,9},{10,11},{12,... | collective-permute-start | bytes 786440 | tf_op jit(solution)/shard_map/ppermute | solution.py:52
  86.4 9.4 %collective-permute-start.14 = (f32[4,3,64,128]{3,2,1,0:T(8,128)S(1)}, f32[4,3,64,128]{3,2,1,0:T(8,128)S(1)}, u32[]{:S(2)}, u32[]{:S(2)}) collective-permute-start(f32[4,3,64,128]{3,2,1,0:T(8,128)S(1)} %get-tuple-element.69), channel_id=1, source_target_pairs={{8,16},{16,8},{9,17},{17,9},{10,18},{18,10},{11,19},{19,11},{12,20... | collective-permute-start | bytes 1179656 | tf_op jit(solution)/shard_map/ppermute | solution.py:52
  88.3 7.5 %collective-permute-start.15 = (f32[4,3,64,128]{3,2,1,0:T(8,128)S(1)}, f32[4,3,64,128]{3,2,1,0:T(8,128)S(1)}, u32[]{:S(2)}, u32[]{:S(2)}) collective-permute-start(f32[4,3,64,128]{3,2,1,0:T(8,128)S(1)} %get-tuple-element.70), channel_id=1, source_target_pairs={{0,8},{16,24},{8,0},{24,16},{1,9},{17,25},{9,1},{25,17},{2,10},{18... | collective-permute-start | bytes 1179656 | tf_op jit(solution)/shard_map/ppermute | solution.py:52
  88.4 13.5 %collective-permute-start.16 = (f32[4,64,128]{2,1,0:T(8,128)S(1)}, f32[4,64,128]{2,1,0:T(8,128)S(1)}, u32[]{:S(2)}, u32[]{:S(2)}) collective-permute-start(f32[4,64,128]{2,1,0:T(8,128)S(1)} %get-tuple-element.75), channel_id=1, source_target_pairs={{1,2},{3,4},{5,6},{2,1},{4,3},{6,5},{9,10},{11,12},{13,14},{10,9},... | collective-permute-start | bytes 393224 | tf_op jit(solution)/shard_map/ppermute | solution.py:52
  89.1 12.8 %collective-permute-start.17 = (f32[4,64,128]{2,1,0:T(8,128)S(1)}, f32[4,64,128]{2,1,0:T(8,128)S(1)}, u32[]{:S(2)}, u32[]{:S(2)}) collective-permute-start(f32[4,64,128]{2,1,0:T(8,128)S(1)} %get-tuple-element.76), channel_id=1, source_target_pairs={{0,1},{2,3},{4,5},{6,7},{1,0},{3,2},{5,4},{7,6},{8,9},{10,11},{12,... | collective-permute-start | bytes 393224 | tf_op jit(solution)/shard_map/ppermute | solution.py:52
  96.0 5.9 %collective-permute-start.18 = (f32[4,64,128]{2,1,0:T(8,128)S(1)}, f32[4,64,128]{2,1,0:T(8,128)S(1)}, u32[]{:S(2)}, u32[]{:S(2)}) collective-permute-start(f32[4,64,128]{2,1,0:T(8,128)S(1)} %get-tuple-element.77), channel_id=1, source_target_pairs={{1,2},{3,4},{5,6},{2,1},{4,3},{6,5},{9,10},{11,12},{13,14},{10,9},... | collective-permute-start | bytes 393224 | tf_op jit(solution)/shard_map/ppermute | solution.py:52
  96.7 10.3 %collective-permute-start.19 = (f32[4,64,128]{2,1,0:T(8,128)S(1)}, f32[4,64,128]{2,1,0:T(8,128)S(1)}, u32[]{:S(2)}, u32[]{:S(2)}) collective-permute-start(f32[4,64,128]{2,1,0:T(8,128)S(1)} %get-tuple-element.78), channel_id=1, source_target_pairs={{0,1},{2,3},{4,5},{6,7},{1,0},{3,2},{5,4},{7,6},{8,9},{10,11},{12,... | collective-permute-start | bytes 393224 | tf_op jit(solution)/shard_map/ppermute | solution.py:52

commit v6 on v5

--- a/solution.py
+++ b/solution.py
@@ -92,7 +92,9 @@
     return ((slice(0, rim), slice(rows - rim, rows)), (slice(rim, half), slice(half, rows - rim)))
 
 
-def pack_kernel(object_ref, turned_ref, odd_edge, even_edge, odd_mid, even_mid):
+def pack_kernel(
+    object_ref, turned_ref, odd_edge, even_edge, odd_mid, even_mid, row_odd, row_even
+):
     planes, rows, cols = object_ref.shape
     tiles = cols // LANES
     pieces = segments(rows, odd_edge.shape[1])
@@ -110,40 +112,38 @@
             odd_ref[plane], even_ref[plane] = paired("col", left, right)
     for plane in range(planes):
         for tile in range(tiles):
-            turned_ref[plane, tile] = swap_halves(
-                object_ref[plane, :, tile * LANES : (tile + 1) * LANES]
-            )
-
-
-def lay(turned_ref, plane, rows, left, right, put):
+            turned = swap_halves(object_ref[plane, :, tile * LANES : (tile + 1) * LANES])
+            turned_ref[plane, tile] = turned
+            upper, lower = pieces[0]
+            row_odd[plane, tile], row_even[plane, tile] = paired("row", turned[upper], turned[lower])
+
+
+def lay(turned_ref, plane, rows, left, right, field_ref, row_at):
     tiles = turned_ref.shape[1]
     parts = [left] + [turned_ref[plane, tile, rows, :] for tile in range(tiles)] + [right]
     for block in range(tiles + 1):
-        put(block, blend(parts[block], parts[block + 1]))
-
-
-def load_kernel(source_hbm, target_ref, sem):
-    copy = pltpu.make_async_copy(source_hbm, target_ref, sem)
-    copy.start()
-    copy.wait()
-
-
-def rows_kernel(turned_ref, from_odd, from_even, up_ref, down_ref, odd_ref, even_ref):
-    planes, _, rows, _ = turned_ref.shape
-    rim = up_ref.shape[2]
-    (upper, lower), _ = segments(rows, rim)
-    for plane in range(planes):
-
-        def put_up(block, values):
-            up_ref[plane, block] = values
-
-        def put_down(block, values):
-            down_ref[plane, block] = values
-
+        field_ref[plane, block, row_at : row_at + rows.stop - rows.start, :] = blend(
+            parts[block], parts[block + 1]
+        )
+
+
+def load_kernel(*refs):
+    count = len(refs) // 3
+    copies = [
+        pltpu.make_async_copy(refs[k], refs[count + k], refs[2 * count + k]) for k in range(count)
+    ]
+    for copy in copies:
+        copy.start()
+    for copy in copies:
+        copy.wait()
+
+
+def corner_kernel(from_odd, from_even, odd_ref, even_ref):
+    for plane in range(odd_ref.shape[0]):
         left, right = paired("col", from_odd[plane], from_even[plane])
-        lay(turned_ref, plane, upper, left, right, put_up)
-        lay(turned_ref, plane, lower, swap_halves(left), swap_halves(right), put_down)
-    odd_ref[...], even_ref[...] = paired("row", up_ref[...], down_ref[...])
+        odd_ref[plane], even_ref[plane] = paired(
+            "row", blend(left, right), swap_halves(blend(right, left))
+        )
 
 
 def gradients(pos_ref, amps_ref, probe_ref, tables_ref, field_ref, grad_ref, work):
@@ -252,16 +252,32 @@
     lax.fori_loop(0, (count + GROUP - 1) // GROUP, group_step, 0)
 
 
+def outer(blocks):
+    return (0, blocks - 1)
+
+
+def inner(blocks):
+    return range(1, blocks - 1)
+
+
 def write_grad(grad_ref, pieces):
-    row_odd, row_even, edges, left, mid, right, band_odd, band_even = pieces
+    (
+        row_odd, row_even, row_mid_odd, row_mid_even, edges, edges_mid, left, mid, right,
+        band_odd, band_even,
+    ) = pieces
     _, blocks, all_rows, _ = grad_ref.shape
     rim = row_odd.shape[2]
     rows = all_rows - 2 * rim
-    row_odd[...], row_even[...] = paired(
-        "row", grad_ref[:, :, 0:rim, :], grad_ref[:, :, rim + rows : all_rows, :]
-    )
-    edges[:, :, 0:rim, :] = grad_ref[:, :, rim : 2 * rim, :]
-    edges[:, :, rim : 2 * rim, :] = grad_ref[:, :, rows : rim + rows, :]
+    for odd, even, edge, group in (
+        (row_odd, row_even, edges, outer(blocks)),
+        (row_mid_odd, row_mid_even, edges_mid, inner(blocks)),
+    ):
+        for at, block in enumerate(group):
+            odd[:, at], even[:, at] = paired(
+                "row", grad_ref[:, block, 0:rim, :], grad_ref[:, block, rim + rows : all_rows, :]
+            )
+            edge[:, at, 0:rim, :] = grad_ref[:, block, rim : 2 * rim, :]
+            edge[:, at, rim : 2 * rim, :] = grad_ref[:, block, rows : rim + rows, :]
     left[...] = grad_ref[:, 0, 2 * rim : rows, :]
     mid[...] = grad_ref[:, 1 : blocks - 1, 2 * rim : rows, :]
     right[...] = grad_ref[:, blocks - 1, 2 * rim : rows, :]
@@ -284,73 +300,75 @@
 
 
 def first_kernel(
-    pos_ref, turned_ref, up_ref, down_ref, from_odd, from_even, row_odd, row_even,
-    amps_ref, probe_ref, tables_ref, field_ref, *rest,
+    pos_ref, turned_ref, edge_odd, edge_even, mid_odd, mid_even, row_odd, row_even,
+    corner_odd, corner_even, amps_ref, probe_ref, tables_ref, field_ref, *rest,
 ):
     pieces, (grad_ref, *work) = rest[:-5], rest[-5:]
     planes, _, rows, _ = turned_ref.shape
-    rim = up_ref.shape[2]
-    _, (upper, lower) = segments(rows, rim)
-    field_ref[:, :, 0:rim, :], field_ref[:, :, rows + rim : rows + 2 * rim, :] = paired(
-        "row", row_odd[...], row_even[...]
-    )
-    field_ref[:, :, rim : 2 * rim, :] = up_ref[...]
-    field_ref[:, :, rows : rows + rim, :] = down_ref[...]
+    rim = edge_odd.shape[1]
     for plane in range(planes):
-
-        def put_upper(block, values):
-            field_ref[plane, block, rim + upper.start : rim + upper.stop, :] = values
-
-        def put_lower(block, values):
-            field_ref[plane, block, rim + lower.start : rim + lower.stop, :] = values
-
-        left, right = paired("col", from_odd[plane], from_even[plane])
-        lay(turned_ref, plane, upper, left, right, put_upper)
-        lay(turned_ref, plane, lower, swap_halves(left), swap_halves(right), put_lower)
+        for (upper, lower), odd, even in zip(
+            segments(rows, rim), (edge_odd, mid_odd), (edge_even, mid_even)
+        ):
+            left, right = paired("col", odd[plane], even[plane])
+            lay(turned_ref, plane, upper, left, right, field_ref, rim + upper.start)
+            left, right = swap_halves(left), swap_halves(right)
+            lay(turned_ref, plane, lower, left, right, field_ref, rim + lower.start)
+        corners = paired("row", corner_odd[plane], corner_even[plane])
+        rims = paired("row", row_odd[plane], row_even[plane])
+        for strip, corner, row_at in zip(rims, corners, (0, rows + rim)):
+            parts = [corner, *strip, corner]
+            for block in range(len(parts) - 1):
+                field_ref[plane, block, row_at : row_at + rim, :] = blend(
+                    parts[block], parts[block + 1]
+                )
     gradients(pos_ref, amps_ref, probe_ref, tables_ref, field_ref, grad_ref, work)
     write_grad(grad_ref, pieces)
 
 
-def folded(edges, row_odd, row_even, plane, block):
+def fold(edges, row_odd, row_even, plane, at):
     rim = row_odd.shape[2]
-    from_up, from_down = paired("row", row_odd[plane, block], row_even[plane, block])
-    return (
-        edges[plane, block, 0:rim, :] + from_up, edges[plane, block, rim : 2 * rim, :] + from_down
-    )
+    from_up, from_down = paired("row", row_odd[plane, at], row_even[plane, at])
+    return edges[plane, at, 0:rim, :] + from_up, edges[plane, at, rim : 2 * rim, :] + from_down
 
 
 def fold_kernel(edges, row_odd, row_even, folded_ref, odd_ref, even_ref):
-    planes, blocks = edges.shape[:2]
+    planes, count = edges.shape[:2]
     rim = row_odd.shape[2]
     for plane in range(planes):
-        for block in range(blocks):
-            upper, lower = folded(edges, row_odd, row_even, plane, block)
-            folded_ref[plane, block, 0:rim, :] = upper
-            folded_ref[plane, block, rim : 2 * rim, :] = lower
+        for at in range(count):
+            upper, lower = fold(edges, row_odd, row_even, plane, at)
+            folded_ref[plane, at, 0:rim, :] = upper
+            folded_ref[plane, at, rim : 2 * rim, :] = lower
     if odd_ref.shape[1] == 2 * rim:
-        odd_ref[...], even_ref[...] = paired("col", folded_ref[:, 0], folded_ref[:, blocks - 1])
+        odd_ref[...], even_ref[...] = paired("col", folded_ref[:, 0], folded_ref[:, count - 1])
     else:
         pack_bands(folded_ref, (odd_ref, even_ref), slice(0, rim), slice(rim, 2 * rim))
 
 
+def fold_mid_kernel(edges, row_odd, row_even, up_ref, down_ref, odd_ref, even_ref):
+    for plane in range(edges.shape[0]):
+        for at in range(edges.shape[1]):
+            upper, lower = fold(edges, row_odd, row_even, plane, at)
+            up_ref[plane, at], down_ref[plane, at] = upper, lower
+            odd_ref[plane, at], even_ref[plane, at] = paired("row", upper, lower)
+
+
 def total_kernel(folded_ref, from_odd, from_even, up_ref, down_ref, odd_ref, even_ref):
-    planes, blocks, rim, _ = up_ref.shape
+    planes, count, rim, _ = up_ref.shape
     for plane in range(planes):
-        left, right = paired("col", from_odd[plane], from_even[plane])
-        for block in range(blocks):
-            values = folded_ref[plane, block]
-            if block == 0:
-                values += left
-            if block == blocks - 1:
-                values += right
-            up_ref[plane, block] = values[0:rim]
-            down_ref[plane, block] = values[rim : 2 * rim]
-    odd_ref[...], even_ref[...] = paired("row", up_ref[...], down_ref[...])
+        sides = paired("col", from_odd[plane], from_even[plane])
+        for at in range(count):
+            values = folded_ref[plane, at] + sides[at]
+            upper, lower = values[0:rim], values[rim : 2 * rim]
+            up_ref[plane, at], down_ref[plane, at] = upper, lower
+            odd_ref[plane, at], even_ref[plane, at] = paired("row", upper, lower)
 
 
 def next_kernel(
-    pos_ref, old_ref, up_ref, down_ref, left_ref, mid_ref, right_ref,
-    from_odd, from_even, row_odd, row_even, amps_ref, probe_ref, tables_ref, field_ref, *rest,
+    pos_ref, old_ref, up_ref, down_ref, up_mid, down_mid, left_ref, mid_ref, right_ref,
+    from_odd, from_even, row_odd, row_even, row_mid_odd, row_mid_even,
+    amps_ref, probe_ref, tables_ref, field_ref, *rest,
 ):
     pieces, (grad_ref, *work) = rest[:-5], rest[-5:]
     _, blocks, all_rows, _ = old_ref.shape
@@ -359,20 +377,24 @@
     from_left, from_right = paired("col", from_odd[...], from_even[...])
     for block in range(blocks):
         lane = lane_ids((1, 1, LANES))
-        from_up, from_down = paired("row", row_odd[:, block], row_even[:, block])
         inside = lane >= 0
-        middle = mid_ref[:, block - 1] if 0 < block < blocks - 1 else None
-        if block == 0:
+        if block in inner(blocks):
+            at, odd, even, up, down = block - 1, row_mid_odd, row_mid_even, up_mid, down_mid
+            middle = mid_ref[:, at]
+        elif block == 0:
+            at, odd, even, up, down = 0, row_odd, row_even, up_ref, down_ref
             inside = lane >= pos_ref[2, 1] * (LANES // 2)
             middle = left_ref[...] + from_left
-        if block == blocks - 1:
+        else:
+            at, odd, even, up, down = 1, row_odd, row_even, up_ref, down_ref
             inside = lane < LANES - pos_ref[2, 2] * (LANES // 2)
             middle = right_ref[...] + from_right
+        from_up, from_down = paired("row", odd[:, at], even[:, at])
         for lo, hi, values in (
             (0, rim, from_up),
-            (rim, 2 * rim, up_ref[:, block]),
+            (rim, 2 * rim, up[:, at]),
             (2 * rim, rows, middle),
-            (rows, rows + rim, down_ref[:, block]),
+            (rows, rows + rim, down[:, at]),
             (rows + rim, all_rows, from_down),
         ):
             updated = old_ref[:, block, lo:hi, :] - values
@@ -382,7 +404,7 @@
 
 
 def finish_kernel(
-    field_ref, edges, left_ref, mid_ref, right_ref,
+    field_ref, edges, edges_mid, row_odd, row_even, left_ref, mid_ref, right_ref,
     mid_odd, mid_even, edge_odd, edge_even, out_ref,
 ):
     planes, blocks, _, _ = field_ref.shape
@@ -394,13 +416,14 @@
     def whole(plane, part, edge):
         size = rim if edge else half
         at = slice(part * size, (part + 1) * size)
-        values = [
-            edges[plane, block, at, :] if edge
-            else left_ref[plane, at, :] if block == 0
-            else right_ref[plane, at, :] if block == blocks - 1
-            else mid_ref[plane, block - 1, at, :]
-            for block in range(blocks)
-        ]
+        if edge:
+            values = [edges[plane, 0, at, :], edges[plane, 1, at, :]]
+            values[1:1] = [
+                fold(edges_mid, row_odd, row_even, plane, k)[part] for k in range(blocks - 2)
+            ]
+        else:
+            values = [left_ref[plane, at, :], right_ref[plane, at, :]]
+            values[1:1] = [mid_ref[plane, k, at, :] for k in range(blocks - 2)]
         odd, even = (edge_odd, edge_even) if edge else (mid_odd, mid_even)
         extras = paired("col", odd[plane], even[plane])
         if part == 1:
@@ -476,65 +499,80 @@
 
         return run
 
-    strip = f32(planes, blocks, rim, LANES)
     packed_edge = f32(planes, rim, LANES)
     packed_mid = f32(planes, band // 2, LANES)
-    packed_both = [packed_edge] * 2
-    turned, odd_edge, even_edge, odd_mid, even_mid = call(
+    row_strip = f32(planes, blocks - 1, rim, LANES)
+    turned, odd_edge, even_edge, odd_mid, even_mid, odd, even = call(
         pack_kernel,
-        [f32(planes, blocks - 1, tile_r, LANES)] + packed_both + [packed_mid] * 2,
+        [f32(planes, blocks - 1, tile_r, LANES)]
+        + [packed_edge] * 2 + [packed_mid] * 2 + [row_strip] * 2,
         4,
     )(tile)
     edge_strips = exchange(odd_edge, even_edge, "col")
+    row_strips = exchange(odd, even, "row")
     mid_strips = exchange(odd_mid, even_mid, "col")
-    up, down, odd, even = call(rows_kernel, [strip] * 4, 4)(turned, *edge_strips)
-    (tables,) = call(
+    constants = (tables, amps, probe)
+    tables, amps, probe = call(
         load_kernel,
-        [pltpu.VMEM(tables.shape, tables.dtype)],
+        [pltpu.VMEM(array.shape, array.dtype) for array in constants],
         4,
-        scratch=[pltpu.SemaphoreType.DMA(())],
-        raw=[tables],
+        scratch=[pltpu.SemaphoreType.DMA(())] * len(constants),
+        raw=constants,
     )()
-    row_strips = exchange(odd, even, "row")
+    odd, even = call(corner_kernel, [packed_edge] * 2, 4)(*edge_strips)
+    corner_strips = exchange(odd, even, "row")
 
     field_shape = f32(planes, blocks, tile_r + frame, LANES)
     work = [field_shape] + [pltpu.VMEM((GROUP, 2, frame, frame), jnp.float32)] * 4
-    edge_rows = f32(planes, blocks, 2 * rim, LANES)
-    pieces = [
-        strip,
-        strip,
+    strip, strip_mid = f32(planes, 2, rim, LANES), f32(planes, blocks - 2, rim, LANES)
+    edge_rows = f32(planes, 2, 2 * rim, LANES)
+    band_rows = f32(planes, band, LANES)
+    pieces = [strip] * 2 + [strip_mid] * 2 + [
         edge_rows,
-        f32(planes, band, LANES),
+        f32(planes, blocks - 2, 2 * rim, LANES),
+        band_rows,
         f32(planes, blocks - 2, band, LANES),
-        f32(planes, band, LANES),
+        band_rows,
     ]
     field, *grads = call(
-        first_kernel, [field_shape] + pieces + [f32(planes, band, LANES)] * 2, 20,
-        scratch=work, scalars=[pos],
-    )(turned, up, down, *mid_strips, *row_strips, amps, probe, tables)
+        first_kernel,
+        [field_shape] + pieces + [band_rows] * 2,
+        20,
+        scratch=work,
+        scalars=[pos],
+    )(turned, *edge_strips, *mid_strips, *row_strips, *corner_strips, amps, probe, tables)
 
     for iteration in range(1, ITERS):
-        odd, even, edges, left, mid, right, band_odd, band_even = grads
+        odd, even, odd_in, even_in, edges, edges_mid, left, mid, right, band_odd, band_even = grads
         row_strips = exchange(odd, even, "row")
         mid_strips = exchange(band_odd, band_even, "col")
+        inner_strips = exchange(odd_in, even_in, "row")
         edges, odd, even = call(
             fold_kernel, [edge_rows] + [f32(planes, 2 * rim, LANES)] * 2, 4
         )(edges, *row_strips)
         edge_strips = exchange(odd, even, "col")
+        up_mid, down_mid, odd_in, even_in = call(fold_mid_kernel, [strip_mid] * 4, 4)(
+            edges_mid, *inner_strips
+        )
+        inner_strips = exchange(odd_in, even_in, "row")
         up, down, odd, even = call(total_kernel, [strip] * 4, 4)(edges, *edge_strips)
         row_strips = exchange(odd, even, "row")
-        bands = [f32(planes, band, LANES)] * 2 if iteration < ITERS - 1 else [packed_mid] * 2
+        bands = [band_rows] * 2 if iteration < ITERS - 1 else [packed_mid] * 2
         field, *grads = call(
             next_kernel, [field_shape] + pieces + bands, 20, scratch=work, scalars=[pos]
-        )(field, up, down, left, mid, right, *mid_strips, *row_strips, amps, probe, tables)
-
-    odd, even, edges, left, mid, right, band_odd, band_even = grads
+        )(
+            field, up, down, up_mid, down_mid, left, mid, right,
+            *mid_strips, *row_strips, *inner_strips, amps, probe, tables,
+        )
+
+    odd, even, odd_in, even_in, edges, edges_mid, left, mid, right, band_odd, band_even = grads
     row_strips = exchange(odd, even, "row")
     mid_strips = exchange(band_odd, band_even, "col")
-    edges, odd, even = call(fold_kernel, [edge_rows] + packed_both, 4)(edges, *row_strips)
+    inner_strips = exchange(odd_in, even_in, "row")
+    edges, odd, even = call(fold_kernel, [edge_rows] + [packed_edge] * 2, 4)(edges, *row_strips)
     edge_strips = exchange(odd, even, "col")
     (out,) = call(finish_kernel, [jax.ShapeDtypeStruct((planes, tile_r, tile_c), jnp.float32)], 8)(
-        field, edges, left, mid, right, *mid_strips, *edge_strips
+        field, edges, edges_mid, *inner_strips, left, mid, right, *mid_strips, *edge_strips
     )
     return out.reshape(object_slices.shape)
 

time: 111 us -> 104 us (0.937)
  the two profiles are of different devices: /device:TPU:1 before, /device:TPU:21 now
where the time goes in v6:
time: 104 us
  starting transfers between devices  49.2 us (47%)
  Pallas kernels  26 us (25%)
  waiting for transfers between devices  25.7 us (25%)
  local copies, waits for them, and re-layouts  1.23 us (1%)
    ppermute x28, starting transfers between devices, exchange(): received.append(lax.ppermute(values, axis, pairs))  49.2 us
    pallas_call x10, Pallas kernels, run(): pl.pallas_call(kernel, out_shape=outs, in_specs=[smem()] * len(scalars) +...  26 us
    ppermute x28, waiting for transfers between devices, exchange(): received.append(lax.ppermute(values, axis, pairs))  25.7 us
  transfers between devices with their start and end apart: 28, of which 10 were waited for; matrix products, arithmetic and copies ran while one was open for 1% of the time, Pallas kernels for 2%

profile of v6, /device:TPU:21, one launch (start us, length us, event | category | flops | bytes accessed | tf_op | source)
XLA Modules:
  0.0 103.9 jit_solution(16284322516790659919)
XLA Ops:
  1.7 3.1 %collective-permute-start = (f32[4,64,128]{2,1,0:T(8,128)S(1)}, f32[4,64,128]{2,1,0:T(8,128)S(1)}, u32[]{:S(2)}, u32[]{:S(2)}) collective-permute-start(f32[4,64,128]{2,1,0:T(8,128)S(1)} %get-tuple-element.56), channel_id=1, source_target_pairs={{1,2},{3,4},{5,6},{2,1},{4,3},{6,5},{9,10},{11,12},{13,14},{10,9},... | collective-permute-start | bytes 393224 | tf_op jit(solution)/shard_map/ppermute | solution.py:52
  5.0 2.9 %collective-permute-start.2 = (f32[4,64,128]{2,1,0:T(8,128)S(1)}, f32[4,64,128]{2,1,0:T(8,128)S(1)}, u32[]{:S(2)}, u32[]{:S(2)}) collective-permute-start(f32[4,64,128]{2,1,0:T(8,128)S(1)} %get-tuple-element.58), channel_id=1, source_target_pairs={{1,2},{3,4},{5,6},{2,1},{4,3},{6,5},{9,10},{11,12},{13,14},{10,9},... | collective-permute-start | bytes 393224 | tf_op jit(solution)/shard_map/ppermute | solution.py:52
  8.0 4.2 %collective-permute-start.4 = (f32[4,2,64,128]{3,2,1,0:T(8,128)S(1)}, f32[4,2,64,128]{3,2,1,0:T(8,128)S(1)}, u32[]{:S(2)}, u32[]{:S(2)}) collective-permute-start(f32[4,2,64,128]{3,2,1,0:T(8,128)S(1)} %get-tuple-element.60), channel_id=1, source_target_pairs={{8,16},{16,8},{9,17},{17,9},{10,18},{18,10},{11,19},{19,11},{12,20... | collective-permute-start | bytes 786440 | tf_op jit(solution)/shard_map/ppermute | solution.py:52
  15.6 3.6 %collective-permute-start.6 = (f32[4,64,128]{2,1,0:T(8,128)S(1)}, f32[4,64,128]{2,1,0:T(8,128)S(1)}, u32[]{:S(2)}, u32[]{:S(2)}) collective-permute-start(f32[4,64,128]{2,1,0:T(8,128)S(1)} %get-tuple-element.62), channel_id=1, source_target_pairs={{8,16},{16,8},{9,17},{17,9},{10,18},{18,10},{11,19},{19,11},{12,20... | collective-permute-start | bytes 393224 | tf_op jit(solution)/shard_map/ppermute | solution.py:52
  19.3 1.6 %shard_map.66 = (bf16[8,256,256]{2,1,0:T(8,128)(2,1)S(1)}, f32[16,128,128]{2,1,0:T(8,128)S(1)}, f32[2,128,128]{2,1,0:T(8,128)S(1)}) custom-call(bf16[8,256,256]{2,1,0:T(8,128)(2,1)} %constant.16.clone.refs_0_, f32[16,128,128]{2,1,0:T(8,128)} %bitcast.14, f32[2,128,128]{2,1,0:T(8,128)} %refs_2_.1), custom_call_target="tpu_custom_call" | custom-call | tf_op jit(solution)/shard_map/pallas_call | solution.py:486
  21.9 10.5 %shard_map.67 = (f32[4,3,384,128]{3,2,1,0:T(8,128)S(1)}, f32[4,2,64,128]{3,2,1,0:T(8,128)S(1)}, f32[4,2,64,128]{3,2,1,0:T(8,128)S(1)}, f32[4,1,64,128]{3,2,1,0:T...) custom-call(s32[3,16]{1,0:T(4,128)S(1)} %pad_add_fusion.pos_ref, ...), custom_call_target="tpu_custom_call" | custom-call | tf_op jit(solution)/shard_map/pallas_call | solution.py:486
  32.5 3.6 %collective-permute-start.8 = (f32[4,2,64,128]{3,2,1,0:T(8,128)S(1)}, f32[4,2,64,128]{3,2,1,0:T(8,128)S(1)}, u32[]{:S(2)}, u32[]{:S(2)}) collective-permute-start(f32[4,2,64,128]{3,2,1,0:T(8,128)S(1)} %get-tuple-element.69), channel_id=1, source_target_pairs={{8,16},{16,8},{9,17},{17,9},{10,18},{18,10},{11,19},{19,11},{12,20... | collective-permute-start | bytes 786440 | tf_op jit(solution)/shard_map/ppermute | solution.py:52
  36.2 4.0 %collective-permute-done.8.row_odd = f32[4,2,64,128]{3,2,1,0:T(8,128)S(1)} collective-permute-done((f32[4,2,64,128]{3,2,1,0:T(8,128)S(1)}, f32[4,2,64,128]{3,2,1,0:T(8,128)S(1)}, u32[]{:S(2)}, u32[]{:S(2)}) %collective-permute-start.8) | collective-permute-done | bytes 262176 | tf_op jit(solution)/shard_map/ppermute | solution.py:52
  40.3 3.2 %collective-permute-start.10 = (f32[4,128,128]{2,1,0:T(8,128)S(1)}, f32[4,128,128]{2,1,0:T(8,128)S(1)}, u32[]{:S(2)}, u32[]{:S(2)}) collective-permute-start(f32[4,128,128]{2,1,0:T(8,128)S(1)} %get-tuple-element.72), channel_id=1, source_target_pairs={{1,2},{3,4},{5,6},{2,1},{4,3},{6,5},{9,10},{11,12},{13,14},{10,9},... | collective-permute-start | bytes 786440 | tf_op jit(solution)/shard_map/ppermute | solution.py:52
  43.6 3.8 %collective-permute-start.12 = (f32[4,1,64,128]{3,2,1,0:T(8,128)S(1)}, f32[4,1,64,128]{3,2,1,0:T(8,128)S(1)}, u32[]{:S(2)}, u32[]{:S(2)}) collective-permute-start(f32[4,1,64,128]{3,2,1,0:T(8,128)S(1)} %get-tuple-element.77), channel_id=1, source_target_pairs={{8,16},{16,8},{9,17},{17,9},{10,18},{18,10},{11,19},{19,11},{12,20... | collective-permute-start | bytes 393224 | tf_op jit(solution)/shard_map/ppermute | solution.py:52
  47.5 3.1 %collective-permute-start.14 = (f32[4,128,128]{2,1,0:T(8,128)S(1)}, f32[4,128,128]{2,1,0:T(8,128)S(1)}, u32[]{:S(2)}, u32[]{:S(2)}) collective-permute-start(f32[4,128,128]{2,1,0:T(8,128)S(1)} %get-tuple-element.84), channel_id=1, source_target_pairs={{1,2},{3,4},{5,6},{2,1},{4,3},{6,5},{9,10},{11,12},{13,14},{10,9},... | collective-permute-start | bytes 786440 | tf_op jit(solution)/shard_map/ppermute | solution.py:52
  50.6 1.5 %collective-permute-start.15 = (f32[4,128,128]{2,1,0:T(8,128)S(1)}, f32[4,128,128]{2,1,0:T(8,128)S(1)}, u32[]{:S(2)}, u32[]{:S(2)}) collective-permute-start(f32[4,128,128]{2,1,0:T(8,128)S(1)} %get-tuple-element.85), channel_id=1, source_target_pairs={{0,1},{2,3},{4,5},{6,7},{1,0},{3,2},{5,4},{7,6},{8,9},{10,11},{12,... | collective-permute-start | bytes 786440 | tf_op jit(solution)/shard_map/ppermute | solution.py:52
  52.1 3.6 %collective-permute-start.18 = (f32[4,1,64,128]{3,2,1,0:T(8,128)S(1)}, f32[4,1,64,128]{3,2,1,0:T(8,128)S(1)}, u32[]{:S(2)}, u32[]{:S(2)}) collective-permute-start(f32[4,1,64,128]{3,2,1,0:T(8,128)S(1)} %get-tuple-element.88), channel_id=1, source_target_pairs={{8,16},{16,8},{9,17},{17,9},{10,18},{18,10},{11,19},{19,11},{12,20... | collective-permute-start | bytes 393224 | tf_op jit(solution)/shard_map/ppermute | solution.py:52
  55.7 5.1 %collective-permute-done.11.from_even = f32[4,128,128]{2,1,0:T(8,128)S(1)} collective-permute-done((f32[4,128,128]{2,1,0:T(8,128)S(1)}, f32[4,128,128]{2,1,0:T(8,128)S(1)}, u32[]{:S(2)}, u32[]{:S(2)}) %collective-permute-start.11) | collective-permute-done | bytes 262176 | tf_op jit(solution)/shard_map/ppermute | solution.py:52
  61.0 2.5 %collective-permute-start.16 = (f32[4,2,64,128]{3,2,1,0:T(8,128)S(1)}, f32[4,2,64,128]{3,2,1,0:T(8,128)S(1)}, u32[]{:S(2)}, u32[]{:S(2)}) collective-permute-start(f32[4,2,64,128]{3,2,1,0:T(8,128)S(1)} %get-tuple-element.86), channel_id=1, source_target_pairs={{8,16},{16,8},{9,17},{17,9},{10,18},{18,10},{11,19},{19,11},{12,20... | collective-permute-start | bytes 786440 | tf_op jit(solution)/shard_map/ppermute | solution.py:52
  66.3 2.4 %collective-permute-done.16.row_odd = f32[4,2,64,128]{3,2,1,0:T(8,128)S(1)} collective-permute-done((f32[4,2,64,128]{3,2,1,0:T(8,128)S(1)}, f32[4,2,64,128]{3,2,1,0:T(8,128)S(1)}, u32[]{:S(2)}, u32[]{:S(2)}) %collective-permute-start.16) | collective-permute-done | bytes 262176 | tf_op jit(solution)/shard_map/ppermute | solution.py:52
  68.7 10.9 %shard_map.71 = (f32[4,3,384,128]{3,2,1,0:T(8,128)S(1)}, f32[4,2,64,128]{3,2,1,0:T(8,128)S(1)}, f32[4,2,64,128]{3,2,1,0:T(8,128)S(1)}, f32[4,1,64,128]{3,2,1,0:T...) custom-call(s32[3,16]{1,0:T(4,128)S(1)} %pad_add_fusion.pos_ref, ...), custom_call_target="tpu_custom_call" | custom-call | tf_op jit(solution)/shard_map/pallas_call | solution.py:486
  79.6 2.5 %collective-permute-start.20 = (f32[4,2,64,128]{3,2,1,0:T(8,128)S(1)}, f32[4,2,64,128]{3,2,1,0:T(8,128)S(1)}, u32[]{:S(2)}, u32[]{:S(2)}) collective-permute-start(f32[4,2,64,128]{3,2,1,0:T(8,128)S(1)} %get-tuple-element.92), channel_id=1, source_target_pairs={{8,16},{16,8},{9,17},{17,9},{10,18},{18,10},{11,19},{19,11},{12,20... | collective-permute-start | bytes 786440 | tf_op jit(solution)/shard_map/ppermute | solution.py:52
  82.1 3.1 %collective-permute-start.22 = (f32[4,1,64,128]{3,2,1,0:T(8,128)S(1)}, f32[4,1,64,128]{3,2,1,0:T(8,128)S(1)}, u32[]{:S(2)}, u32[]{:S(2)}) collective-permute-start(f32[4,1,64,128]{3,2,1,0:T(8,128)S(1)} %get-tuple-element.96), channel_id=1, source_target_pairs={{8,16},{16,8},{9,17},{17,9},{10,18},{18,10},{11,19},{19,11},{12,20... | collective-permute-start | bytes 393224 | tf_op jit(solution)/shard_map/ppermute | solution.py:52
  85.3 3.1 %collective-permute-start.24 = (f32[4,64,128]{2,1,0:T(8,128)S(1)}, f32[4,64,128]{2,1,0:T(8,128)S(1)}, u32[]{:S(2)}, u32[]{:S(2)}) collective-permute-start(f32[4,64,128]{2,1,0:T(8,128)S(1)} %get-tuple-element.101), channel_id=1, source_target_pairs={{1,2},{3,4},{5,6},{2,1},{4,3},{6,5},{9,10},{11,12},{13,14},{10,9},... | collective-permute-start | bytes 393224 | tf_op jit(solution)/shard_map/ppermute | solution.py:52
  88.7 3.0 %collective-permute-start.26 = (f32[4,64,128]{2,1,0:T(8,128)S(1)}, f32[4,64,128]{2,1,0:T(8,128)S(1)}, u32[]{:S(2)}, u32[]{:S(2)}) collective-permute-start(f32[4,64,128]{2,1,0:T(8,128)S(1)} %get-tuple-element.103), channel_id=1, source_target_pairs={{1,2},{3,4},{5,6},{2,1},{4,3},{6,5},{9,10},{11,12},{13,14},{10,9},... | collective-permute-start | bytes 393224 | tf_op jit(solution)/shard_map/ppermute | solution.py:52
  92.7 6.5 %collective-permute-done.25.mid_even = f32[4,64,128]{2,1,0:T(8,128)S(1)} collective-permute-done((f32[4,64,128]{2,1,0:T(8,128)S(1)}, f32[4,64,128]{2,1,0:T(8,128)S(1)}, u32[]{:S(2)}, u32[]{:S(2)}) %collective-permute-start.25) | collective-permute-done | bytes 131104 | tf_op jit(solution)/shard_map/ppermute | solution.py:52
  99.1 2.8 %collective-permute-done.27.edge_even = f32[4,64,128]{2,1,0:T(8,128)S(1)} collective-permute-done((f32[4,64,128]{2,1,0:T(8,128)S(1)}, f32[4,64,128]{2,1,0:T(8,128)S(1)}, u32[]{:S(2)}, u32[]{:S(2)}) %collective-permute-start.27) | collective-permute-done | bytes 131104 | tf_op jit(solution)/shard_map/ppermute | solution.py:52
  101.9 2.0 %shard_map.73 = f32[4,256,256]{2,1,0:T(8,128)} custom-call(f32[4,3,384,128]{3,2,1,0:T(8,128)S(1)} %get-tuple-element.90.field_ref, f32[4,2,128,128]{3,2,1,0:T(8,128)S(1)} %get-tuple-element.94.edges, f32[4,1,128,128]{3,2,1,0:T(8,128)S(1)} %get-tuple-element.95.edges_mid, f32[4,1,64,128]{3,2,1,0:T(8,128)S(1)} %collective-permute-done.22.row_odd, ...), custom_call_target="tpu_custom_call" | custom-call | tf_op jit(solution)/shard_map/pallas_call | solution.py:486
  (48 shorter events, 10.3 us)
Async XLA Ops:
  1.7 12.0 %collective-permute-start = (f32[4,64,128]{2,1,0:T(8,128)S(1)}, f32[4,64,128]{2,1,0:T(8,128)S(1)}, u32[]{:S(2)}, u32[]{:S(2)}) collective-permute-start(f32[4,64,128]{2,1,0:T(8,128)S(1)} %get-tuple-element.56), channel_id=1, source_target_pairs={{1,2},{3,4},{5,6},{2,1},{4,3},{6,5},{9,10},{11,12},{13,14},{10,9},... | collective-permute-start | bytes 393224 | tf_op jit(solution)/shard_map/ppermute | solution.py:52
  4.9 10.7 %collective-permute-start.1 = (f32[4,64,128]{2,1,0:T(8,128)S(1)}, f32[4,64,128]{2,1,0:T(8,128)S(1)}, u32[]{:S(2)}, u32[]{:S(2)}) collective-permute-start(f32[4,64,128]{2,1,0:T(8,128)S(1)} %get-tuple-element.57), channel_id=1, source_target_pairs={{0,1},{2,3},{4,5},{6,7},{1,0},{3,2},{5,4},{7,6},{8,9},{10,11},{12,... | collective-permute-start | bytes 393224 | tf_op jit(solution)/shard_map/ppermute | solution.py:52
  5.0 14.2 %collective-permute-start.2 = (f32[4,64,128]{2,1,0:T(8,128)S(1)}, f32[4,64,128]{2,1,0:T(8,128)S(1)}, u32[]{:S(2)}, u32[]{:S(2)}) collective-permute-start(f32[4,64,128]{2,1,0:T(8,128)S(1)} %get-tuple-element.58), channel_id=1, source_target_pairs={{1,2},{3,4},{5,6},{2,1},{4,3},{6,5},{9,10},{11,12},{13,14},{10,9},... | collective-permute-start | bytes 393224 | tf_op jit(solution)/shard_map/ppermute | solution.py:52
  8.0 14.0 %collective-permute-start.4 = (f32[4,2,64,128]{3,2,1,0:T(8,128)S(1)}, f32[4,2,64,128]{3,2,1,0:T(8,128)S(1)}, u32[]{:S(2)}, u32[]{:S(2)}) collective-permute-start(f32[4,2,64,128]{3,2,1,0:T(8,128)S(1)} %get-tuple-element.60), channel_id=1, source_target_pairs={{8,16},{16,8},{9,17},{17,9},{10,18},{18,10},{11,19},{19,11},{12,20... | collective-permute-start | bytes 786440 | tf_op jit(solution)/shard_map/ppermute | solution.py:52
  12.2 9.7 %collective-permute-start.5 = (f32[4,2,64,128]{3,2,1,0:T(8,128)S(1)}, f32[4,2,64,128]{3,2,1,0:T(8,128)S(1)}, u32[]{:S(2)}, u32[]{:S(2)}) collective-permute-start(f32[4,2,64,128]{3,2,1,0:T(8,128)S(1)} %get-tuple-element.61), channel_id=1, source_target_pairs={{0,8},{16,24},{8,0},{24,16},{1,9},{17,25},{9,1},{25,17},{2,10},{18... | collective-permute-start | bytes 786440 | tf_op jit(solution)/shard_map/ppermute | solution.py:52
  13.7 7.2 %collective-permute-start.3 = (f32[4,64,128]{2,1,0:T(8,128)S(1)}, f32[4,64,128]{2,1,0:T(8,128)S(1)}, u32[]{:S(2)}, u32[]{:S(2)}) collective-permute-start(f32[4,64,128]{2,1,0:T(8,128)S(1)} %get-tuple-element.59), channel_id=1, source_target_pairs={{0,1},{2,3},{4,5},{6,7},{1,0},{3,2},{5,4},{7,6},{8,9},{10,11},{12,... | collective-permute-start | bytes 393224 | tf_op jit(solution)/shard_map/ppermute | solution.py:52
  15.6 6.3 %collective-permute-start.6 = (f32[4,64,128]{2,1,0:T(8,128)S(1)}, f32[4,64,128]{2,1,0:T(8,128)S(1)}, u32[]{:S(2)}, u32[]{:S(2)}) collective-permute-start(f32[4,64,128]{2,1,0:T(8,128)S(1)} %get-tuple-element.62), channel_id=1, source_target_pairs={{8,16},{16,8},{9,17},{17,9},{10,18},{18,10},{11,19},{19,11},{12,20... | collective-permute-start | bytes 393224 | tf_op jit(solution)/shard_map/ppermute | solution.py:52
  32.5 7.7 %collective-permute-start.8 = (f32[4,2,64,128]{3,2,1,0:T(8,128)S(1)}, f32[4,2,64,128]{3,2,1,0:T(8,128)S(1)}, u32[]{:S(2)}, u32[]{:S(2)}) collective-permute-start(f32[4,2,64,128]{3,2,1,0:T(8,128)S(1)} %get-tuple-element.69), channel_id=1, source_target_pairs={{8,16},{16,8},{9,17},{17,9},{10,18},{18,10},{11,19},{19,11},{12,20... | collective-permute-start | bytes 786440 | tf_op jit(solution)/shard_map/ppermute | solution.py:52
  40.3 15.4 %collective-permute-start.10 = (f32[4,128,128]{2,1,0:T(8,128)S(1)}, f32[4,128,128]{2,1,0:T(8,128)S(1)}, u32[]{:S(2)}, u32[]{:S(2)}) collective-permute-start(f32[4,128,128]{2,1,0:T(8,128)S(1)} %get-tuple-element.72), channel_id=1, source_target_pairs={{1,2},{3,4},{5,6},{2,1},{4,3},{6,5},{9,10},{11,12},{13,14},{10,9},... | collective-permute-start | bytes 786440 | tf_op jit(solution)/shard_map/ppermute | solution.py:52
  43.5 17.4 %collective-permute-start.11 = (f32[4,128,128]{2,1,0:T(8,128)S(1)}, f32[4,128,128]{2,1,0:T(8,128)S(1)}, u32[]{:S(2)}, u32[]{:S(2)}) collective-permute-start(f32[4,128,128]{2,1,0:T(8,128)S(1)} %get-tuple-element.73), channel_id=1, source_target_pairs={{0,1},{2,3},{4,5},{6,7},{1,0},{3,2},{5,4},{7,6},{8,9},{10,11},{12,... | collective-permute-start | bytes 786440 | tf_op jit(solution)/shard_map/ppermute | solution.py:52
  43.6 7.0 %collective-permute-start.12 = (f32[4,1,64,128]{3,2,1,0:T(8,128)S(1)}, f32[4,1,64,128]{3,2,1,0:T(8,128)S(1)}, u32[]{:S(2)}, u32[]{:S(2)}) collective-permute-start(f32[4,1,64,128]{3,2,1,0:T(8,128)S(1)} %get-tuple-element.77), channel_id=1, source_target_pairs={{8,16},{16,8},{9,17},{17,9},{10,18},{18,10},{11,19},{19,11},{12,20... | collective-permute-start | bytes 393224 | tf_op jit(solution)/shard_map/ppermute | solution.py:52
  47.5 17.7 %collective-permute-start.14 = (f32[4,128,128]{2,1,0:T(8,128)S(1)}, f32[4,128,128]{2,1,0:T(8,128)S(1)}, u32[]{:S(2)}, u32[]{:S(2)}) collective-permute-start(f32[4,128,128]{2,1,0:T(8,128)S(1)} %get-tuple-element.84), channel_id=1, source_target_pairs={{1,2},{3,4},{5,6},{2,1},{4,3},{6,5},{9,10},{11,12},{13,14},{10,9},... | collective-permute-start | bytes 786440 | tf_op jit(solution)/shard_map/ppermute | solution.py:52
  50.6 15.7 %collective-permute-start.15 = (f32[4,128,128]{2,1,0:T(8,128)S(1)}, f32[4,128,128]{2,1,0:T(8,128)S(1)}, u32[]{:S(2)}, u32[]{:S(2)}) collective-permute-start(f32[4,128,128]{2,1,0:T(8,128)S(1)} %get-tuple-element.85), channel_id=1, source_target_pairs={{0,1},{2,3},{4,5},{6,7},{1,0},{3,2},{5,4},{7,6},{8,9},{10,11},{12,... | collective-permute-start | bytes 786440 | tf_op jit(solution)/shard_map/ppermute | solution.py:52
  52.1 11.4 %collective-permute-start.18 = (f32[4,1,64,128]{3,2,1,0:T(8,128)S(1)}, f32[4,1,64,128]{3,2,1,0:T(8,128)S(1)}, u32[]{:S(2)}, u32[]{:S(2)}) collective-permute-start(f32[4,1,64,128]{3,2,1,0:T(8,128)S(1)} %get-tuple-element.88), channel_id=1, source_target_pairs={{8,16},{16,8},{9,17},{17,9},{10,18},{18,10},{11,19},{19,11},{12,20... | collective-permute-start | bytes 393224 | tf_op jit(solution)/shard_map/ppermute | solution.py:52
  61.0 7.7 %collective-permute-start.16 = (f32[4,2,64,128]{3,2,1,0:T(8,128)S(1)}, f32[4,2,64,128]{3,2,1,0:T(8,128)S(1)}, u32[]{:S(2)}, u32[]{:S(2)}) collective-permute-start(f32[4,2,64,128]{3,2,1,0:T(8,128)S(1)} %get-tuple-element.86), channel_id=1, source_target_pairs={{8,16},{16,8},{9,17},{17,9},{10,18},{18,10},{11,19},{19,11},{12,20... | collective-permute-start | bytes 786440 | tf_op jit(solution)/shard_map/ppermute | solution.py:52
  63.4 5.2 %collective-permute-start.17 = (f32[4,2,64,128]{3,2,1,0:T(8,128)S(1)}, f32[4,2,64,128]{3,2,1,0:T(8,128)S(1)}, u32[]{:S(2)}, u32[]{:S(2)}) collective-permute-start(f32[4,2,64,128]{3,2,1,0:T(8,128)S(1)} %get-tuple-element.87), channel_id=1, source_target_pairs={{0,8},{16,24},{8,0},{24,16},{1,9},{17,25},{9,1},{25,17},{2,10},{18... | collective-permute-start | bytes 786440 | tf_op jit(solution)/shard_map/ppermute | solution.py:52
  79.6 8.9 %collective-permute-start.20 = (f32[4,2,64,128]{3,2,1,0:T(8,128)S(1)}, f32[4,2,64,128]{3,2,1,0:T(8,128)S(1)}, u32[]{:S(2)}, u32[]{:S(2)}) collective-permute-start(f32[4,2,64,128]{3,2,1,0:T(8,128)S(1)} %get-tuple-element.92), channel_id=1, source_target_pairs={{8,16},{16,8},{9,17},{17,9},{10,18},{18,10},{11,19},{19,11},{12,20... | collective-permute-start | bytes 786440 | tf_op jit(solution)/shard_map/ppermute | solution.py:52
  82.1 6.5 %collective-permute-start.21 = (f32[4,2,64,128]{3,2,1,0:T(8,128)S(1)}, f32[4,2,64,128]{3,2,1,0:T(8,128)S(1)}, u32[]{:S(2)}, u32[]{:S(2)}) collective-permute-start(f32[4,2,64,128]{3,2,1,0:T(8,128)S(1)} %get-tuple-element.93), channel_id=1, source_target_pairs={{0,8},{16,24},{8,0},{24,16},{1,9},{17,25},{9,1},{25,17},{2,10},{18... | collective-permute-start | bytes 786440 | tf_op jit(solution)/shard_map/ppermute | solution.py:52
  82.1 9.7 %collective-permute-start.22 = (f32[4,1,64,128]{3,2,1,0:T(8,128)S(1)}, f32[4,1,64,128]{3,2,1,0:T(8,128)S(1)}, u32[]{:S(2)}, u32[]{:S(2)}) collective-permute-start(f32[4,1,64,128]{3,2,1,0:T(8,128)S(1)} %get-tuple-element.96), channel_id=1, source_target_pairs={{8,16},{16,8},{9,17},{17,9},{10,18},{18,10},{11,19},{19,11},{12,20... | collective-permute-start | bytes 393224 | tf_op jit(solution)/shard_map/ppermute | solution.py:52
  85.2 7.0 %collective-permute-start.23 = (f32[4,1,64,128]{3,2,1,0:T(8,128)S(1)}, f32[4,1,64,128]{3,2,1,0:T(8,128)S(1)}, u32[]{:S(2)}, u32[]{:S(2)}) collective-permute-start(f32[4,1,64,128]{3,2,1,0:T(8,128)S(1)} %get-tuple-element.97), channel_id=1, source_target_pairs={{0,8},{16,24},{8,0},{24,16},{1,9},{17,25},{9,1},{25,17},{2,10},{18... | collective-permute-start | bytes 393224 | tf_op jit(solution)/shard_map/ppermute | solution.py:52
  85.3 7.4 %collective-permute-start.24 = (f32[4,64,128]{2,1,0:T(8,128)S(1)}, f32[4,64,128]{2,1,0:T(8,128)S(1)}, u32[]{:S(2)}, u32[]{:S(2)}) collective-permute-start(f32[4,64,128]{2,1,0:T(8,128)S(1)} %get-tuple-element.101), channel_id=1, source_target_pairs={{1,2},{3,4},{5,6},{2,1},{4,3},{6,5},{9,10},{11,12},{13,14},{10,9},... | collective-permute-start | bytes 393224 | tf_op jit(solution)/shard_map/ppermute | solution.py:52
  88.4 10.7 %collective-permute-start.25 = (f32[4,64,128]{2,1,0:T(8,128)S(1)}, f32[4,64,128]{2,1,0:T(8,128)S(1)}, u32[]{:S(2)}, u32[]{:S(2)}) collective-permute-start(f32[4,64,128]{2,1,0:T(8,128)S(1)} %get-tuple-element.102), channel_id=1, source_target_pairs={{0,1},{2,3},{4,5},{6,7},{1,0},{3,2},{5,4},{7,6},{8,9},{10,11},{12,... | collective-permute-start | bytes 393224 | tf_op jit(solution)/shard_map/ppermute | solution.py:52
  88.7 10.4 %collective-permute-start.26 = (f32[4,64,128]{2,1,0:T(8,128)S(1)}, f32[4,64,128]{2,1,0:T(8,128)S(1)}, u32[]{:S(2)}, u32[]{:S(2)}) collective-permute-start(f32[4,64,128]{2,1,0:T(8,128)S(1)} %get-tuple-element.103), channel_id=1, source_target_pairs={{1,2},{3,4},{5,6},{2,1},{4,3},{6,5},{9,10},{11,12},{13,14},{10,9},... | collective-permute-start | bytes 393224 | tf_op jit(solution)/shard_map/ppermute | solution.py:52
  91.8 10.1 %collective-permute-start.27 = (f32[4,64,128]{2,1,0:T(8,128)S(1)}, f32[4,64,128]{2,1,0:T(8,128)S(1)}, u32[]{:S(2)}, u32[]{:S(2)}) collective-permute-start(f32[4,64,128]{2,1,0:T(8,128)S(1)} %get-tuple-element.104), channel_id=1, source_target_pairs={{0,1},{2,3},{4,5},{6,7},{1,0},{3,2},{5,4},{7,6},{8,9},{10,11},{12,... | collective-permute-start | bytes 393224 | tf_op jit(solution)/shard_map/ppermute | solution.py:52
  (5 other events, 14.3 us)

commit v7 on v6

--- a/solution.py
+++ b/solution.py
@@ -146,10 +146,12 @@
         )
 
 
-def gradients(pos_ref, amps_ref, probe_ref, tables_ref, field_ref, grad_ref, work):
+def gradients(pos_ref, count_ref, amps_ref, probe_ref, tables_ref, field_ref, grad_ref, work):
     frame = probe_ref.shape[-1]
     o0, o1, inc, wave = work
-    count = pos_ref[2, 0]
+    count = count_ref[0, 0]
+    first_row = lax.axis_index("row") * (field_ref.shape[2] - frame)
+    first_col = lax.axis_index("col") * ((field_ref.shape[1] - 1) * LANES)
     lanes = lane_ids((frame, LANES))
 
     grad_ref[...] = jnp.zeros_like(grad_ref)
@@ -196,7 +198,8 @@
         base = group * GROUP
         where = []
         for k in range(GROUP):
-            row_at, col_at = pos_ref[0, base + k], pos_ref[1, base + k]
+            row_at = pos_ref[0, 0, 0, base + k] - first_row
+            col_at = pos_ref[1, 0, 0, base + k] - first_col
             block = lax.shift_right_logical(col_at, 7)
             shift = jnp.bitwise_and(col_at, LANES - 1)
             where.append((pl.ds(row_at, frame), block, shift))
@@ -266,18 +269,34 @@
         band_odd, band_even,
     ) = pieces
     _, blocks, all_rows, _ = grad_ref.shape
-    rim = row_odd.shape[2]
+    rim = row_odd.shape[-2]
     rows = all_rows - 2 * rim
+    closing = len(row_odd.shape) == 3
+
+    def row_pieces(block):
+        def rows_of(lo):
+            if block is outside:
+                return blend(grad_ref[:, 0, lo : lo + rim, :], grad_ref[:, blocks - 1, lo : lo + rim, :])
+            if block is rest:
+                return blend(grad_ref[:, blocks - 1, lo : lo + rim, :], grad_ref[:, 0, lo : lo + rim, :])
+            return grad_ref[:, block, lo : lo + rim, :]
+
+        return [rows_of(lo) for lo in (0, rim, rows, rows + rim)]
+
+    outside, rest = object(), object()
+    groups = (outer(blocks), inner(blocks))
+    if closing:
+        groups = ((outside,), (rest, *inner(blocks)))
     for odd, even, edge, group in (
-        (row_odd, row_even, edges, outer(blocks)),
-        (row_mid_odd, row_mid_even, edges_mid, inner(blocks)),
+        (row_odd, row_even, edges, groups[0]),
+        (row_mid_odd, row_mid_even, edges_mid, groups[1]),
     ):
         for at, block in enumerate(group):
-            odd[:, at], even[:, at] = paired(
-                "row", grad_ref[:, block, 0:rim, :], grad_ref[:, block, rim + rows : all_rows, :]
-            )
-            edge[:, at, 0:rim, :] = grad_ref[:, block, rim : 2 * rim, :]
-            edge[:, at, rim : 2 * rim, :] = grad_ref[:, block, rows : rim + rows, :]
+            top, upper, lower, bottom = row_pieces(block)
+            view = (slice(None),) if block is outside else (slice(None), at)
+            odd[view], even[view] = paired("row", top, bottom)
+            edge[*view, 0:rim, :] = upper
+            edge[*view, rim : 2 * rim, :] = lower
     left[...] = grad_ref[:, 0, 2 * rim : rows, :]
     mid[...] = grad_ref[:, 1 : blocks - 1, 2 * rim : rows, :]
     right[...] = grad_ref[:, blocks - 1, 2 * rim : rows, :]
@@ -300,7 +319,7 @@
 
 
 def first_kernel(
-    pos_ref, turned_ref, edge_odd, edge_even, mid_odd, mid_even, row_odd, row_even,
+    pos_ref, count_ref, turned_ref, edge_odd, edge_even, mid_odd, mid_even, row_odd, row_even,
     corner_odd, corner_even, amps_ref, probe_ref, tables_ref, field_ref, *rest,
 ):
     pieces, (grad_ref, *work) = rest[:-5], rest[-5:]
@@ -322,7 +341,7 @@
                 field_ref[plane, block, row_at : row_at + rim, :] = blend(
                     parts[block], parts[block + 1]
                 )
-    gradients(pos_ref, amps_ref, probe_ref, tables_ref, field_ref, grad_ref, work)
+    gradients(pos_ref, count_ref, amps_ref, probe_ref, tables_ref, field_ref, grad_ref, work)
     write_grad(grad_ref, pieces)
 
 
@@ -340,10 +359,16 @@
             upper, lower = fold(edges, row_odd, row_even, plane, at)
             folded_ref[plane, at, 0:rim, :] = upper
             folded_ref[plane, at, rim : 2 * rim, :] = lower
-    if odd_ref.shape[1] == 2 * rim:
-        odd_ref[...], even_ref[...] = paired("col", folded_ref[:, 0], folded_ref[:, count - 1])
-    else:
-        pack_bands(folded_ref, (odd_ref, even_ref), slice(0, rim), slice(rim, 2 * rim))
+    odd_ref[...], even_ref[...] = paired("col", folded_ref[:, 0], folded_ref[:, count - 1])
+
+
+def last_fold_kernel(edges, row_odd, row_even, odd_ref, even_ref):
+    rim = row_odd.shape[1]
+    for plane in range(edges.shape[0]):
+        from_up, from_down = paired("row", row_odd[plane], row_even[plane])
+        upper = edges[plane, 0:rim, :] + from_up
+        lower = swap_halves(edges[plane, rim : 2 * rim, :] + from_down)
+        odd_ref[plane], even_ref[plane] = paired("col", blend(upper, lower), blend(lower, upper))
 
 
 def fold_mid_kernel(edges, row_odd, row_even, up_ref, down_ref, odd_ref, even_ref):
@@ -366,7 +391,7 @@
 
 
 def next_kernel(
-    pos_ref, old_ref, up_ref, down_ref, up_mid, down_mid, left_ref, mid_ref, right_ref,
+    pos_ref, count_ref, old_ref, up_ref, down_ref, up_mid, down_mid, left_ref, mid_ref, right_ref,
     from_odd, from_even, row_odd, row_even, row_mid_odd, row_mid_even,
     amps_ref, probe_ref, tables_ref, field_ref, *rest,
 ):
@@ -383,11 +408,12 @@
             middle = mid_ref[:, at]
         elif block == 0:
             at, odd, even, up, down = 0, row_odd, row_even, up_ref, down_ref
-            inside = lane >= pos_ref[2, 1] * (LANES // 2)
+            inside = lane >= jnp.where(lax.axis_index("col") == 0, LANES // 2, 0)
             middle = left_ref[...] + from_left
         else:
             at, odd, even, up, down = 1, row_odd, row_even, up_ref, down_ref
-            inside = lane < LANES - pos_ref[2, 2] * (LANES // 2)
+            at_end = lax.axis_index("col") == lax.axis_size("col") - 1
+            inside = lane < jnp.where(at_end, LANES // 2, LANES)
             middle = right_ref[...] + from_right
         from_up, from_down = paired("row", odd[:, at], even[:, at])
         for lo, hi, values in (
@@ -399,50 +425,72 @@
         ):
             updated = old_ref[:, block, lo:hi, :] - values
             field_ref[:, block, lo:hi, :] = jnp.where(inside, updated, 0.0)
-    gradients(pos_ref, amps_ref, probe_ref, tables_ref, field_ref, grad_ref, work)
+    gradients(pos_ref, count_ref, amps_ref, probe_ref, tables_ref, field_ref, grad_ref, work)
     write_grad(grad_ref, pieces)
 
 
-def finish_kernel(
-    field_ref, edges, edges_mid, row_odd, row_even, left_ref, mid_ref, right_ref,
-    mid_odd, mid_even, edge_odd, edge_even, out_ref,
+def put_rows(field_ref, plane, row_at, values, sides, part, target_ref, put_at):
+    size = values[0].shape[0]
+    if part == 1:
+        sides = [swap_halves(side) for side in sides]
+    values = [values[0] + sides[0], *values[1:-1], values[-1] + sides[1]]
+    turned = [
+        swap_halves(field_ref[plane, block, row_at : row_at + size, :] - block_values)
+        for block, block_values in enumerate(values)
+    ]
+    for block in range(len(turned) - 1):
+        target_ref[plane, put_at : put_at + size, block * LANES : (block + 1) * LANES] = blend(
+            turned[block], turned[block + 1]
+        )
+
+
+def finish_mid_kernel(
+    field_ref, left_ref, mid_ref, right_ref, from_odd, from_even, out_hbm, result, sem
 ):
-    planes, blocks, _, _ = field_ref.shape
-    rows = out_ref.shape[1]
-    rim = edge_odd.shape[1]
-    (first, last), (upper, lower) = segments(rows, rim)
-    half = upper.stop - upper.start
-
-    def whole(plane, part, edge):
-        size = rim if edge else half
-        at = slice(part * size, (part + 1) * size)
-        if edge:
-            values = [edges[plane, 0, at, :], edges[plane, 1, at, :]]
-            values[1:1] = [
-                fold(edges_mid, row_odd, row_even, plane, k)[part] for k in range(blocks - 2)
-            ]
-        else:
+    planes, blocks, all_rows, _ = field_ref.shape
+    band = result.shape[1]
+    rim = (all_rows - band) // 4
+    half = band // 2
+    for plane in range(planes):
+        sides = paired("col", from_odd[plane], from_even[plane])
+        for part in range(2):
+            at = slice(part * half, (part + 1) * half)
             values = [left_ref[plane, at, :], right_ref[plane, at, :]]
             values[1:1] = [mid_ref[plane, k, at, :] for k in range(blocks - 2)]
-        odd, even = (edge_odd, edge_even) if edge else (mid_odd, mid_even)
-        extras = paired("col", odd[plane], even[plane])
-        if part == 1:
-            extras = [swap_halves(extra) for extra in extras]
-        values[0] += extras[0]
-        values[-1] += extras[1]
-        return values
-
-    for plane in range(planes):
-        for part, edge, at in ((0, True, first), (0, False, upper), (1, False, lower), (1, True, last)):
-            values = whole(plane, part, edge)
-            turned = [
-                swap_halves(field_ref[plane, block, rim + at.start : rim + at.stop, :] - values[block])
-                for block in range(blocks)
-            ]
-            for block in range(blocks - 1):
-                out_ref[plane, at, block * LANES : (block + 1) * LANES] = blend(
-                    turned[block], turned[block + 1]
-                )
+            put_rows(
+                field_ref, plane, 2 * rim + part * half, values, sides, part, result, part * half
+            )
+    copy = pltpu.make_async_copy(result, out_hbm.at[:, rim : rim + band, :], sem)
+    copy.start()
+    copy.wait()
+
+
+def finish_edge_kernel(
+    field_ref, edges_mid, row_odd, row_even, from_odd, from_even, _, out_hbm, result, *sems
+):
+    planes, blocks, all_rows, _ = field_ref.shape
+    rim = from_odd.shape[1]
+    rows = all_rows - 2 * rim
+    copies = []
+    for part in range(2):
+        for plane in range(planes):
+            sides = paired("col", from_odd[plane], from_even[plane])
+            folded = [fold(edges_mid, row_odd, row_even, plane, k)[part] for k in range(blocks - 1)]
+            values = [*folded, folded[0]]
+            put_rows(
+                field_ref, plane, rim + part * (rows - rim), values, sides, part, result, part * rim
+            )
+        at = part * (rows - rim)
+        copies.append(
+            pltpu.make_async_copy(
+                result.at[:, part * rim : (part + 1) * rim, :],
+                out_hbm.at[:, at : at + rim, :],
+                sems[part],
+            )
+        )
+        copies[-1].start()
+    for copy in copies:
+        copy.wait()
 
 
 def f32(*shape):
@@ -460,35 +508,23 @@
     rim = frame // 2
     blocks = tile_c // LANES + 1
     slots = amplitudes.shape[2]
-    row_id, col_id = lax.axis_index("row"), lax.axis_index("col")
+    assert slots % GROUP == 0
     amps = amplitudes[0, 0]
-    flags = jnp.stack(
-        [
-            scan_count[0, 0],
-            (col_id == 0).astype(jnp.int32),
-            (col_id == lax.axis_size("col") - 1).astype(jnp.int32),
-        ]
-    )
-    pos = jnp.stack(
-        [
-            scan_pos[0, 0, 0] - row_id * tile_r,
-            scan_pos[1, 0, 0] - col_id * tile_c,
-            jnp.pad(flags, (0, slots - 3)),
-        ]
-    )
+    scalars = [scan_pos, scan_count]
     tables = jnp.asarray(transform_tables(frame))
     tile = object_slices.reshape(planes, tile_r, tile_c)
 
     band = tile_r - 2 * rim
 
-    def call(kernel, outs, mib, scratch=(), scalars=(), raw=()):
+    def call(kernel, outs, mib, scratch=(), scalars=(), raw=(), in_hbm=False, alias=None):
         def run(*arrays):
             return pl.pallas_call(
                 kernel,
                 out_shape=outs,
+                input_output_aliases=alias or {},
                 in_specs=[smem()] * len(scalars) + [vmem()] * len(arrays)
                 + [pl.BlockSpec(memory_space=pltpu.HBM)] * len(raw),
-                out_specs=[vmem()] * len(outs),
+                out_specs=[pl.BlockSpec(memory_space=pltpu.HBM) if in_hbm else vmem()] * len(outs),
                 scratch_shapes=list(scratch),
                 compiler_params=pltpu.CompilerParams(vmem_limit_bytes=mib << 20),
             )(
@@ -539,7 +575,7 @@
         [field_shape] + pieces + [band_rows] * 2,
         20,
         scratch=work,
-        scalars=[pos],
+        scalars=scalars,
     )(turned, *edge_strips, *mid_strips, *row_strips, *corner_strips, amps, probe, tables)
 
     for iteration in range(1, ITERS):
@@ -557,9 +593,19 @@
         inner_strips = exchange(odd_in, even_in, "row")
         up, down, odd, even = call(total_kernel, [strip] * 4, 4)(edges, *edge_strips)
         row_strips = exchange(odd, even, "row")
-        bands = [band_rows] * 2 if iteration < ITERS - 1 else [packed_mid] * 2
+        if iteration < ITERS - 1:
+            outs = pieces + [band_rows] * 2
+        else:
+            rest = f32(planes, blocks - 1, rim, LANES)
+            outs = [packed_edge] * 2 + [rest] * 2 + [
+                f32(planes, 2 * rim, LANES),
+                f32(planes, blocks - 1, 2 * rim, LANES),
+                *pieces[6:],
+                packed_mid,
+                packed_mid,
+            ]
         field, *grads = call(
-            next_kernel, [field_shape] + pieces + bands, 20, scratch=work, scalars=[pos]
+            next_kernel, [field_shape] + outs, 20, scratch=work, scalars=scalars
         )(
             field, up, down, up_mid, down_mid, left, mid, right,
             *mid_strips, *row_strips, *inner_strips, amps, probe, tables,
@@ -569,11 +615,25 @@
     row_strips = exchange(odd, even, "row")
     mid_strips = exchange(band_odd, band_even, "col")
     inner_strips = exchange(odd_in, even_in, "row")
-    edges, odd, even = call(fold_kernel, [edge_rows] + [packed_edge] * 2, 4)(edges, *row_strips)
+    odd, even = call(last_fold_kernel, [packed_edge] * 2, 4)(edges, *row_strips)
     edge_strips = exchange(odd, even, "col")
-    (out,) = call(finish_kernel, [jax.ShapeDtypeStruct((planes, tile_r, tile_c), jnp.float32)], 8)(
-        field, edges, edges_mid, *inner_strips, left, mid, right, *mid_strips, *edge_strips
-    )
+    whole = pltpu.HBM((planes, tile_r, tile_c), jnp.float32)
+    (out,) = call(
+        finish_mid_kernel,
+        [whole],
+        4,
+        scratch=[f32(planes, band, tile_c), pltpu.SemaphoreType.DMA(())],
+        in_hbm=True,
+    )(field, left, mid, right, *mid_strips)
+    (out,) = call(
+        finish_edge_kernel,
+        [whole],
+        4,
+        scratch=[f32(planes, 2 * rim, tile_c)] + [pltpu.SemaphoreType.DMA(())] * 2,
+        raw=[out],
+        in_hbm=True,
+        alias={6: 0},
+    )(field, edges_mid, *inner_strips, *edge_strips)
     return out.reshape(object_slices.shape)
 
 

time: 104 us -> 102 us (0.981)
  the two profiles are of different devices: /device:TPU:21 before, /device:TPU:16 now
where the time goes in v7:
time: 102 us
  starting transfers between devices  53.9 us (53%)
  Pallas kernels  26.5 us (26%)
  waiting for transfers between devices  19 us (19%)
  local copies, waits for them, and re-layouts  1.24 us (1%)
  between operations  1.09 us (1%)
    ppermute x28, starting transfers between devices, exchange(): received.append(lax.ppermute(values, axis, pairs))  53.9 us
    pallas_call x11, Pallas kernels, run(): pl.pallas_call(kernel, out_shape=outs, input_output_aliases=alias or {},...  26.5 us
    ppermute x28, waiting for transfers between devices, exchange(): received.append(lax.ppermute(values, axis, pairs))  19 us
  transfers between devices with their start and end apart: 28, of which 8 were waited for; matrix products, arithmetic and copies ran while one was open for 0% of the time, Pallas kernels for 3%

profile of v7, /device:TPU:16, one launch (start us, length us, event | category | flops | bytes accessed | tf_op | source)
XLA Modules:
  0.0 101.7 jit_solution(8017141822441412615)
XLA Ops:
  1.7 3.3 %collective-permute-start = (f32[4,64,128]{2,1,0:T(8,128)S(1)}, f32[4,64,128]{2,1,0:T(8,128)S(1)}, u32[]{:S(2)}, u32[]{:S(2)}) collective-permute-start(f32[4,64,128]{2,1,0:T(8,128)S(1)} %get-tuple-element.55), channel_id=1, source_target_pairs={{1,2},{3,4},{5,6},{2,1},{4,3},{6,5},{9,10},{11,12},{13,14},{10,9},... | collective-permute-start | bytes 393224 | tf_op jit(solution)/shard_map/ppermute | solution.py:52
  5.0 1.7 %collective-permute-start.1 = (f32[4,64,128]{2,1,0:T(8,128)S(1)}, f32[4,64,128]{2,1,0:T(8,128)S(1)}, u32[]{:S(2)}, u32[]{:S(2)}) collective-permute-start(f32[4,64,128]{2,1,0:T(8,128)S(1)} %get-tuple-element.56), channel_id=1, source_target_pairs={{0,1},{2,3},{4,5},{6,7},{1,0},{3,2},{5,4},{7,6},{8,9},{10,11},{12,... | collective-permute-start | bytes 393224 | tf_op jit(solution)/shard_map/ppermute | solution.py:52
  6.7 2.2 %collective-permute-start.2 = (f32[4,64,128]{2,1,0:T(8,128)S(1)}, f32[4,64,128]{2,1,0:T(8,128)S(1)}, u32[]{:S(2)}, u32[]{:S(2)}) collective-permute-start(f32[4,64,128]{2,1,0:T(8,128)S(1)} %get-tuple-element.57), channel_id=1, source_target_pairs={{1,2},{3,4},{5,6},{2,1},{4,3},{6,5},{9,10},{11,12},{13,14},{10,9},... | collective-permute-start | bytes 393224 | tf_op jit(solution)/shard_map/ppermute | solution.py:52
  9.6 2.9 %collective-permute-start.5 = (f32[4,2,64,128]{3,2,1,0:T(8,128)S(1)}, f32[4,2,64,128]{3,2,1,0:T(8,128)S(1)}, u32[]{:S(2)}, u32[]{:S(2)}) collective-permute-start(f32[4,2,64,128]{3,2,1,0:T(8,128)S(1)} %get-tuple-element.60), channel_id=1, source_target_pairs={{0,8},{16,24},{8,0},{24,16},{1,9},{17,25},{9,1},{25,17},{2,10},{18... | collective-permute-start | bytes 786440 | tf_op jit(solution)/shard_map/ppermute | solution.py:52
  13.7 1.8 %collective-permute-done.1.from_even.edge_even = f32[4,64,128]{2,1,0:T(8,128)S(1)} collective-permute-done((f32[4,64,128]{2,1,0:T(8,128)S(1)}, f32[4,64,128]{2,1,0:T(8,128)S(1)}, u32[]{:S(2)}, u32[]{:S(2)}) %collective-permute-start.1) | collective-permute-done | bytes 131104 | tf_op jit(solution)/shard_map/ppermute | solution.py:52
  16.3 2.9 %collective-permute-start.7 = (f32[4,64,128]{2,1,0:T(8,128)S(1)}, f32[4,64,128]{2,1,0:T(8,128)S(1)}, u32[]{:S(2)}, u32[]{:S(2)}) collective-permute-start(f32[4,64,128]{2,1,0:T(8,128)S(1)} %get-tuple-element.62), channel_id=1, source_target_pairs={{0,8},{16,24},{8,0},{24,16},{1,9},{17,25},{9,1},{25,17},{2,10},{18... | collective-permute-start | bytes 393224 | tf_op jit(solution)/shard_map/ppermute | solution.py:52
  19.8 1.6 %shard_map.66 = (bf16[8,256,256]{2,1,0:T(8,128)(2,1)S(1)}, f32[16,128,128]{2,1,0:T(8,128)S(1)}, f32[2,128,128]{2,1,0:T(8,128)S(1)}) custom-call(bf16[8,256,256]{2,1,0:T(8,128)(2,1)} %constant.2.clone.refs_0_, f32[16,128,128]{2,1,0:T(8,128)} %bitcast.4, f32[2,128,128]{2,1,0:T(8,128)} %refs_2_.1), custom_call_target="tpu_custom_call" | custom-call | tf_op jit(solution)/shard_map/pallas_call | solution.py:521
  21.5 10.6 %shard_map.67 = (f32[4,3,384,128]{3,2,1,0:T(8,128)S(1)}, f32[4,2,64,128]{3,2,1,0:T(8,128)S(1)}, f32[4,2,64,128]{3,2,1,0:T(8,128)S(1)}, f32[4,1,64,128]{3,2,1,0:T...) custom-call(s32[2,1,1,16]{3,2,1,0:T(1,128)S(1)} %copy-done.1, ...), custom_call_target="tpu_custom_call" | custom-call | tf_op jit(solution)/shard_map/pallas_call | solution.py:521
  32.7 3.4 %collective-permute-start.9 = (f32[4,2,64,128]{3,2,1,0:T(8,128)S(1)}, f32[4,2,64,128]{3,2,1,0:T(8,128)S(1)}, u32[]{:S(2)}, u32[]{:S(2)}) collective-permute-start(f32[4,2,64,128]{3,2,1,0:T(8,128)S(1)} %get-tuple-element.69), channel_id=1, source_target_pairs={{0,8},{16,24},{8,0},{24,16},{1,9},{17,25},{9,1},{25,17},{2,10},{18... | collective-permute-start | bytes 786440 | tf_op jit(solution)/shard_map/ppermute | solution.py:52
  37.4 1.9 %collective-permute-start.10 = (f32[4,128,128]{2,1,0:T(8,128)S(1)}, f32[4,128,128]{2,1,0:T(8,128)S(1)}, u32[]{:S(2)}, u32[]{:S(2)}) collective-permute-start(f32[4,128,128]{2,1,0:T(8,128)S(1)} %get-tuple-element.71), channel_id=1, source_target_pairs={{1,2},{3,4},{5,6},{2,1},{4,3},{6,5},{9,10},{11,12},{13,14},{10,9},... | collective-permute-start | bytes 786440 | tf_op jit(solution)/shard_map/ppermute | solution.py:52
  39.3 3.1 %collective-permute-start.11 = (f32[4,128,128]{2,1,0:T(8,128)S(1)}, f32[4,128,128]{2,1,0:T(8,128)S(1)}, u32[]{:S(2)}, u32[]{:S(2)}) collective-permute-start(f32[4,128,128]{2,1,0:T(8,128)S(1)} %get-tuple-element.72), channel_id=1, source_target_pairs={{0,1},{2,3},{4,5},{6,7},{1,0},{3,2},{5,4},{7,6},{8,9},{10,11},{12,... | collective-permute-start | bytes 786440 | tf_op jit(solution)/shard_map/ppermute | solution.py:52
  43.1 5.9 %collective-permute-start.13 = (f32[4,1,64,128]{3,2,1,0:T(8,128)S(1)}, f32[4,1,64,128]{3,2,1,0:T(8,128)S(1)}, u32[]{:S(2)}, u32[]{:S(2)}) collective-permute-start(f32[4,1,64,128]{3,2,1,0:T(8,128)S(1)} %get-tuple-element.77), channel_id=1, source_target_pairs={{0,8},{16,24},{8,0},{24,16},{1,9},{17,25},{9,1},{25,17},{2,10},{18... | collective-permute-start | bytes 393224 | tf_op jit(solution)/shard_map/ppermute | solution.py:52
  48.9 1.9 %collective-permute-start.14 = (f32[4,128,128]{2,1,0:T(8,128)S(1)}, f32[4,128,128]{2,1,0:T(8,128)S(1)}, u32[]{:S(2)}, u32[]{:S(2)}) collective-permute-start(f32[4,128,128]{2,1,0:T(8,128)S(1)} %get-tuple-element.83), channel_id=1, source_target_pairs={{1,2},{3,4},{5,6},{2,1},{4,3},{6,5},{9,10},{11,12},{13,14},{10,9},... | collective-permute-start | bytes 786440 | tf_op jit(solution)/shard_map/ppermute | solution.py:52
  50.8 1.4 %collective-permute-start.15 = (f32[4,128,128]{2,1,0:T(8,128)S(1)}, f32[4,128,128]{2,1,0:T(8,128)S(1)}, u32[]{:S(2)}, u32[]{:S(2)}) collective-permute-start(f32[4,128,128]{2,1,0:T(8,128)S(1)} %get-tuple-element.84), channel_id=1, source_target_pairs={{0,1},{2,3},{4,5},{6,7},{1,0},{3,2},{5,4},{7,6},{8,9},{10,11},{12,... | collective-permute-start | bytes 786440 | tf_op jit(solution)/shard_map/ppermute | solution.py:52
  53.0 7.5 %collective-permute-done.11.from_even = f32[4,128,128]{2,1,0:T(8,128)S(1)} collective-permute-done((f32[4,128,128]{2,1,0:T(8,128)S(1)}, f32[4,128,128]{2,1,0:T(8,128)S(1)}, u32[]{:S(2)}, u32[]{:S(2)}) %collective-permute-start.11) | collective-permute-done | bytes 262176 | tf_op jit(solution)/shard_map/ppermute | solution.py:52
  61.3 1.6 %collective-permute-start.17 = (f32[4,2,64,128]{3,2,1,0:T(8,128)S(1)}, f32[4,2,64,128]{3,2,1,0:T(8,128)S(1)}, u32[]{:S(2)}, u32[]{:S(2)}) collective-permute-start(f32[4,2,64,128]{3,2,1,0:T(8,128)S(1)} %get-tuple-element.86), channel_id=1, source_target_pairs={{0,8},{16,24},{8,0},{24,16},{1,9},{17,25},{9,1},{25,17},{2,10},{18... | collective-permute-start | bytes 786440 | tf_op jit(solution)/shard_map/ppermute | solution.py:52
  64.3 1.9 %collective-permute-done.15.from_even = f32[4,128,128]{2,1,0:T(8,128)S(1)} collective-permute-done((f32[4,128,128]{2,1,0:T(8,128)S(1)}, f32[4,128,128]{2,1,0:T(8,128)S(1)}, u32[]{:S(2)}, u32[]{:S(2)}) %collective-permute-start.15) | collective-permute-done | bytes 262176 | tf_op jit(solution)/shard_map/ppermute | solution.py:52
  66.1 10.9 %shard_map.71 = (f32[4,3,384,128]{3,2,1,0:T(8,128)S(1)}, f32[4,64,128]{2,1,0:T(8,128)S(1)}, f32[4,64,128]{2,1,0:T(8,128)S(1)}, f32[4,2,64,128]{3,2,1,0:T(8,128)S...) custom-call(s32[2,1,1,16]{3,2,1,0:T(1,128)S(1)} %copy-done.1, ...), custom_call_target="tpu_custom_call" | custom-call | tf_op jit(solution)/shard_map/pallas_call | solution.py:521
  77.7 3.9 %collective-permute-start.23 = (f32[4,64,128]{2,1,0:T(8,128)S(1)}, f32[4,64,128]{2,1,0:T(8,128)S(1)}, u32[]{:S(2)}, u32[]{:S(2)}) collective-permute-start(f32[4,64,128]{2,1,0:T(8,128)S(1)} %get-tuple-element.95), channel_id=1, source_target_pairs={{0,8},{16,24},{8,0},{24,16},{1,9},{17,25},{9,1},{25,17},{2,10},{18... | collective-permute-start | bytes 393224 | tf_op jit(solution)/shard_map/ppermute | solution.py:52
  81.6 1.9 %collective-permute-start.26 = (f32[4,64,128]{2,1,0:T(8,128)S(1)}, f32[4,64,128]{2,1,0:T(8,128)S(1)}, u32[]{:S(2)}, u32[]{:S(2)}) collective-permute-start(f32[4,64,128]{2,1,0:T(8,128)S(1)} %get-tuple-element.101), channel_id=1, source_target_pairs={{1,2},{3,4},{5,6},{2,1},{4,3},{6,5},{9,10},{11,12},{13,14},{10,9},... | collective-permute-start | bytes 393224 | tf_op jit(solution)/shard_map/ppermute | solution.py:52
  85.5 4.7 %collective-permute-start.27 = (f32[4,64,128]{2,1,0:T(8,128)S(1)}, f32[4,64,128]{2,1,0:T(8,128)S(1)}, u32[]{:S(2)}, u32[]{:S(2)}) collective-permute-start(f32[4,64,128]{2,1,0:T(8,128)S(1)} %get-tuple-element.102), channel_id=1, source_target_pairs={{0,1},{2,3},{4,5},{6,7},{1,0},{3,2},{5,4},{7,6},{8,9},{10,11},{12,... | collective-permute-start | bytes 393224 | tf_op jit(solution)/shard_map/ppermute | solution.py:52
  90.3 1.9 %collective-permute-start.24 = (f32[4,64,128]{2,1,0:T(8,128)S(1)}, f32[4,64,128]{2,1,0:T(8,128)S(1)}, u32[]{:S(2)}, u32[]{:S(2)}) collective-permute-start(f32[4,64,128]{2,1,0:T(8,128)S(1)} %get-tuple-element.96), channel_id=1, source_target_pairs={{1,2},{3,4},{5,6},{2,1},{4,3},{6,5},{9,10},{11,12},{13,14},{10,9},... | collective-permute-start | bytes 393224 | tf_op jit(solution)/shard_map/ppermute | solution.py:52
  95.3 3.2 %collective-permute-done.24.from_odd = f32[4,64,128]{2,1,0:T(8,128)S(1)} collective-permute-done((f32[4,64,128]{2,1,0:T(8,128)S(1)}, f32[4,64,128]{2,1,0:T(8,128)S(1)}, u32[]{:S(2)}, u32[]{:S(2)}) %collective-permute-start.24) | collective-permute-done | bytes 131104 | tf_op jit(solution)/shard_map/ppermute | solution.py:52
  98.4 1.9 %collective-permute-done.25.from_even = f32[4,64,128]{2,1,0:T(8,128)S(1)} collective-permute-done((f32[4,64,128]{2,1,0:T(8,128)S(1)}, f32[4,64,128]{2,1,0:T(8,128)S(1)}, u32[]{:S(2)}, u32[]{:S(2)}) %collective-permute-start.25) | collective-permute-done | bytes 131104 | tf_op jit(solution)/shard_map/ppermute | solution.py:52
  (47 shorter events, 16.8 us)
Async XLA Ops:
  1.7 10.8 %collective-permute-start = (f32[4,64,128]{2,1,0:T(8,128)S(1)}, f32[4,64,128]{2,1,0:T(8,128)S(1)}, u32[]{:S(2)}, u32[]{:S(2)}) collective-permute-start(f32[4,64,128]{2,1,0:T(8,128)S(1)} %get-tuple-element.55), channel_id=1, source_target_pairs={{1,2},{3,4},{5,6},{2,1},{4,3},{6,5},{9,10},{11,12},{13,14},{10,9},... | collective-permute-start | bytes 393224 | tf_op jit(solution)/shard_map/ppermute | solution.py:52
  5.0 10.4 %collective-permute-start.1 = (f32[4,64,128]{2,1,0:T(8,128)S(1)}, f32[4,64,128]{2,1,0:T(8,128)S(1)}, u32[]{:S(2)}, u32[]{:S(2)}) collective-permute-start(f32[4,64,128]{2,1,0:T(8,128)S(1)} %get-tuple-element.56), channel_id=1, source_target_pairs={{0,1},{2,3},{4,5},{6,7},{1,0},{3,2},{5,4},{7,6},{8,9},{10,11},{12,... | collective-permute-start | bytes 393224 | tf_op jit(solution)/shard_map/ppermute | solution.py:52
  6.7 9.5 %collective-permute-start.2 = (f32[4,64,128]{2,1,0:T(8,128)S(1)}, f32[4,64,128]{2,1,0:T(8,128)S(1)}, u32[]{:S(2)}, u32[]{:S(2)}) collective-permute-start(f32[4,64,128]{2,1,0:T(8,128)S(1)} %get-tuple-element.57), channel_id=1, source_target_pairs={{1,2},{3,4},{5,6},{2,1},{4,3},{6,5},{9,10},{11,12},{13,14},{10,9},... | collective-permute-start | bytes 393224 | tf_op jit(solution)/shard_map/ppermute | solution.py:52
  8.9 12.5 %collective-permute-start.4 = (f32[4,2,64,128]{3,2,1,0:T(8,128)S(1)}, f32[4,2,64,128]{3,2,1,0:T(8,128)S(1)}, u32[]{:S(2)}, u32[]{:S(2)}) collective-permute-start(f32[4,2,64,128]{3,2,1,0:T(8,128)S(1)} %get-tuple-element.59), channel_id=1, source_target_pairs={{8,16},{16,8},{9,17},{17,9},{10,18},{18,10},{11,19},{19,11},{12,20... | collective-permute-start | bytes 786440 | tf_op jit(solution)/shard_map/ppermute | solution.py:52
  9.6 11.8 %collective-permute-start.5 = (f32[4,2,64,128]{3,2,1,0:T(8,128)S(1)}, f32[4,2,64,128]{3,2,1,0:T(8,128)S(1)}, u32[]{:S(2)}, u32[]{:S(2)}) collective-permute-start(f32[4,2,64,128]{3,2,1,0:T(8,128)S(1)} %get-tuple-element.60), channel_id=1, source_target_pairs={{0,8},{16,24},{8,0},{24,16},{1,9},{17,25},{9,1},{25,17},{2,10},{18... | collective-permute-start | bytes 786440 | tf_op jit(solution)/shard_map/ppermute | solution.py:52
  12.5 8.9 %collective-permute-start.3 = (f32[4,64,128]{2,1,0:T(8,128)S(1)}, f32[4,64,128]{2,1,0:T(8,128)S(1)}, u32[]{:S(2)}, u32[]{:S(2)}) collective-permute-start(f32[4,64,128]{2,1,0:T(8,128)S(1)} %get-tuple-element.58), channel_id=1, source_target_pairs={{0,1},{2,3},{4,5},{6,7},{1,0},{3,2},{5,4},{7,6},{8,9},{10,11},{12,... | collective-permute-start | bytes 393224 | tf_op jit(solution)/shard_map/ppermute | solution.py:52
  15.6 5.8 %collective-permute-start.6 = (f32[4,64,128]{2,1,0:T(8,128)S(1)}, f32[4,64,128]{2,1,0:T(8,128)S(1)}, u32[]{:S(2)}, u32[]{:S(2)}) collective-permute-start(f32[4,64,128]{2,1,0:T(8,128)S(1)} %get-tuple-element.61), channel_id=1, source_target_pairs={{8,16},{16,8},{9,17},{17,9},{10,18},{18,10},{11,19},{19,11},{12,20... | collective-permute-start | bytes 393224 | tf_op jit(solution)/shard_map/ppermute | solution.py:52
  16.3 5.2 %collective-permute-start.7 = (f32[4,64,128]{2,1,0:T(8,128)S(1)}, f32[4,64,128]{2,1,0:T(8,128)S(1)}, u32[]{:S(2)}, u32[]{:S(2)}) collective-permute-start(f32[4,64,128]{2,1,0:T(8,128)S(1)} %get-tuple-element.62), channel_id=1, source_target_pairs={{0,8},{16,24},{8,0},{24,16},{1,9},{17,25},{9,1},{25,17},{2,10},{18... | collective-permute-start | bytes 393224 | tf_op jit(solution)/shard_map/ppermute | solution.py:52
  37.4 15.6 %collective-permute-start.10 = (f32[4,128,128]{2,1,0:T(8,128)S(1)}, f32[4,128,128]{2,1,0:T(8,128)S(1)}, u32[]{:S(2)}, u32[]{:S(2)}) collective-permute-start(f32[4,128,128]{2,1,0:T(8,128)S(1)} %get-tuple-element.71), channel_id=1, source_target_pairs={{1,2},{3,4},{5,6},{2,1},{4,3},{6,5},{9,10},{11,12},{13,14},{10,9},... | collective-permute-start | bytes 786440 | tf_op jit(solution)/shard_map/ppermute | solution.py:52
  39.3 21.2 %collective-permute-start.11 = (f32[4,128,128]{2,1,0:T(8,128)S(1)}, f32[4,128,128]{2,1,0:T(8,128)S(1)}, u32[]{:S(2)}, u32[]{:S(2)}) collective-permute-start(f32[4,128,128]{2,1,0:T(8,128)S(1)} %get-tuple-element.72), channel_id=1, source_target_pairs={{0,1},{2,3},{4,5},{6,7},{1,0},{3,2},{5,4},{7,6},{8,9},{10,11},{12,... | collective-permute-start | bytes 786440 | tf_op jit(solution)/shard_map/ppermute | solution.py:52
  42.4 8.4 %collective-permute-start.12 = (f32[4,1,64,128]{3,2,1,0:T(8,128)S(1)}, f32[4,1,64,128]{3,2,1,0:T(8,128)S(1)}, u32[]{:S(2)}, u32[]{:S(2)}) collective-permute-start(f32[4,1,64,128]{3,2,1,0:T(8,128)S(1)} %get-tuple-element.76), channel_id=1, source_target_pairs={{8,16},{16,8},{9,17},{17,9},{10,18},{18,10},{11,19},{19,11},{12,20... | collective-permute-start | bytes 393224 | tf_op jit(solution)/shard_map/ppermute | solution.py:52
  43.1 9.2 %collective-permute-start.13 = (f32[4,1,64,128]{3,2,1,0:T(8,128)S(1)}, f32[4,1,64,128]{3,2,1,0:T(8,128)S(1)}, u32[]{:S(2)}, u32[]{:S(2)}) collective-permute-start(f32[4,1,64,128]{3,2,1,0:T(8,128)S(1)} %get-tuple-element.77), channel_id=1, source_target_pairs={{0,8},{16,24},{8,0},{24,16},{1,9},{17,25},{9,1},{25,17},{2,10},{18... | collective-permute-start | bytes 393224 | tf_op jit(solution)/shard_map/ppermute | solution.py:52
  48.9 15.4 %collective-permute-start.14 = (f32[4,128,128]{2,1,0:T(8,128)S(1)}, f32[4,128,128]{2,1,0:T(8,128)S(1)}, u32[]{:S(2)}, u32[]{:S(2)}) collective-permute-start(f32[4,128,128]{2,1,0:T(8,128)S(1)} %get-tuple-element.83), channel_id=1, source_target_pairs={{1,2},{3,4},{5,6},{2,1},{4,3},{6,5},{9,10},{11,12},{13,14},{10,9},... | collective-permute-start | bytes 786440 | tf_op jit(solution)/shard_map/ppermute | solution.py:52
  50.8 15.3 %collective-permute-start.15 = (f32[4,128,128]{2,1,0:T(8,128)S(1)}, f32[4,128,128]{2,1,0:T(8,128)S(1)}, u32[]{:S(2)}, u32[]{:S(2)}) collective-permute-start(f32[4,128,128]{2,1,0:T(8,128)S(1)} %get-tuple-element.84), channel_id=1, source_target_pairs={{0,1},{2,3},{4,5},{6,7},{1,0},{3,2},{5,4},{7,6},{8,9},{10,11},{12,... | collective-permute-start | bytes 786440 | tf_op jit(solution)/shard_map/ppermute | solution.py:52
  52.3 10.6 %collective-permute-start.18 = (f32[4,1,64,128]{3,2,1,0:T(8,128)S(1)}, f32[4,1,64,128]{3,2,1,0:T(8,128)S(1)}, u32[]{:S(2)}, u32[]{:S(2)}) collective-permute-start(f32[4,1,64,128]{3,2,1,0:T(8,128)S(1)} %get-tuple-element.87), channel_id=1, source_target_pairs={{8,16},{16,8},{9,17},{17,9},{10,18},{18,10},{11,19},{19,11},{12,20... | collective-permute-start | bytes 393224 | tf_op jit(solution)/shard_map/ppermute | solution.py:52
  60.6 5.5 %collective-permute-start.16 = (f32[4,2,64,128]{3,2,1,0:T(8,128)S(1)}, f32[4,2,64,128]{3,2,1,0:T(8,128)S(1)}, u32[]{:S(2)}, u32[]{:S(2)}) collective-permute-start(f32[4,2,64,128]{3,2,1,0:T(8,128)S(1)} %get-tuple-element.85), channel_id=1, source_target_pairs={{8,16},{16,8},{9,17},{17,9},{10,18},{18,10},{11,19},{19,11},{12,20... | collective-permute-start | bytes 786440 | tf_op jit(solution)/shard_map/ppermute | solution.py:52
  77.1 8.5 %collective-permute-start.22 = (f32[4,64,128]{2,1,0:T(8,128)S(1)}, f32[4,64,128]{2,1,0:T(8,128)S(1)}, u32[]{:S(2)}, u32[]{:S(2)}) collective-permute-start(f32[4,64,128]{2,1,0:T(8,128)S(1)} %get-tuple-element.94), channel_id=1, source_target_pairs={{8,16},{16,8},{9,17},{17,9},{10,18},{18,10},{11,19},{19,11},{12,20... | collective-permute-start | bytes 393224 | tf_op jit(solution)/shard_map/ppermute | solution.py:52
  77.7 12.5 %collective-permute-start.23 = (f32[4,64,128]{2,1,0:T(8,128)S(1)}, f32[4,64,128]{2,1,0:T(8,128)S(1)}, u32[]{:S(2)}, u32[]{:S(2)}) collective-permute-start(f32[4,64,128]{2,1,0:T(8,128)S(1)} %get-tuple-element.95), channel_id=1, source_target_pairs={{0,8},{16,24},{8,0},{24,16},{1,9},{17,25},{9,1},{25,17},{2,10},{18... | collective-permute-start | bytes 393224 | tf_op jit(solution)/shard_map/ppermute | solution.py:52
  81.6 10.7 %collective-permute-start.26 = (f32[4,64,128]{2,1,0:T(8,128)S(1)}, f32[4,64,128]{2,1,0:T(8,128)S(1)}, u32[]{:S(2)}, u32[]{:S(2)}) collective-permute-start(f32[4,64,128]{2,1,0:T(8,128)S(1)} %get-tuple-element.101), channel_id=1, source_target_pairs={{1,2},{3,4},{5,6},{2,1},{4,3},{6,5},{9,10},{11,12},{13,14},{10,9},... | collective-permute-start | bytes 393224 | tf_op jit(solution)/shard_map/ppermute | solution.py:52
  83.5 16.8 %collective-permute-start.20 = (f32[4,2,64,128]{3,2,1,0:T(8,128)S(1)}, f32[4,2,64,128]{3,2,1,0:T(8,128)S(1)}, u32[]{:S(2)}, u32[]{:S(2)}) collective-permute-start(f32[4,2,64,128]{3,2,1,0:T(8,128)S(1)} %get-tuple-element.91), channel_id=1, source_target_pairs={{8,16},{16,8},{9,17},{17,9},{10,18},{18,10},{11,19},{19,11},{12,20... | collective-permute-start | bytes 786440 | tf_op jit(solution)/shard_map/ppermute | solution.py:52
  84.2 16.2 %collective-permute-start.21 = (f32[4,2,64,128]{3,2,1,0:T(8,128)S(1)}, f32[4,2,64,128]{3,2,1,0:T(8,128)S(1)}, u32[]{:S(2)}, u32[]{:S(2)}) collective-permute-start(f32[4,2,64,128]{3,2,1,0:T(8,128)S(1)} %get-tuple-element.92), channel_id=1, source_target_pairs={{0,8},{16,24},{8,0},{24,16},{1,9},{17,25},{9,1},{25,17},{2,10},{18... | collective-permute-start | bytes 786440 | tf_op jit(solution)/shard_map/ppermute | solution.py:52
  85.5 8.4 %collective-permute-start.27 = (f32[4,64,128]{2,1,0:T(8,128)S(1)}, f32[4,64,128]{2,1,0:T(8,128)S(1)}, u32[]{:S(2)}, u32[]{:S(2)}) collective-permute-start(f32[4,64,128]{2,1,0:T(8,128)S(1)} %get-tuple-element.102), channel_id=1, source_target_pairs={{0,1},{2,3},{4,5},{6,7},{1,0},{3,2},{5,4},{7,6},{8,9},{10,11},{12,... | collective-permute-start | bytes 393224 | tf_op jit(solution)/shard_map/ppermute | solution.py:52
  90.3 8.1 %collective-permute-start.24 = (f32[4,64,128]{2,1,0:T(8,128)S(1)}, f32[4,64,128]{2,1,0:T(8,128)S(1)}, u32[]{:S(2)}, u32[]{:S(2)}) collective-permute-start(f32[4,64,128]{2,1,0:T(8,128)S(1)} %get-tuple-element.96), channel_id=1, source_target_pairs={{1,2},{3,4},{5,6},{2,1},{4,3},{6,5},{9,10},{11,12},{13,14},{10,9},... | collective-permute-start | bytes 393224 | tf_op jit(solution)/shard_map/ppermute | solution.py:52
  92.3 8.1 %collective-permute-start.25 = (f32[4,64,128]{2,1,0:T(8,128)S(1)}, f32[4,64,128]{2,1,0:T(8,128)S(1)}, u32[]{:S(2)}, u32[]{:S(2)}) collective-permute-start(f32[4,64,128]{2,1,0:T(8,128)S(1)} %get-tuple-element.97), channel_id=1, source_target_pairs={{0,1},{2,3},{4,5},{6,7},{1,0},{3,2},{5,4},{7,6},{8,9},{10,11},{12,... | collective-permute-start | bytes 393224 | tf_op jit(solution)/shard_map/ppermute | solution.py:52
  (6 other events, 37.5 us)
